TPU v7x, 32 devices: a whole 2x2x4 slice. The times are simulated.
32 devices in a mesh: dp: 4 (over y, x), fsdp: 4 (over z), ctx: 2 (over core).
Axes of the slice: x: 2, y: 2, z: 4, core: 2. Of those that a mesh axis runs over, the one named last changes fastest.
Arguments:
- inputs: bfloat16 [16, 1024, 1024], P(('dp', 'fsdp'), 'ctx'), may hold values from -6 to 6
- lengths: int32 [16], P(('dp', 'fsdp')), may hold values from 256 to 1024, as said below
- cotangent: bfloat16 [16, 1024, 1024], P(('dp', 'fsdp'), 'ctx'), may hold values from -6 to 6
- norm_gain1: float32 [1024], replicated, may hold values from 0.5 to 1.5
- w_qkv: bfloat16 [1024, 3072], P('fsdp'), may hold values from -0.1875 to 0.1875
- w_beta: bfloat16 [1024, 8], P('fsdp'), may hold values from -0.1875 to 0.1875
- conv_weight: float32 [4, 3072], replicated, may hold values from -3 to 3
- head_gain: float32 [128], replicated, may hold values from 0.5 to 1.5
- w_out: bfloat16 [1024, 1024], P('fsdp'), may hold values from -0.1875 to 0.1875
- norm_gain2: float32 [1024], replicated, may hold values from 0.5 to 1.5
- w_gateup: bfloat16 [1024, 5632], P('fsdp'), may hold values from -0.1875 to 0.1875
- w_down: bfloat16 [2816, 1024], P('fsdp'), may hold values from -0.109375 to 0.109375
Outputs:
- output: bfloat16 [16, 1024, 1024], P(('dp', 'fsdp'), 'ctx')
- grad_inputs: bfloat16 [16, 1024, 1024], P(('dp', 'fsdp'), 'ctx')
- grad_gain1: float32 [1024], replicated
- grad_qkv: float32 [1024, 3072], P(('fsdp', 'ctx'))
- grad_beta: float32 [1024, 8], P(('fsdp', 'ctx'))
- grad_conv: float32 [4, 3072], replicated
- grad_head_gain: float32 [128], replicated
- grad_out: float32 [1024, 1024], P(('fsdp', 'ctx'))
- grad_gain2: float32 [1024], replicated
- grad_gateup: float32 [1024, 5632], P(('fsdp', 'ctx'))
- grad_down: float32 [2816, 1024], P(('fsdp', 'ctx'))
Inputs may be any that keep to these rules, and one draw needn't show every extreme that they name: `lengths`: valid tokens of each sequence; they come first in it. Some sequence has all 1024 positions valid and some sequence has 256.
All inputs are finite; a program needn't handle non-finite values.
Results may differ from a plain program's by a relative error of at most 0.014.
Values may be sent and summed in bfloat16 or wider, within the bound.
No kernel may reach another device: no remote copies, remote signals or barrier semaphores. Data moves between devices by JAX's collectives and lax.ppermute only.
A program may use at most 256 MiB of HBM per device.

v0:
```python
import jax
import jax.numpy as jnp
from jax import lax
from jax.sharding import PartitionSpec as P

H = 8
HD = 128
KERNEL = 4
SPAN = 64


exact_precision = lax.Precision.HIGHEST


def passed_along(value, axis, steps):
    count = lax.axis_size(axis)
    first, last = (max(0, -steps), min(count, count - steps))
    return lax.ppermute(value, axis, [(source, source + steps) for source in range(first, last)])


def as_sent(value):
    return jax.tree.map(lambda a: a.astype(jnp.bfloat16) if a.dtype == jnp.float32 else a, value)


def span_factors(key_row_block, value_rows, strength):
    block_len = key_row_block.shape[1]
    head_width = key_row_block.shape[2]
    gram_matrix = jnp.einsum(
        "hik,hjk->hij", key_row_block, key_row_block, precision=exact_precision
    )
    system = jnp.tril(gram_matrix * strength[:, :, None], -1) + jnp.eye(
        block_len, dtype=key_row_block.dtype
    )
    right_side = strength[:, :, None] * jnp.concatenate([key_row_block, value_rows], -1)
    solved = jax.scipy.linalg.solve_triangular(system, right_side, lower=True, unit_diagonal=True)
    return (solved[..., :head_width], solved[..., head_width:])


def span_output(memory_matrix, blocks):
    query_rows, key_row_block, value_rows, strength = blocks
    key_blend, value_blend = span_factors(key_row_block, value_rows, strength)
    prediction_error = value_blend - jnp.einsum(
        "ist,itn->isn", key_blend, memory_matrix, precision=exact_precision
    )
    scores = jnp.tril(
        jnp.einsum("hik,hjk->hij", query_rows, key_row_block, precision=exact_precision)
    )
    final_result = jnp.einsum("ist,itn->isn", query_rows, memory_matrix, precision=exact_precision)
    final_result = final_result + jnp.einsum(
        "hij,hjv->hiv", scores, prediction_error, precision=exact_precision
    )
    updated_memory = memory_matrix + jnp.einsum(
        "xzn,xzf->xnf", key_row_block, prediction_error, precision=exact_precision
    )
    return (updated_memory, final_result)


def span_advance(carry, blocks):
    memory_matrix, transition = carry
    key_row_block, value_rows, strength = blocks
    key_blend, value_blend = span_factors(key_row_block, value_rows, strength)
    prediction_error = value_blend - jnp.einsum(
        "ist,itn->isn", key_blend, memory_matrix, precision=exact_precision
    )
    memory_matrix = memory_matrix + jnp.einsum(
        "xzn,xzf->xnf", key_row_block, prediction_error, precision=exact_precision
    )
    identity = jnp.eye(key_row_block.shape[2], dtype=key_row_block.dtype)
    step_map = identity - jnp.einsum(
        "hck,hcl->hkl", key_row_block, key_blend, precision=exact_precision
    )
    transition = jnp.einsum("hij,hjk->hik", step_map, transition, precision=exact_precision)
    return ((memory_matrix, transition), None)


def to_blocks(tensor):
    shape_now = tensor.shape
    grouped = tensor.reshape((shape_now[0], shape_now[1] // SPAN, SPAN) + shape_now[2:])
    return jnp.moveaxis(grouped, 1, 0)


def from_blocks(tensor):
    moved = jnp.moveaxis(tensor, 0, 1)
    return moved.reshape((moved.shape[0], moved.shape[1] * moved.shape[2]) + moved.shape[3:])


def delta_outputs(query_rows, key_row_block, value_rows, strength, memory_matrix):
    blocks = (
        to_blocks(query_rows),
        to_blocks(key_row_block),
        to_blocks(value_rows),
        to_blocks(strength),
    )
    memory_end, outputs = lax.scan(span_output, memory_matrix, blocks)
    return (from_blocks(outputs), memory_end)


def apply_map(matrix, tensor):
    return jnp.einsum("hij,hjk->hik", matrix, tensor, precision=exact_precision)


def split_heads(tensor):
    return jnp.transpose(tensor.reshape(tensor.shape[0], H, HD), (1, 0, 2))


def join_heads(tensor):
    return jnp.transpose(tensor, (1, 0, 2)).reshape(tensor.shape[1], H * HD)


def local(
    inputs,
    lengths,
    cotangent,
    norm_gain1,
    w_qkv,
    w_beta,
    conv_weight,
    head_gain,
    w_out,
    norm_gain2,
    w_gateup,
    w_down,
):
    tokens_in = inputs[0].astype(jnp.float32)
    piece_len, model_width = tokens_in.shape
    positions = lax.axis_index("ctx") * piece_len + jnp.arange(piece_len, dtype=jnp.int32)
    valid = (positions < lengths[0]).astype(jnp.float32)
    qkv_full, beta_full, out_full = (
        lax.all_gather(w_qkv, "fsdp", axis=0, tiled=True),
        lax.all_gather(w_beta, "fsdp", axis=0, tiled=True),
        lax.all_gather(w_out, "fsdp", axis=0, tiled=True),
    )
    gateup_full, down_full = (
        lax.all_gather(w_gateup, "fsdp", axis=0, tiled=True),
        lax.all_gather(w_down, "fsdp", axis=0, tiled=True),
    )
    scale_one = lax.rsqrt(jnp.mean(tokens_in * tokens_in, -1, keepdims=True) + 1e-06)
    normed_one = (tokens_in * scale_one * norm_gain1).astype(jnp.bfloat16)
    projected = jnp.dot(normed_one, qkv_full, preferred_element_type=jnp.float32)
    beta_logits = jnp.dot(normed_one, beta_full, preferred_element_type=jnp.float32)
    conv_in = projected * valid[:, None]
    carried_rows = passed_along(
        conv_in[piece_len - KERNEL + 1 :].astype(jnp.bfloat16), "ctx", 1
    ).astype(jnp.float32)
    extended = jnp.concatenate([carried_rows, conv_in], 0)
    conv_pre = conv_weight[0] * extended[0:piece_len]
    for offset in range(1, KERNEL):
        conv_pre = conv_pre + conv_weight[offset] * extended[offset : offset + piece_len]
    gate_conv = jax.nn.sigmoid(conv_pre)
    activated = conv_pre * gate_conv
    raw_queries = split_heads(activated[:, :model_width])
    raw_keys = split_heads(activated[:, model_width : 2 * model_width])
    value_rows = split_heads(activated[:, 2 * model_width :])
    query_scale = lax.rsqrt(jnp.sum(raw_queries * raw_queries, -1, keepdims=True) + 1e-06)
    key_scale = lax.rsqrt(jnp.sum(raw_keys * raw_keys, -1, keepdims=True) + 1e-06)
    query_rows = raw_queries * query_scale * HD ** (-0.5)
    key_row_block = raw_keys * key_scale
    beta_gate = jax.nn.sigmoid(beta_logits)
    strength = jnp.transpose(beta_gate * valid[:, None])
    zero_memory = jnp.zeros((H, HD, HD), jnp.float32)
    identity = jnp.broadcast_to(jnp.eye(HD, dtype=jnp.float32), (H, HD, HD))
    advanced, _ = lax.scan(
        span_advance,
        (zero_memory, identity),
        (to_blocks(key_row_block), to_blocks(value_rows), to_blocks(strength)),
    )
    local_end, transition = advanced

    def relay_forward(step_index, memory_matrix):
        return passed_along(
            (apply_map(transition, memory_matrix) + local_end).astype(jnp.bfloat16), "ctx", 1
        ).astype(jnp.float32)

    memory_in = lax.fori_loop(0, lax.axis_size("ctx") - 1, relay_forward, zero_memory)
    (heads_out, memory_out), pull_back = jax.vjp(
        delta_outputs, query_rows, key_row_block, value_rows, strength, memory_in
    )
    head_scale = lax.rsqrt(jnp.mean(heads_out * heads_out, -1, keepdims=True) + 1e-05)
    merged = join_heads(heads_out * head_scale * head_gain).astype(jnp.bfloat16)
    attention = jnp.dot(merged, out_full, preferred_element_type=jnp.float32)
    middle = tokens_in + attention
    scale_two = lax.rsqrt(jnp.mean(middle * middle, -1, keepdims=True) + 1e-06)
    normed_two = (middle * scale_two * norm_gain2).astype(jnp.bfloat16)
    gate_up = jnp.dot(normed_two, gateup_full, preferred_element_type=jnp.float32)
    ff_width = gate_up.shape[1] // 2
    gate_part = gate_up[:, :ff_width]
    up_part = gate_up[:, ff_width:]
    gate_sig = jax.nn.sigmoid(gate_part)
    hidden = (gate_part * gate_sig * up_part).astype(jnp.bfloat16)
    feed_out = jnp.dot(hidden, down_full, preferred_element_type=jnp.float32)
    output = (middle + feed_out).astype(jnp.bfloat16)
    qkv_back, beta_back, out_back = (
        lax.all_gather(w_qkv, "fsdp", axis=0, tiled=True),
        lax.all_gather(w_beta, "fsdp", axis=0, tiled=True),
        lax.all_gather(w_out, "fsdp", axis=0, tiled=True),
    )
    gateup_back, down_back = (
        lax.all_gather(w_gateup, "fsdp", axis=0, tiled=True),
        lax.all_gather(w_down, "fsdp", axis=0, tiled=True),
    )
    contract_cols = (((1,), (1,)), ((), ()))
    masked_cotangent = cotangent[0].astype(jnp.float32) * valid[:, None]
    grad_feed = masked_cotangent.astype(jnp.bfloat16)
    grad_hidden = lax.dot_general(
        grad_feed, down_back, contract_cols, preferred_element_type=jnp.float32
    )
    grad_gate = grad_hidden * up_part * gate_sig * (1.0 + gate_part * (1.0 - gate_sig))
    grad_up = grad_hidden * gate_part * gate_sig
    grad_gate_up = jnp.concatenate([grad_gate, grad_up], 1).astype(jnp.bfloat16)
    grad_normed_two = lax.dot_general(
        grad_gate_up, gateup_back, contract_cols, preferred_element_type=jnp.float32
    )
    gain_two_term = jnp.sum(grad_normed_two * middle * scale_two, 0)
    scaled_two = grad_normed_two * norm_gain2
    grad_middle = (
        masked_cotangent
        + scale_two * scaled_two
        - scale_two
        * scale_two
        * scale_two
        * middle
        * jnp.mean(scaled_two * middle, -1, keepdims=True)
    )
    grad_attention = grad_middle.astype(jnp.bfloat16)
    grad_merged = lax.dot_general(
        grad_attention, out_back, contract_cols, preferred_element_type=jnp.float32
    )
    grad_heads = split_heads(grad_merged)
    head_gain_term = jnp.sum(grad_heads * heads_out * head_scale, (0, 1))
    scaled_heads = grad_heads * head_gain
    grad_heads_out = (
        head_scale * scaled_heads
        - head_scale
        * head_scale
        * head_scale
        * heads_out
        * jnp.mean(scaled_heads * heads_out, -1, keepdims=True)
    )
    local_grads = pull_back((grad_heads_out, jnp.zeros_like(memory_out)))
    local_part = local_grads[4]
    transposed = jnp.transpose(transition, (0, 2, 1))

    def relay_backward(step_index, memory_grad):
        return passed_along(
            (apply_map(transposed, memory_grad) + local_part).astype(jnp.bfloat16), "ctx", -1
        ).astype(jnp.float32)

    grad_memory_out = lax.fori_loop(0, lax.axis_size("ctx") - 1, relay_backward, zero_memory)
    grad_queries, grad_keys, grad_values, grad_strength, _ = pull_back(
        (grad_heads_out, grad_memory_out)
    )
    grad_beta_logits = (
        jnp.transpose(grad_strength) * valid[:, None] * beta_gate * (1.0 - beta_gate)
    ).astype(jnp.bfloat16)
    grad_raw_queries = HD ** (-0.5) * (
        query_scale * grad_queries
        - query_scale
        * query_scale
        * query_scale
        * raw_queries
        * jnp.sum(raw_queries * grad_queries, -1, keepdims=True)
    )
    grad_raw_keys = key_scale * grad_keys - key_scale * key_scale * key_scale * raw_keys * jnp.sum(
        raw_keys * grad_keys, -1, keepdims=True
    )
    grad_activated = jnp.concatenate(
        [join_heads(grad_raw_queries), join_heads(grad_raw_keys), join_heads(grad_values)], 1
    )
    grad_conv_pre = grad_activated * gate_conv * (1.0 + conv_pre * (1.0 - gate_conv))
    conv_rows = [
        jnp.sum(grad_conv_pre * extended[offset : offset + piece_len], 0)
        for offset in range(KERNEL)
    ]
    conv_term = jnp.stack(conv_rows, 0)
    grad_extended = jnp.pad(conv_weight[0] * grad_conv_pre, ((0, KERNEL - 1), (0, 0)))
    for offset in range(1, KERNEL):
        grad_extended = grad_extended + jnp.pad(
            conv_weight[offset] * grad_conv_pre, ((offset, KERNEL - 1 - offset), (0, 0))
        )
    returned_rows = passed_along(as_sent(grad_extended[: KERNEL - 1]), "ctx", -1)
    grad_conv_in = grad_extended[KERNEL - 1 :] + jnp.pad(
        returned_rows, ((piece_len - KERNEL + 1, 0), (0, 0))
    )
    grad_projected = (grad_conv_in * valid[:, None]).astype(jnp.bfloat16)
    grad_normed_one = lax.dot_general(
        grad_projected, qkv_back, contract_cols, preferred_element_type=jnp.float32
    )
    grad_normed_one = grad_normed_one + lax.dot_general(
        grad_beta_logits, beta_back, contract_cols, preferred_element_type=jnp.float32
    )
    gain_one_term = jnp.sum(grad_normed_one * tokens_in * scale_one, 0)
    scaled_one = grad_normed_one * norm_gain1
    grad_tokens = (
        grad_middle
        + scale_one * scaled_one
        - scale_one
        * scale_one
        * scale_one
        * tokens_in
        * jnp.mean(scaled_one * tokens_in, -1, keepdims=True)
    )
    contract_rows = (((0,), (0,)), ((), ()))
    parts = [
        lax.dot_general(
            normed_one, grad_projected, contract_rows, preferred_element_type=jnp.float32
        ),
        lax.dot_general(merged, grad_attention, contract_rows, preferred_element_type=jnp.float32),
        lax.dot_general(
            normed_two, grad_gate_up, contract_rows, preferred_element_type=jnp.float32
        ),
        lax.dot_general(
            normed_one, grad_beta_logits, contract_rows, preferred_element_type=jnp.float32
        ),
    ]
    wide_share = lax.psum_scatter(
        jnp.concatenate(parts, 1), ("fsdp", "ctx"), scatter_dimension=0, tiled=True
    )
    down_share = lax.psum_scatter(
        lax.dot_general(hidden, grad_feed, contract_rows, preferred_element_type=jnp.float32),
        ("fsdp", "ctx"),
        scatter_dimension=0,
        tiled=True,
    )
    small_sums = lax.psum(
        (gain_one_term, conv_term, head_gain_term, gain_two_term), ("fsdp", "ctx")
    )
    totals = (
        lax.psum(wide_share.astype(jnp.bfloat16), "dp").astype(jnp.float32),
        lax.psum(down_share.astype(jnp.bfloat16), "dp").astype(jnp.float32),
        lax.psum(small_sums[0].astype(jnp.bfloat16), "dp").astype(jnp.float32),
        lax.psum(small_sums[1].astype(jnp.bfloat16), "dp").astype(jnp.float32),
        lax.psum(small_sums[2].astype(jnp.bfloat16), "dp").astype(jnp.float32),
        lax.psum(small_sums[3].astype(jnp.bfloat16), "dp").astype(jnp.float32),
    )
    wide_total = totals[0]
    qkv_cols = 3 * model_width
    out_end = qkv_cols + model_width
    gateup_end = out_end + gate_up.shape[1]
    return (
        output[None],
        grad_tokens.astype(jnp.bfloat16)[None],
        totals[2],
        wide_total[:, :qkv_cols],
        wide_total[:, gateup_end:],
        totals[3],
        totals[4],
        wide_total[:, qkv_cols:out_end],
        totals[5],
        wide_total[:, out_end:gateup_end],
        totals[1],
    )


def solution(mesh):
    placed = (
        P(("dp", "fsdp"), "ctx", None),
        P(("dp", "fsdp")),
        P(("dp", "fsdp"), "ctx", None),
        P(),
        P("fsdp", None),
        P("fsdp", None),
        P(),
        P(),
        P("fsdp", None),
        P(),
        P("fsdp", None),
        P("fsdp", None),
    )
    return jax.shard_map(
        local,
        mesh=mesh,
        in_specs=placed,
        out_specs=(
            P(("dp", "fsdp"), "ctx", None),
            P(("dp", "fsdp"), "ctx", None),
            P(),
            P(("fsdp", "ctx"), None),
            P(("fsdp", "ctx"), None),
            P(),
            P(),
            P(("fsdp", "ctx"), None),
            P(),
            P(("fsdp", "ctx"), None),
            P(("fsdp", "ctx"), None),
        ),
        check_vma=False,
    )
```

profile of v0, /device:TPU:10, one launch (start us, length us, event | category | flops | bytes accessed | tf_op | source)
XLA Modules:
  0.0 2304.7 jit_solution(14385309891945264913)
XLA Ops:
  11.7 13.4 all_gather.21
  25.7 97.8 %all-gather.5.cloned.1.call-done = bf16[1024,3072]{1,0:T(8,128)(2,1)} async-done(((bf16[256,3072]{1,0:T(8,128)(2,1)}), bf16[1024,3072]{1,0:T(8,128)(2,1)}) %all-gather.5.cloned.1.call-update) | async-done | bytes 6291472 | tf_op jit(solution)/shard_map/all_gather | solution.py:129
  123.4 5.6 convolution_multiply_fusion.1
  134.4 12.9 fusion.151
  154.6 413.5 %while.99 = (s32[]{:T(128)}, f32[8,128,128]{2,1,0:T(8,128)S(1)}, f32[8,128,128]{2,1,0:T(8,128)}, f32[8,8,64,128]{3,2,1,0:T(8,128)S(1)}, f32[8,8,64]{2,1,0:T(8,12...) while((s32[]{:T(128)}, f32[8,128,128]{2,1,0:T(8,128)S(1)}, ...), condition=%wide.region_3.5_spmd.clone, body=%wide.region_2.4_spmd.clone.sunk | while | flops 655380544 | bytes 13583016 | solution.py:162
  157.7 40.7 %custom-call.39 = f32[8,1,64,64]{2,3,1,0:T(8,128)} custom-call(f32[8,1,64,64]{3,2,1,0:T(8,128)} %fusion.417), custom_call_target="InvertDiagBlocksLowerTriangular" | custom-call | tf_op jit(solution)/shard_map/while/body/eval_jaxpr/jit(_solve_triangular)/vmap()/triangular_solve/custom-call.1 | solution.py:35
  209.3 40.7 %custom-call.39 = f32[8,1,64,64]{2,3,1,0:T(8,128)} custom-call(f32[8,1,64,64]{3,2,1,0:T(8,128)} %fusion.417), custom_call_target="InvertDiagBlocksLowerTriangular" | custom-call | tf_op jit(solution)/shard_map/while/body/eval_jaxpr/jit(_solve_triangular)/vmap()/triangular_solve/custom-call.1 | solution.py:35
  261.0 40.7 %custom-call.39 = f32[8,1,64,64]{2,3,1,0:T(8,128)} custom-call(f32[8,1,64,64]{3,2,1,0:T(8,128)} %fusion.417), custom_call_target="InvertDiagBlocksLowerTriangular" | custom-call | tf_op jit(solution)/shard_map/while/body/eval_jaxpr/jit(_solve_triangular)/vmap()/triangular_solve/custom-call.1 | solution.py:35
  312.7 40.7 %custom-call.39 = f32[8,1,64,64]{2,3,1,0:T(8,128)} custom-call(f32[8,1,64,64]{3,2,1,0:T(8,128)} %fusion.417), custom_call_target="InvertDiagBlocksLowerTriangular" | custom-call | tf_op jit(solution)/shard_map/while/body/eval_jaxpr/jit(_solve_triangular)/vmap()/triangular_solve/custom-call.1 | solution.py:35
  364.4 40.7 %custom-call.39 = f32[8,1,64,64]{2,3,1,0:T(8,128)} custom-call(f32[8,1,64,64]{3,2,1,0:T(8,128)} %fusion.417), custom_call_target="InvertDiagBlocksLowerTriangular" | custom-call | tf_op jit(solution)/shard_map/while/body/eval_jaxpr/jit(_solve_triangular)/vmap()/triangular_solve/custom-call.1 | solution.py:35
  416.1 40.7 %custom-call.39 = f32[8,1,64,64]{2,3,1,0:T(8,128)} custom-call(f32[8,1,64,64]{3,2,1,0:T(8,128)} %fusion.417), custom_call_target="InvertDiagBlocksLowerTriangular" | custom-call | tf_op jit(solution)/shard_map/while/body/eval_jaxpr/jit(_solve_triangular)/vmap()/triangular_solve/custom-call.1 | solution.py:35
  467.8 40.7 %custom-call.39 = f32[8,1,64,64]{2,3,1,0:T(8,128)} custom-call(f32[8,1,64,64]{3,2,1,0:T(8,128)} %fusion.417), custom_call_target="InvertDiagBlocksLowerTriangular" | custom-call | tf_op jit(solution)/shard_map/while/body/eval_jaxpr/jit(_solve_triangular)/vmap()/triangular_solve/custom-call.1 | solution.py:35
  519.5 40.7 %custom-call.39 = f32[8,1,64,64]{2,3,1,0:T(8,128)} custom-call(f32[8,1,64,64]{3,2,1,0:T(8,128)} %fusion.417), custom_call_target="InvertDiagBlocksLowerTriangular" | custom-call | tf_op jit(solution)/shard_map/while/body/eval_jaxpr/jit(_solve_triangular)/vmap()/triangular_solve/custom-call.1 | solution.py:35
  578.5 469.8 %while.97 = (s32[]{:T(128)}, f32[8,128,128]{2,1,0:T(8,128)S(1)}, f32[8,8,64,128]{3,2,0,1:T(8,128)}, f32[8,8,64,1]{2,1,3,0:T(8,128)S(1)}, f32[8,8,64,64]{3,2,1,0:...) while((s32[]{:T(128)}, f32[8,128,128]{2,1,0:T(8,128)S(1)}, ...), condition=%wide.region_6.8_spmd.clone, body=%wide.region_5.7_spmd.clone.sunk | while | flops 554618944 | bytes 16134973 | solution.py:94
  585.6 40.7 %custom-call.37 = f32[8,1,64,64]{2,3,1,0:T(8,128)} custom-call(f32[8,1,64,64]{3,2,1,0:T(8,128)} %add_bitcast_fusion.4), custom_call_target="InvertDiagBlocksLowerTriangular" | custom-call | tf_op jit(solution)/shard_map/jvp()/while/body/eval_jaxpr/jit(_solve_triangular)/vmap()/triangular_solve/custom-call.1 | solution.py:35
  644.2 40.7 %custom-call.37 = f32[8,1,64,64]{2,3,1,0:T(8,128)} custom-call(f32[8,1,64,64]{3,2,1,0:T(8,128)} %add_bitcast_fusion.4), custom_call_target="InvertDiagBlocksLowerTriangular" | custom-call | tf_op jit(solution)/shard_map/jvp()/while/body/eval_jaxpr/jit(_solve_triangular)/vmap()/triangular_solve/custom-call.1 | solution.py:35
  703.0 40.7 %custom-call.37 = f32[8,1,64,64]{2,3,1,0:T(8,128)} custom-call(f32[8,1,64,64]{3,2,1,0:T(8,128)} %add_bitcast_fusion.4), custom_call_target="InvertDiagBlocksLowerTriangular" | custom-call | tf_op jit(solution)/shard_map/jvp()/while/body/eval_jaxpr/jit(_solve_triangular)/vmap()/triangular_solve/custom-call.1 | solution.py:35
  761.8 40.7 %custom-call.37 = f32[8,1,64,64]{2,3,1,0:T(8,128)} custom-call(f32[8,1,64,64]{3,2,1,0:T(8,128)} %add_bitcast_fusion.4), custom_call_target="InvertDiagBlocksLowerTriangular" | custom-call | tf_op jit(solution)/shard_map/jvp()/while/body/eval_jaxpr/jit(_solve_triangular)/vmap()/triangular_solve/custom-call.1 | solution.py:35
  820.5 40.7 %custom-call.37 = f32[8,1,64,64]{2,3,1,0:T(8,128)} custom-call(f32[8,1,64,64]{3,2,1,0:T(8,128)} %add_bitcast_fusion.4), custom_call_target="InvertDiagBlocksLowerTriangular" | custom-call | tf_op jit(solution)/shard_map/jvp()/while/body/eval_jaxpr/jit(_solve_triangular)/vmap()/triangular_solve/custom-call.1 | solution.py:35
  879.3 40.7 %custom-call.37 = f32[8,1,64,64]{2,3,1,0:T(8,128)} custom-call(f32[8,1,64,64]{3,2,1,0:T(8,128)} %add_bitcast_fusion.4), custom_call_target="InvertDiagBlocksLowerTriangular" | custom-call | tf_op jit(solution)/shard_map/jvp()/while/body/eval_jaxpr/jit(_solve_triangular)/vmap()/triangular_solve/custom-call.1 | solution.py:35
  938.0 40.7 %custom-call.37 = f32[8,1,64,64]{2,3,1,0:T(8,128)} custom-call(f32[8,1,64,64]{3,2,1,0:T(8,128)} %add_bitcast_fusion.4), custom_call_target="InvertDiagBlocksLowerTriangular" | custom-call | tf_op jit(solution)/shard_map/jvp()/while/body/eval_jaxpr/jit(_solve_triangular)/vmap()/triangular_solve/custom-call.1 | solution.py:35
  996.7 40.7 %custom-call.37 = f32[8,1,64,64]{2,3,1,0:T(8,128)} custom-call(f32[8,1,64,64]{3,2,1,0:T(8,128)} %add_bitcast_fusion.4), custom_call_target="InvertDiagBlocksLowerTriangular" | custom-call | tf_op jit(solution)/shard_map/jvp()/while/body/eval_jaxpr/jit(_solve_triangular)/vmap()/triangular_solve/custom-call.1 | solution.py:35
  1060.5 12.3 fusion.218
  1072.8 11.9 multiply_convert_fusion.1
  1087.3 11.1 fusion.152
  1098.4 13.4 multiply_reduce_fusion.4
  1121.6 48.7 %while.100 = (s32[]{:T(128)}, f32[8,128,128]{2,1,0:T(8,128)S(1)}, f32[8,8,64,128]{3,2,1,0:T(8,128)}, f32[8,8,64,128]{3,2,1,0:T(8,128)}, f32[8,8,64,128]{3,2,1,0:...) while((s32[]{:T(128)}, f32[8,128,128]{2,1,0:T(8,128)S(1)}, ...), condition=%wide.region_12.14_spmd.clone, body=%wide.region_11.13_spmd.clone.sunk | while | flops 352976896 | bytes 5245579 | solution.py:94
  1172.6 9.6 fusion.204
  1194.1 541.8 %while.98 = (s32[]{:T(128)}, f32[8,128,128]{2,1,0:T(8,128)S(1)}, f32[8,8,64,128]{3,2,0,1:T(8,128)}, f32[8,8,64,128]{3,2,0,1:T(8,128)}, f32[8,8,64,128]{3,2,0,1:T...) while((s32[]{:T(128)}, f32[8,128,128]{2,1,0:T(8,128)S(1)}, ...), condition=%wide.region_16.18_spmd.clone.clone, body=%wide.region_13.17_spmd.clone.clone.sunk | while | flops 1134243328 | bytes 18174760 | solution.py:94
  1212.0 40.7 %custom-call.38 = f32[8,1,64,64]{2,3,1,0:T(8,128)} custom-call(f32[8,1,64,64]{3,2,1,0:T(8,128)} %add_bitcast_fusion.5), custom_call_target="InvertDiagBlocksLowerTriangular" | custom-call | tf_op jit(solution)/shard_map/transpose(jvp())/while/body/eval_jaxpr/jit(_solve_triangular)/vmap()/triangular_solve | solution.py:35
  1279.8 40.7 %custom-call.38 = f32[8,1,64,64]{2,3,1,0:T(8,128)} custom-call(f32[8,1,64,64]{3,2,1,0:T(8,128)} %add_bitcast_fusion.5), custom_call_target="InvertDiagBlocksLowerTriangular" | custom-call | tf_op jit(solution)/shard_map/transpose(jvp())/while/body/eval_jaxpr/jit(_solve_triangular)/vmap()/triangular_solve | solution.py:35
  1347.5 40.7 %custom-call.38 = f32[8,1,64,64]{2,3,1,0:T(8,128)} custom-call(f32[8,1,64,64]{3,2,1,0:T(8,128)} %add_bitcast_fusion.5), custom_call_target="InvertDiagBlocksLowerTriangular" | custom-call | tf_op jit(solution)/shard_map/transpose(jvp())/while/body/eval_jaxpr/jit(_solve_triangular)/vmap()/triangular_solve | solution.py:35
  1415.1 40.7 %custom-call.38 = f32[8,1,64,64]{2,3,1,0:T(8,128)} custom-call(f32[8,1,64,64]{3,2,1,0:T(8,128)} %add_bitcast_fusion.5), custom_call_target="InvertDiagBlocksLowerTriangular" | custom-call | tf_op jit(solution)/shard_map/transpose(jvp())/while/body/eval_jaxpr/jit(_solve_triangular)/vmap()/triangular_solve | solution.py:35
  1482.8 40.7 %custom-call.38 = f32[8,1,64,64]{2,3,1,0:T(8,128)} custom-call(f32[8,1,64,64]{3,2,1,0:T(8,128)} %add_bitcast_fusion.5), custom_call_target="InvertDiagBlocksLowerTriangular" | custom-call | tf_op jit(solution)/shard_map/transpose(jvp())/while/body/eval_jaxpr/jit(_solve_triangular)/vmap()/triangular_solve | solution.py:35
  1550.5 40.7 %custom-call.38 = f32[8,1,64,64]{2,3,1,0:T(8,128)} custom-call(f32[8,1,64,64]{3,2,1,0:T(8,128)} %add_bitcast_fusion.5), custom_call_target="InvertDiagBlocksLowerTriangular" | custom-call | tf_op jit(solution)/shard_map/transpose(jvp())/while/body/eval_jaxpr/jit(_solve_triangular)/vmap()/triangular_solve | solution.py:35
  1618.2 40.7 %custom-call.38 = f32[8,1,64,64]{2,3,1,0:T(8,128)} custom-call(f32[8,1,64,64]{3,2,1,0:T(8,128)} %add_bitcast_fusion.5), custom_call_target="InvertDiagBlocksLowerTriangular" | custom-call | tf_op jit(solution)/shard_map/transpose(jvp())/while/body/eval_jaxpr/jit(_solve_triangular)/vmap()/triangular_solve | solution.py:35
  1685.9 40.7 %custom-call.38 = f32[8,1,64,64]{2,3,1,0:T(8,128)} custom-call(f32[8,1,64,64]{3,2,1,0:T(8,128)} %add_bitcast_fusion.5), custom_call_target="InvertDiagBlocksLowerTriangular" | custom-call | tf_op jit(solution)/shard_map/transpose(jvp())/while/body/eval_jaxpr/jit(_solve_triangular)/vmap()/triangular_solve | solution.py:35
  1748.9 5.7 multiply_reduce_fusion.3
  1754.7 6.9 broadcast_multiply_fusion.4
  1761.6 8.1 pad_add_fusion.3
  1773.5 6.9 fusion.221
  1780.3 26.0 %pad_maximum_fusion.2 = f32[1024,9736]{1,0:T(8,128)} fusion(f32[1024,8]{1,0:T(8,128)S(1)} %fusion.219, f32[1024,5632]{1,0:T(8,128)} %fusion.152, f32[1024,1024]{1,0:T(8,128)S(1)} %copy-done.10, f32[1024,3072]{1,0:T(8,128)} %fusion.221), kind=kLoop, calls=%fused_computation.201 | loop fusion | flops 29908992 | bytes 79757312 | tf_op jit(solution)/shard_map/concatenate | solution.py:316
  1809.1 385.7 %reduce-scatter.3.cloned.1.call-done = f32[128,9736]{1,0:T(8,128)} async-done(((f32[1024,9736]{1,0:T(8,128)}), f32[128,9736]{1,0:T(8,128)}) %reduce-scatter.3.cloned.1.call-update) | async-done | bytes 4984848 | tf_op jit(solution)/shard_map/reduce_scatter | solution.py:315
  2200.5 7.6 fusion.194
  2208.8 9.9 fusion.162
  2218.7 26.6 %all-reduce.7 = (bf16[1024]{0:T(1024)(128)(2,1)S(1)}, bf16[4,3072]{1,0:T(4,128)(2,1)S(1)}, bf16[128]{0:T(256)(128)(2,1)S(1)}, bf16[1024]{0:T(1024)(128)(2,1)S(1)}) all-reduce(f32[1024]{0:T(1024)S(1)} %get-tuple-element.1318, f32[4,3072]{1,0:T(4,128)S(1)} %pad_maximum_fusion.7, ...), channel_id=1, replica_groups=mesh['dp'=4,'fsdp'=4,'ctx'=2] {'fsdp','ctx'}, use_global_device_ids=true, to_apply=%region_21.23 | all-reduce | flops 14464 | bytes 86784 | tf_op jit(solution)/shard_map/psum | solution.py:324
  2245.3 14.9 all-reduce.8
  2265.6 24.5 %all-reduce.12.cloned.1.call-done = (bf16[128,9736]{1,0:T(8,128)(2,1)}, bf16[352,1024]{1,0:T(8,128)(2,1)}) async-done(((bf16[128,9736]{1,0:T(8,128)(2,1)}, bf16[352,1024]{1,0:T(8,128)(2,1)}), (bf16[128,9736]{1,0:T(8,128)(2,1)}, bf16[352,1024]{1,0:T(8,128)(2,1)})) %all-reduce.12.cloned.1.call-update) | async-done | bytes 3213328 | tf_op jit(solution)/shard_map/psum | solution.py:328
  (779 shorter events, 598.4 us)
Async XLA Ops:
  7.2 116.3 %all-gather.5.cloned.1.call-start = ((), (), s32[]{:S(2)}) async-start(), calls=%async_computation.2 | async-start | bytes 7864320 | tf_op jit(solution)/shard_map/all_gather | solution.py:129
  7.9 1047.7 %all-gather.7.cloned.1.call-start = ((), (), s32[]{:S(2)}) async-start(), calls=%async_computation.3 | async-start | bytes 2621440 | tf_op jit(solution)/shard_map/all_gather | solution.py:131
  8.7 16.5 copy-start.55
  8.7 1051.8 %all-gather.9.cloned.1.call-start = ((), (), s32[]{:S(2)}) async-start(), calls=%async_computation.4 | async-start | bytes 14417920 | tf_op jit(solution)/shard_map/all_gather | solution.py:134
  9.4 1063.4 %all-gather.11.cloned.1.call-start = ((), (), s32[]{:S(2)}) async-start(), calls=%async_computation.5 | async-start | bytes 7208960 | tf_op jit(solution)/shard_map/all_gather | solution.py:135
  10.0 1796.7 %reduce-scatter.5.cloned.1.call-start = ((), (), s32[]{:S(2)}) async-start(), calls=%async_computation.7 | async-start | bytes 12976128 | tf_op jit(solution)/shard_map/reduce_scatter | solution.py:318
  11.6 117.5 %copy-start.50 = (f32[512]{0:T(512)}, f32[512]{0:T(512)S(1)}, u32[]{:S(2)}) copy-start(f32[512]{0:T(512)S(1)} %get-tuple-element.1475) | copy-start | bytes 6148
  11.7 122.7 %copy-start.35 = (f32[1,3072]{1,0:T(1,128)}, f32[1,3072]{1,0:T(1,128)S(1)}, u32[]{:S(2)}) copy-start(f32[1,3072]{1,0:T(1,128)S(1)} %get-tuple-element.1466) | copy-start | bytes 36868
  11.7 122.7 %copy-start.37 = (f32[1,3072]{1,0:T(1,128)}, f32[1,3072]{1,0:T(1,128)S(1)}, u32[]{:S(2)}) copy-start(f32[1,3072]{1,0:T(1,128)S(1)} %get-tuple-element.1467) | copy-start | bytes 36868
  11.7 122.7 %copy-start.39 = (f32[1,3072]{1,0:T(1,128)}, f32[1,3072]{1,0:T(1,128)S(1)}, u32[]{:S(2)}) copy-start(f32[1,3072]{1,0:T(1,128)S(1)} %get-tuple-element.1468) | copy-start | bytes 36868
  11.7 122.7 %copy-start.41 = (f32[1,3072]{1,0:T(1,128)}, f32[1,3072]{1,0:T(1,128)S(1)}, u32[]{:S(2)}) copy-start(f32[1,3072]{1,0:T(1,128)S(1)} %get-tuple-element.1469) | copy-start | bytes 36868
  25.1 104.0 %copy-start.44 = (bf16[1024,8]{0,1:T(8,128)(2,1)}, bf16[1024,8]{0,1:T(8,128)(2,1)S(1)}, u32[]{:S(2)}) copy-start(bf16[1024,8]{0,1:T(8,128)(2,1)S(1)} %all_gather.21) | copy-start | bytes 49156
  25.6 103.5 %copy-start.46 = (f32[512,8]{0,1:T(8,128)}, f32[512,8]{0,1:T(8,128)S(1)}, u32[]{:S(2)}) copy-start(f32[512,8]{0,1:T(8,128)S(1)} %fusion.199) | copy-start | bytes 49156
  131.8 2.6 collective-permute-start
  134.3 12.9 copy-start.30
  568.1 6.5 copy-start.4
  569.8 6.9 collective-permute-start.1
  687.5 5.0 copy-start.1
  746.3 5.0 copy-start.1
  1072.8 14.5 copy-start.16
  1098.4 13.4 copy-start.28
  1121.6 48.7 %copy-start.9 = (f32[8,128,128]{2,1,0:T(8,128)S(1)}, f32[8,128,128]{2,1,0:T(8,128)}, u32[]{:S(2)}) copy-start(f32[8,128,128]{2,1,0:T(8,128)} %get-tuple-element.962) | copy-start | bytes 1572868
  1171.3 16.9 collective-permute-start.2
  1182.2 1012.6 %reduce-scatter.3.cloned.1.call-start = ((), (), s32[]{:S(2)}) async-start(), calls=%async_computation.6 | async-start | bytes 45416448 | tf_op jit(solution)/shard_map/reduce_scatter | solution.py:315
  1252.7 5.2 copy-start.12
  1320.5 5.2 copy-start.12
  1388.2 5.2 copy-start.12
  1455.8 5.2 copy-start.12
  1523.5 5.2 copy-start.12
  1591.2 5.2 copy-start.12
  1658.9 5.2 copy-start.12
  1726.6 5.2 copy-start.12
  1741.7 6.1 slice-start.2
  1748.8 5.8 copy-start.36
  1748.8 5.8 copy-start.38
  1748.8 5.8 copy-start.40
  1748.9 5.8 copy-start.42
  1761.6 9.4 copy-start.47
  1761.6 9.5 copy-start.23
  1761.6 9.5 copy-start.51
  1761.6 9.5 copy-start.56
  1769.7 3.8 collective-permute-start.3
  1773.5 6.9 copy-start.10
  1806.4 483.7 %all-reduce.12.cloned.1.call-start = ((), (), s32[]{:S(2)}) async-start(), calls=%async_computation.8 | async-start | bytes 6488064 | tf_op jit(solution)/shard_map/psum | solution.py:328
  2200.5 7.6 copy-start.45
  2208.7 10.0 copy-start.53
  2208.7 53.7 %copy-start.15 = (f32[512,1024]{1,0:T(8,128)S(1)}, f32[512,1024]{1,0:T(8,128)}, u32[]{:S(2)}) copy-start(f32[512,1024]{1,0:T(8,128)} %copy-done.14) | copy-start | bytes 6291460
  2208.7 53.7 %copy-start.49 = (f32[512]{0:T(512)S(1)}, f32[512]{0:T(512)}, u32[]{:S(2)}) copy-start(f32[512]{0:T(512)} %get-tuple-element.1474) | copy-start | bytes 6148
  (66 other events, 195.5 us)
Sparse Core Ops, SparseCore 0:
  9.6 113.8 all-gather.4
  125.0 45.3 all-gather.6
  172.0 198.8 all-gather.8
  372.4 105.7 all-gather.10
  1182.4 119.1 reduce-scatter.4
  1806.5 388.2 reduce-scatter.2
  2199.1 90.9 all-reduce.11
where the time goes:
time: 2320 us; the launch traced here: 2300 us
  other arithmetic  1100 us (47%)
  waiting for transfers between devices  513 us (22%)
  matrix products  508 us (22%)
  local copies, waits for them, and re-layouts  97.5 us (4%)
  blocking collectives  54.8 us (2%)
    another operation x96, other arithmetic, span_factors(): jax.scipy.linalg.solve_triangular(system, right_side, lower=True, unit_di...  999 us
    reduce_scatter x1, waiting for transfers between devices, local(): lax.psum_scatter(jnp.concatenate(parts, 1), ('fsdp', 'ctx'), scatter_dime...  386 us
    all_gather x1, waiting for transfers between devices, local(): lax.all_gather(w_qkv, 'fsdp', axis=0, tiled=True)  97.8 us
    another operation x32, matrix products, span_factors(): jax.scipy.linalg.solve_triangular(system, right_side, lower=True, unit_di...  68.7 us
    dot_general x32, matrix products, span_output(): jnp.einsum('ist,itn->isn', query_rows, memory_matrix, precision=exact_pre...  68.5 us
    dot_general x32, matrix products, span_output(): jnp.einsum('ist,itn->isn', key_blend, memory_matrix, precision=exact_prec...  59 us
  transfers between devices with their start and end apart: 11, of which 5 were waited for; matrix products, arithmetic and copies ran while one was open for 69% of the time, Pallas kernels for 0%

commit v1 on v0

v1 whole, which is shorter than its diff:
```python
import functools
import jax, jax.numpy as jnp
from jax import lax
from jax.experimental import pallas as pl
from jax.experimental.pallas import tpu as pltpu
from jax.sharding import PartitionSpec as P

HD = 128
KERNEL = 4
CHUNK = 128
bf16 = jnp.bfloat16
f32 = jnp.float32

def dot(a, b):
    return jnp.dot(a, b, preferred_element_type=f32)

def dot_nt(a, b):
    return lax.dot_general(a, b, (((1,), (1,)), ((), ())), preferred_element_type=f32)

def dot_tn(a, b):
    return lax.dot_general(a, b, (((0,), (0,)), ((), ())), preferred_element_type=f32)

def halves(a):
    high = a.astype(bf16)
    return high, (a - high.astype(f32)).astype(bf16)

def fine_dot(a, b):
    n = b[0].shape[1]
    left = jnp.concatenate(a, 1)
    row = jnp.concatenate(b, 1)
    both = dot(left, jnp.concatenate([row, row], 0))
    return both[:, :n] + both[:, n:]

def unit_lower_inverses(lowers, size):
    rows = lax.broadcasted_iota(jnp.int32, (size, size), 0)
    cols = lax.broadcasted_iota(jnp.int32, (size, size), 1)
    eye = jnp.where(rows == cols, 1.0, 0.0)
    def joins(b):
        return (rows // (2 * b) == cols // (2 * b)) & ((rows // b) % 2 == 1) & ((cols // b) % 2 == 0)
    mask = joins(1)
    invs = [eye - jnp.where(mask, t, 0.0) for t in lowers]
    b = 2
    while b < size:
        mask = joins(b)
        parts = [halves(jnp.where(mask, t, 0.0)) for t in lowers]
        splits = [halves(t) for t in invs]
        inner = [halves(fine_dot(p, t)) for p, t in zip(parts, splits)]
        invs = [i - fine_dot(t, n) for i, t, n in zip(invs, splits, inner)]
        b *= 2
    return invs

def conv_rows(ref, weight, length):
    total = weight[0:1] * ref[pl.ds(5, length), :]
    for j in range(1, KERNEL):
        total = total + weight[j:j+1] * ref[pl.ds(5 + j, length), :]
    return total

def fd_kernel(hb, nv_ref, pq, pk, pv, hq, hk, hv, wq, wk, wv, bl_ref,
              q_ref, k_ref, t_ref, x_ref, o_ref, z_ref, ze_ref, ext):
    length = pq.shape[0]
    nv = nv_ref[0]
    valid = lax.broadcasted_iota(jnp.int32, (length, 1), 0) < nv
    rows = lax.broadcasted_iota(jnp.int32, (CHUNK, CHUNK), 0)
    cols = lax.broadcasted_iota(jnp.int32, (CHUNK, CHUNK), 1)
    eye = jnp.where(rows == cols, 1.0, 0.0)
    group = pl.program_id(0)
    lane8 = lax.broadcasted_iota(jnp.int32, bl_ref.shape, 1)
    acts = []
    for i, (p, h, w) in enumerate(((pq, hq, wq), (pk, hk, wk), (pv, hv, wv))):
        ext[i, 0:8, :] = h[...]
        ext[i, 8:, :] = jnp.where(valid, p[...], 0.0)
        c = conv_rows(ext.at[i], w, length)
        acts.append(c * jax.nn.sigmoid(c))
    count = length // CHUNK
    spans = [slice(c * CHUNK, (c + 1) * CHUNK) for c in range(count)]
    heads = []
    for h in range(hb):
        lanes = slice(h * HD, (h + 1) * HD)
        a, b, v = (t[:, lanes] for t in acts)
        q = (a * (lax.rsqrt(jnp.sum(a * a, -1, keepdims=True) + 1e-6) * HD ** -0.5)).astype(bf16)
        k = (b * lax.rsqrt(jnp.sum(b * b, -1, keepdims=True) + 1e-6)).astype(bf16)
        logit = jnp.sum(jnp.where(lane8 == group * hb + h, bl_ref[...], 0.0), -1, keepdims=True)
        beta = jnp.where(valid, jax.nn.sigmoid(logit), 0.0)
        q_ref[:, lanes] = q
        k_ref[:, lanes] = k
        heads.append((q, k, (k.astype(f32) * beta).astype(bf16), (v * beta).astype(bf16)))
    cells = [(h, s) for h in range(hb) for s in spans]
    boths = [dot_nt(jnp.concatenate([heads[h][2][s], heads[h][0][s]], 0), heads[h][1][s]) for h, s in cells]
    invs = unit_lower_inverses([jnp.where(rows > cols, t[:CHUNK], 0.0) for t in boths], CHUNK)
    invs = [t.astype(bf16) for t in invs]
    blends = [dot(t, jnp.concatenate([heads[h][2][s], heads[h][3][s]], 1)) for t, (h, s) in zip(invs, cells)]
    states = [jnp.concatenate([jnp.zeros((HD, HD), f32), eye], 1)] * hb
    for c, s in enumerate(spans):
        for h in range(hb):
            q, k = heads[h][:2]
            cell = h * count + c
            t_ref[h, c] = invs[cell]
            score = jnp.where(rows >= cols, boths[cell][CHUNK:], 0.0).astype(bf16)
            low = states[h].astype(bf16)
            z_ref[h, c] = low
            both = dot(jnp.concatenate([blends[cell][:, :HD].astype(bf16), q[s]], 0), low)
            err = jnp.concatenate([blends[cell][:, HD:] - both[:CHUNK, :HD], -both[:CHUNK, HD:]], 1).astype(bf16)
            wide = slice(2 * h * HD, 2 * (h + 1) * HD)
            x_ref[s, wide] = err
            o_ref[s, wide] = both[CHUNK:] + dot(score, err)
            states[h] = states[h] + dot_tn(k[s], err)
    for h in range(hb):
        ze_ref[h] = states[h]

def fd(proj, halo, conv_w, logits, nv, hb=1):
    length = proj.shape[0]
    heads = proj.shape[1] // (3 * HD)
    nc = length // CHUNK
    g = heads // hb
    w = hb * HD
    col = lambda off: (lambda i, *_: (0, i + off * g))
    in_specs = [pl.BlockSpec((length, w), col(o)) for o in range(3)]
    in_specs += [pl.BlockSpec((8, w), col(o)) for o in range(3)]
    in_specs += [pl.BlockSpec((KERNEL, w), col(o)) for o in range(3)]
    in_specs += [pl.BlockSpec((length, heads), lambda i, *_: (0, 0))]
    out_shape = (
        jax.ShapeDtypeStruct((length, heads * HD), bf16),
        jax.ShapeDtypeStruct((length, heads * HD), bf16),
        jax.ShapeDtypeStruct((heads, nc, CHUNK, CHUNK), bf16),
        jax.ShapeDtypeStruct((length, heads * 2 * HD), bf16),
        jax.ShapeDtypeStruct((length, heads * 2 * HD), f32),
        jax.ShapeDtypeStruct((heads, nc, HD, 2 * HD), bf16),
        jax.ShapeDtypeStruct((heads, HD, 2 * HD), f32),
    )
    out_specs = (
        pl.BlockSpec((length, w), lambda i, *_: (0, i)),
        pl.BlockSpec((length, w), lambda i, *_: (0, i)),
        pl.BlockSpec((hb, nc, CHUNK, CHUNK), lambda i, *_: (i, 0, 0, 0)),
        pl.BlockSpec((length, 2 * w), lambda i, *_: (0, i)),
        pl.BlockSpec((length, 2 * w), lambda i, *_: (0, i)),
        pl.BlockSpec((hb, nc, HD, 2 * HD), lambda i, *_: (i, 0, 0, 0)),
        pl.BlockSpec((hb, HD, 2 * HD), lambda i, *_: (i, 0, 0)),
    )
    return pl.pallas_call(
        functools.partial(fd_kernel, hb), out_shape=out_shape,
        grid_spec=pltpu.PrefetchScalarGridSpec(num_scalar_prefetch=1, grid=(g,), in_specs=in_specs, out_specs=out_specs,
            scratch_shapes=[pltpu.VMEM((3, length + 8, w), f32)]),
        name="delta_forward",
    )(nv, proj, proj, proj, halo, halo, halo, conv_w, conv_w, conv_w, logits)
def fc_kernel(hb, oq, x, z, s_in, gain, o_ref, m_ref, e_ref, s_ref):
    length = oq.shape[0]
    for h in range(hb):
        lanes = slice(h * HD, (h + 1) * HD)
        left = slice(2 * h * HD, (2 * h + 1) * HD)
        right = slice((2 * h + 1) * HD, 2 * (h + 1) * HD)
        enter = s_in[h]
        out = oq[:, left] + dot(oq[:, right].astype(bf16), enter)
        scale = lax.rsqrt(jnp.mean(out * out, -1, keepdims=True) + 1e-05)
        o_ref[:, lanes] = out.astype(bf16)
        m_ref[:, lanes] = (out * scale * gain[...]).astype(bf16)
        e_ref[:, lanes] = (x[:, left].astype(f32) + dot(x[:, right], enter)).astype(bf16)
        for c in range(length // CHUNK):
            s_ref[h, c] = (z[h, c, :, :HD].astype(f32) + dot(z[h, c, :, HD:], enter)).astype(bf16)

def fc(oq, x, z, s_in, gain, hb=2):
    length = oq.shape[0]
    heads, nc = z.shape[:2]
    w = hb * HD
    tok = lambda m: pl.BlockSpec((length, m * w), lambda i: (0, i))
    return pl.pallas_call(
        functools.partial(fc_kernel, hb),
        out_shape=(
            jax.ShapeDtypeStruct((length, heads * HD), bf16),
            jax.ShapeDtypeStruct((length, heads * HD), bf16),
            jax.ShapeDtypeStruct((length, heads * HD), bf16),
            jax.ShapeDtypeStruct((heads, nc, HD, HD), bf16),
        ),
        grid=(heads // hb,),
        in_specs=[tok(2), tok(2), pl.BlockSpec((hb, nc, HD, 2 * HD), lambda i: (i, 0, 0, 0)),
                  pl.BlockSpec((hb, HD, HD), lambda i: (i, 0, 0)), pl.BlockSpec((1, HD), lambda i: (0, 0))],
        out_specs=(tok(1), tok(1), tok(1), pl.BlockSpec((hb, nc, HD, HD), lambda i: (i, 0, 0, 0))),
        name="heads_out",
    )(oq, x, z, s_in, gain)

def head_beta(logits, head, valid):
    lane = lax.broadcasted_iota(jnp.int32, logits.shape, 1)
    logit = jnp.sum(jnp.where(lane == head, logits, 0.0), -1, keepdims=True)
    return jnp.where(valid, jax.nn.sigmoid(logit), 0.0)

def bd_kernel(hb, nv_ref, gm, o, q, k, t, bl, gain, g_ref, d_ref, de_ref, do_ref, hg_ref):
    length = gm.shape[0]
    count = length // CHUNK
    group = pl.program_id(0)
    valid = lax.broadcasted_iota(jnp.int32, (length, 1), 0) < nv_ref[0]
    rows = lax.broadcasted_iota(jnp.int32, (CHUNK, CHUNK), 0)
    cols = lax.broadcasted_iota(jnp.int32, (CHUNK, CHUNK), 1)
    eye = jnp.where(rows == cols, 1.0, 0.0)
    spans = [slice(c * CHUNK, (c + 1) * CHUNK) for c in range(count)]
    @pl.when(group == 0)
    def _():
        hg_ref[...] = jnp.zeros_like(hg_ref)
    heads = []
    for h in range(hb):
        lanes = slice(h * HD, (h + 1) * HD)
        grad, out = gm[:, lanes].astype(f32), o[:, lanes].astype(f32)
        scale = lax.rsqrt(jnp.mean(out * out, -1, keepdims=True) + 1e-05)
        hg_ref[0:1, :] += jnp.sum(grad * out * scale, 0, keepdims=True)
        scaled = grad * gain[...]
        down = (scale * scaled - scale * scale * scale * out * jnp.mean(scaled * out, -1, keepdims=True)).astype(bf16)
        do_ref[:, lanes] = down
        heads.append((q[:, lanes], k[:, lanes], down, head_beta(bl[...], group * hb + h, valid)))
    cells = [(h, c) for h in range(hb) for c in range(count)]
    scores = [jnp.where(rows >= cols, dot_nt(heads[h][0][spans[c]], heads[h][1][spans[c]]), 0.0).astype(bf16) for h, c in cells]
    errs = [dot_tn(m, heads[h][2][spans[c]]).astype(bf16) for m, (h, c) in zip(scores, cells)]
    firsts = [dot_tn(t[h, c], jnp.concatenate([e, heads[h][1][spans[c]]], 1)) for e, (h, c) in zip(errs, cells)]
    adds = [dot_tn(heads[h][0][spans[c]], heads[h][2][spans[c]]) for h, c in cells]
    states = [jnp.concatenate([jnp.zeros((HD, HD), f32), eye], 1)] * hb
    for c in reversed(range(count)):
        s = spans[c]
        for h in range(hb):
            cell = h * count + c
            low = states[h].astype(bf16)
            d_ref[h, c] = low
            both = dot(firsts[cell][:, HD:].astype(bf16), low)
            full = jnp.concatenate([both[:, :HD] + firsts[cell][:, :HD], both[:, HD:]], 1)
            g_ref[s, 2 * h * HD:2 * (h + 1) * HD] = full.astype(bf16)
            back = (full * heads[h][3][s]).astype(bf16)
            change = dot_tn(heads[h][1][s], back)
            states[h] = states[h] - change + jnp.concatenate([adds[cell], jnp.zeros((HD, HD), f32)], 1)
    for h in range(hb):
        de_ref[h] = states[h]

def bd(gm, o, q, k, t, logits, gain, nv, hb=2):
    length = gm.shape[0]
    heads, nc = t.shape[:2]
    w = hb * HD
    tok = lambda m: pl.BlockSpec((length, m * w), lambda i, *_: (0, i))
    sq = lambda m: pl.BlockSpec((hb, nc, HD, m * HD), lambda i, *_: (i, 0, 0, 0))
    return pl.pallas_call(
        functools.partial(bd_kernel, hb),
        out_shape=(
            jax.ShapeDtypeStruct((length, heads * 2 * HD), bf16),
            jax.ShapeDtypeStruct((heads, nc, HD, 2 * HD), bf16),
            jax.ShapeDtypeStruct((heads, HD, 2 * HD), f32),
            jax.ShapeDtypeStruct((length, heads * HD), bf16),
            jax.ShapeDtypeStruct((8, HD), f32),
        ),
        grid_spec=pltpu.PrefetchScalarGridSpec(
            num_scalar_prefetch=1, grid=(heads // hb,),
            in_specs=[tok(1), tok(1), tok(1), tok(1), sq(1),
                      pl.BlockSpec((length, heads), lambda i, *_: (0, 0)), pl.BlockSpec((1, HD), lambda i, *_: (0, 0))],
            out_specs=(tok(2), sq(2), pl.BlockSpec((hb, HD, 2 * HD), lambda i, *_: (i, 0, 0)), tok(1),
                       pl.BlockSpec((8, HD), lambda i, *_: (0, 0)))),
        name="delta_backward",
    )(nv, gm, o, q, k, t, logits, gain)

TAIL = 16

def bg_kernel(hb, nv_ref, g, d, ds, do, q, k, e, s_c, bl, pq, pk, pv, hq, hk, hv, wq, wk, wv,
              gp_ref, tail_ref, back_ref, conv_ref, gl_ref, ext, gext):
    length = pq.shape[0]
    count = length // CHUNK
    group = pl.program_id(0)
    valid = lax.broadcasted_iota(jnp.int32, (length, 1), 0) < nv_ref[0]
    rows = lax.broadcasted_iota(jnp.int32, (CHUNK, CHUNK), 0)
    cols = lax.broadcasted_iota(jnp.int32, (CHUNK, CHUNK), 1)
    spans = [slice(c * CHUNK, (c + 1) * CHUNK) for c in range(count)]
    weights = (wq, wk, wv)
    pres = []
    for i, (p, h, w) in enumerate(((pq, hq, wq), (pk, hk, wk), (pv, hv, wv))):
        ext[i, 0:8, :] = h[...]
        ext[i, 8:, :] = jnp.where(valid, p[...], 0.0)
        pres.append(conv_rows(ext.at[i], w, length))
    @pl.when(group == 0)
    def _():
        gl_ref[...] = jnp.zeros_like(gl_ref)
    lane8 = lax.broadcasted_iota(jnp.int32, (length, bl.shape[1]), 1)
    grads = ([], [], [])
    for h in range(hb):
        lanes = slice(h * HD, (h + 1) * HD)
        wide = slice(2 * h * HD, (2 * h + 1) * HD)
        wider = slice((2 * h + 1) * HD, 2 * (h + 1) * HD)
        beta = head_beta(bl[...], group * hb + h, valid)
        enter = ds[h]
        full = g[:, wide].astype(f32) + dot(g[:, wider], enter)
        back32 = full * beta
        grads[2].append(back32)
        err = e[:, lanes]
        gl = jnp.sum(full * err.astype(f32), -1, keepdims=True) * (1.0 - beta)
        gl_ref[...] += jnp.where((lane8 == group * hb + h) & valid, gl, 0.0)
        back = back32.astype(bf16)
        nback = (-back32).astype(bf16)
        qh, kh, dh = q[:, lanes], k[:, lanes], do[:, lanes]
        outs = [(d[h, c, :, :HD].astype(f32) + dot(d[h, c, :, HD:], enter)).astype(bf16) for c in range(count)]
        pairs = [dot_nt(jnp.concatenate([dh[s], nback[s]], 0), err[s]) for s in spans]
        pairs = [jnp.concatenate([jnp.where(rows >= cols, p[:CHUNK], 0.0), jnp.where(rows > cols, p[CHUNK:], 0.0)], 0).astype(bf16) for p in pairs]
        first = [dot_nt(jnp.concatenate([dh[s], nback[s]], 0), s_c[h, c]) for c, s in enumerate(spans)]
        second = [dot(p, kh[s]) for p, s in zip(pairs, spans)]
        third = [dot_nt(err[s], o) for o, s in zip(outs, spans)]
        fourth = [dot_tn(p, jnp.concatenate([qh[s], kh[s]], 0)) for p, s in zip(pairs, spans)]
        grads[0].append(jnp.concatenate([a[:CHUNK] + b[:CHUNK] for a, b in zip(first, second)], 0))
        grads[1].append(jnp.concatenate([a[CHUNK:] + b[CHUNK:] + t + f for a, b, t, f in zip(first, second, third, fourth)], 0))
    for i in range(3):
        pre = pres[i]
        sig = jax.nn.sigmoid(pre)
        pieces = []
        for h in range(hb):
            grad = grads[i][h]
            if i < 2:
                raw = (pre * sig)[:, h * HD:(h + 1) * HD]
                scale = lax.rsqrt(jnp.sum(raw * raw, -1, keepdims=True) + 1e-06)
                grad = scale * (grad - scale * scale * raw * jnp.sum(raw * grad, -1, keepdims=True))
                if i == 0:
                    grad = grad * HD ** -0.5
            pieces.append(grad)
        grad = jnp.concatenate(pieces, 1) if hb > 1 else pieces[0]
        grad = grad * sig * (1.0 + pre * (1.0 - sig))
        gext[i, 0:8, :] = jnp.zeros((8, gext.shape[2]), f32)
        gext[i, 8:8 + length, :] = grad
        gext[i, 8 + length:, :] = jnp.zeros((8, gext.shape[2]), f32)
        w = weights[i]
        for j in range(KERNEL):
            conv_ref[i, j:j + 1, :] = jnp.sum(grad * ext[i, 5 + j:5 + j + length, :], 0, keepdims=True)
        total = w[0:1] * gext[i, 3:3 + length + 8, :]
        for j in range(1, KERNEL):
            total = total + w[j:j + 1] * gext[i, 3 - j:3 - j + length + 8, :]
        back_ref[i] = total[:8]
        tail_ref[i] = total[8 + length - TAIL:]
        gp_ref[i] = jnp.where(valid, total[8:], 0.0).astype(bf16)

def bg(g, d, ds, do, q, k, e, s_c, logits, proj, halo, conv_w, nv, hb=2):
    length = do.shape[0]
    heads, nc = d.shape[:2]
    w = hb * HD
    groups = heads // hb
    tok = lambda m: pl.BlockSpec((length, m * w), lambda i, *_: (0, i))
    sq = lambda m: pl.BlockSpec((hb, nc, HD, m * HD), lambda i, *_: (i, 0, 0, 0))
    col = lambda off: (lambda i, *_: (0, i + off * groups))
    three = lambda n: pl.BlockSpec((3, n, w), lambda i, *_: (0, 0, i))
    in_specs = [tok(2), sq(2), pl.BlockSpec((hb, HD, HD), lambda i, *_: (i, 0, 0)), tok(1), tok(1), tok(1), tok(1), sq(1),
                pl.BlockSpec((length, heads), lambda i, *_: (0, 0))]
    in_specs += [pl.BlockSpec((length, w), col(o)) for o in range(3)]
    in_specs += [pl.BlockSpec((8, w), col(o)) for o in range(3)]
    in_specs += [pl.BlockSpec((KERNEL, w), col(o)) for o in range(3)]
    width = heads * HD
    return pl.pallas_call(
        functools.partial(bg_kernel, hb),
        out_shape=(
            jax.ShapeDtypeStruct((3, length, width), bf16),
            jax.ShapeDtypeStruct((3, TAIL, width), f32),
            jax.ShapeDtypeStruct((3, 8, width), f32),
            jax.ShapeDtypeStruct((3, KERNEL, width), f32),
            jax.ShapeDtypeStruct((length, heads), f32),
        ),
        grid_spec=pltpu.PrefetchScalarGridSpec(
            num_scalar_prefetch=1, grid=(groups,), in_specs=in_specs,
            out_specs=(three(length), three(TAIL), three(8), three(KERNEL), pl.BlockSpec((length, heads), lambda i, *_: (0, 0))),
            scratch_shapes=[pltpu.VMEM((3, length + 8, w), f32), pltpu.VMEM((3, length + 16, w), f32)]),
        name="mixer_gradients",
    )(nv, g, d, ds, do, q, k, e, s_c, logits, proj, proj, proj, halo, halo, halo, conv_w, conv_w, conv_w)


def passed_along(value, axis, steps):
    count = lax.axis_size(axis)
    first, last = (max(0, -steps), min(count, count - steps))
    return lax.ppermute(value, axis, [(source, source + steps) for source in range(first, last)])


def apply_map(matrix, tensor):
    return jnp.einsum("hij,hjk->hik", matrix, tensor, precision=lax.Precision.HIGHEST)


def gathered(shard):
    rows = shard.shape[0] // lax.axis_size("ctx")
    mine = lax.dynamic_slice_in_dim(shard, lax.axis_index("ctx") * rows, rows, 0)
    return lax.all_gather(mine, ("fsdp", "ctx"), axis=0, tiled=True)


def summed(partial):
    share = lax.psum_scatter(partial.astype(bf16), ("fsdp", "ctx"), scatter_dimension=0, tiled=True)
    return lax.psum(share, "dp").astype(f32)


def local(
    inputs,
    lengths,
    cotangent,
    norm_gain1,
    w_qkv,
    w_beta,
    conv_weight,
    head_gain,
    w_out,
    norm_gain2,
    w_gateup,
    w_down,
):
    tokens_in = inputs[0].astype(f32)
    piece_len, model_width = tokens_in.shape
    heads = w_beta.shape[1]
    width = heads * HD
    start = lax.axis_index("ctx") * piece_len
    left_valid = lengths - start
    positions = start + jnp.arange(piece_len, dtype=jnp.int32)
    valid = (positions < lengths[0]).astype(f32)
    mixed = jnp.concatenate([w_qkv, jnp.pad(w_beta, ((0, 0), (0, HD - heads)))], 1)
    mixed_full = gathered(mixed)
    out_full = gathered(w_out)
    gateup_full = gathered(w_gateup)
    down_full = gathered(w_down)
    qkv_full, beta_full = mixed_full[:, : 3 * width], mixed_full[:, 3 * width :]
    scale_one = lax.rsqrt(jnp.mean(tokens_in * tokens_in, -1, keepdims=True) + 1e-06)
    normed_one = (tokens_in * scale_one * norm_gain1).astype(bf16)
    projected = jnp.dot(normed_one, qkv_full, preferred_element_type=f32)
    beta_logits = jnp.dot(normed_one, beta_full, preferred_element_type=f32)[:, :heads]
    last_rows = jnp.where(valid[piece_len - 8 :, None] > 0, projected[piece_len - 8 :], 0.0)
    halo = passed_along(last_rows.astype(bf16), "ctx", 1).astype(f32)
    queries, keys, inverse, errors, outs, states, ends = fd(
        projected, halo, conv_weight, beta_logits, left_valid, hb=2
    )
    local_end, transition = ends[:, :, :HD], ends[:, :, HD:]
    zero_memory = jnp.zeros((heads, HD, HD), f32)

    def relay_forward(step_index, memory):
        return passed_along(
            (apply_map(transition, memory) + local_end).astype(bf16), "ctx", 1
        ).astype(f32)

    memory_in = passed_along(local_end.astype(bf16), "ctx", 1)
    memory_in = lax.fori_loop(
        0, lax.axis_size("ctx") - 2, relay_forward, memory_in.astype(f32)
    ).astype(bf16)
    heads_out, merged, errors, states = fc(outs, errors, states, memory_in, head_gain[None])
    attention = jnp.dot(merged, out_full, preferred_element_type=f32)
    middle = tokens_in + attention
    scale_two = lax.rsqrt(jnp.mean(middle * middle, -1, keepdims=True) + 1e-06)
    normed_two = (middle * scale_two * norm_gain2).astype(bf16)
    gate_up = jnp.dot(normed_two, gateup_full, preferred_element_type=f32)
    ff_width = gate_up.shape[1] // 2
    gate_part = gate_up[:, :ff_width]
    up_part = gate_up[:, ff_width:]
    gate_sig = jax.nn.sigmoid(gate_part)
    hidden = (gate_part * gate_sig * up_part).astype(bf16)
    feed_out = jnp.dot(hidden, down_full, preferred_element_type=f32)
    output = (middle + feed_out).astype(bf16)
    contract_cols = (((1,), (1,)), ((), ()))
    contract_rows = (((0,), (0,)), ((), ()))
    masked_cotangent = cotangent[0].astype(f32) * valid[:, None]
    grad_feed = masked_cotangent.astype(bf16)
    grad_hidden = lax.dot_general(grad_feed, down_full, contract_cols, preferred_element_type=f32)
    grad_gate = grad_hidden * up_part * gate_sig * (1.0 + gate_part * (1.0 - gate_sig))
    grad_up = grad_hidden * gate_part * gate_sig
    grad_gate_up = jnp.concatenate([grad_gate, grad_up], 1).astype(bf16)
    down_total = summed(
        lax.dot_general(hidden, grad_feed, contract_rows, preferred_element_type=f32)
    )
    gateup_total = summed(
        lax.dot_general(normed_two, grad_gate_up, contract_rows, preferred_element_type=f32)
    )
    grad_normed_two = lax.dot_general(
        grad_gate_up, gateup_full, contract_cols, preferred_element_type=f32
    )
    gain_two_term = jnp.sum(grad_normed_two * middle * scale_two, 0)
    scaled_two = grad_normed_two * norm_gain2
    grad_middle = (
        masked_cotangent
        + scale_two * scaled_two
        - scale_two
        * scale_two
        * scale_two
        * middle
        * jnp.mean(scaled_two * middle, -1, keepdims=True)
    )
    grad_attention = grad_middle.astype(bf16)
    out_total = summed(
        lax.dot_general(merged, grad_attention, contract_rows, preferred_element_type=f32)
    )
    grad_merged = lax.dot_general(
        grad_attention, out_full, contract_cols, preferred_element_type=f32
    )
    grads, pulls, ends, grad_outs, gain_rows = bd(
        grad_merged, heads_out, queries, keys, inverse, beta_logits, head_gain[None], left_valid
    )
    head_gain_term = gain_rows[0]
    local_part, transposed = ends[:, :, :HD], ends[:, :, HD:]

    def relay_backward(step_index, memory_grad):
        return passed_along(
            (apply_map(transposed, memory_grad) + local_part).astype(bf16), "ctx", -1
        ).astype(f32)

    grad_memory = passed_along(local_part.astype(bf16), "ctx", -1)
    grad_memory = lax.fori_loop(
        0, lax.axis_size("ctx") - 2, relay_backward, grad_memory.astype(f32)
    ).astype(bf16)
    grad_three, tails, returns, conv_terms, grad_logits = bg(
        grads, pulls, grad_memory, grad_outs, queries, keys, errors, states, beta_logits,
        projected, halo, conv_weight, left_valid,
    )
    returned = passed_along(returns.astype(bf16), "ctx", -1).astype(f32)
    ending = jnp.where(
        valid[None, piece_len - 8 :, None] > 0, tails[:, TAIL - 8 :] + returned, 0.0
    ).astype(bf16)
    grad_three = lax.dynamic_update_slice(grad_three, ending, (0, piece_len - 8, 0))
    grad_projected = jnp.concatenate([grad_three[0], grad_three[1], grad_three[2]], 1)
    grad_logits = jnp.pad(grad_logits, ((0, 0), (0, HD - heads))).astype(bf16)
    grad_mixed = jnp.concatenate([grad_projected, grad_logits], 1)
    grad_normed_one = lax.dot_general(
        grad_mixed, mixed_full, contract_cols, preferred_element_type=f32
    )
    gain_one_term = jnp.sum(grad_normed_one * tokens_in * scale_one, 0)
    scaled_one = grad_normed_one * norm_gain1
    grad_tokens = (
        grad_middle
        + scale_one * scaled_one
        - scale_one
        * scale_one
        * scale_one
        * tokens_in
        * jnp.mean(scaled_one * tokens_in, -1, keepdims=True)
    )
    mixed_total = summed(
        lax.dot_general(normed_one, grad_mixed, contract_rows, preferred_element_type=f32)
    )
    conv_terms = jnp.concatenate([conv_terms[0], conv_terms[1], conv_terms[2]], 1)
    small = jnp.concatenate(
        [gain_one_term, gain_two_term, head_gain_term, conv_terms.reshape(-1)], 0
    )
    small = lax.psum(small, ("dp", "fsdp", "ctx"))
    cuts = [model_width, 2 * model_width, 2 * model_width + HD]
    gain_one, gain_two, gain_head, conv_total = jnp.split(small, cuts)
    return (
        output[None],
        grad_tokens.astype(bf16)[None],
        gain_one,
        mixed_total[:, : 3 * width],
        mixed_total[:, 3 * width : 3 * width + heads],
        conv_total.reshape(conv_weight.shape),
        gain_head,
        out_total,
        gain_two,
        gateup_total,
        down_total,
    )


def solution(mesh):
    placed = (
        P(("dp", "fsdp"), "ctx", None),
        P(("dp", "fsdp")),
        P(("dp", "fsdp"), "ctx", None),
        P(),
        P("fsdp", None),
        P("fsdp", None),
        P(),
        P(),
        P("fsdp", None),
        P(),
        P("fsdp", None),
        P("fsdp", None),
    )
    return jax.shard_map(
        local,
        mesh=mesh,
        in_specs=placed,
        out_specs=(
            P(("dp", "fsdp"), "ctx", None),
            P(("dp", "fsdp"), "ctx", None),
            P(),
            P(("fsdp", "ctx"), None),
            P(("fsdp", "ctx"), None),
            P(),
            P(),
            P(("fsdp", "ctx"), None),
            P(),
            P(("fsdp", "ctx"), None),
            P(("fsdp", "ctx"), None),
        ),
        check_vma=False,
    )
```

time: 2320 us -> 718 us (0.31)
  other arithmetic: 1100 us -> 18.7 us
  matrix products: 508 us -> 99.9 us
  waiting for transfers between devices: 513 us -> 433 us
  local copies, waits for them, and re-layouts: 97.5 us -> 21.6 us
  Pallas kernels: 0 us -> 71.8 us
    another operation x105 -> x1, other arithmetic: 999 us -> 0.97 us  [the longest x96 999 us: span_factors(): jax.scipy.linalg.solve_triangular(system, right_side, lower=True, unit_di...]
    dot_general x238 -> x10, matrix products: 414 us -> 77.1 us  [the longest x1 13.2 us: local(): gate_up = jnp.dot(normed_two, gateup_full, preferred_element_type=f32)]
    reduce_scatter x2 -> x4, waiting for transfers between devices: 386 us -> 207 us  [summed(): lax.psum_scatter(partial.astype(bf16), ('fsdp', 'ctx'), scatter_dimension...]
    all_gather x4, waiting for transfers between devices: 97.8 us -> 191 us  [gathered(): return lax.all_gather(mine, ('fsdp', 'ctx'), axis=0, tiled=True)]
    pallas_call x0 -> x4, Pallas kernels: none -> 71.8 us  [the longest x1 27.9 us: fd(): pl.pallas_call(functools.partial(fd_kernel, hb), out_shape=out_shape, gri...]
    another operation x32 -> x0, matrix products: 68.7 us -> none  [span_factors(): jax.scipy.linalg.solve_triangular(system, right_side, lower=True, unit_di...]
    dynamic_update_slice x48 -> x0, local copies, waits for them, and re-layouts: 32.7 us -> none  [delta_outputs(): memory_end, outputs = lax.scan(span_output, memory_matrix, blocks)]
    mul x11 -> x0, other arithmetic: 26.8 us -> none  [the longest x1 12.9 us: local(): activated = conv_pre * gate_conv]
  transfers between devices with their start and end apart: 11 -> 13, of which waited for: 5 -> 10; matrix products, arithmetic and copies ran while one was open for 69% -> 13% of each run, Pallas kernels for 0% -> 10%
where the time goes in v1:
time: 718 us; the launch traced here: 710 us
  waiting for transfers between devices  433 us (60%)
  matrix products  99.9 us (14%)
  Pallas kernels  71.8 us (10%)
  blocking collectives  42.7 us (6%)
  local copies, waits for them, and re-layouts  21.6 us (3%)
  other arithmetic  18.7 us (3%)
  between operations  15.1 us (2%)
  starting transfers between devices  7.37 us (1%)
    reduce_scatter x4, waiting for transfers between devices, summed(): lax.psum_scatter(partial.astype(bf16), ('fsdp', 'ctx'), scatter_dimension...  207 us
    all_gather x4, waiting for transfers between devices, gathered(): return lax.all_gather(mine, ('fsdp', 'ctx'), axis=0, tiled=True)  191 us
    psum x1, blocking collectives, local(): small = lax.psum(small, ('dp', 'fsdp', 'ctx'))  42.7 us
    psum x1, waiting for transfers between devices, summed(): return lax.psum(share, 'dp').astype(f32)  29.8 us
    pallas_call x1, Pallas kernels, fd(): pl.pallas_call(functools.partial(fd_kernel, hb), out_shape=out_shape, gri...  27.9 us
    pallas_call x1, Pallas kernels, bg(): pl.pallas_call(functools.partial(bg_kernel, hb), out_shape=(jax.ShapeDtyp...  26.5 us
  transfers between devices with their start and end apart: 13, of which 10 were waited for; matrix products, arithmetic and copies ran while one was open for 13% of the time, Pallas kernels for 10%

profile of v1, /device:TPU:10, one launch (start us, length us, event | category | flops | bytes accessed | tf_op | source)
XLA Modules:
  0.0 709.7 jit_solution(8973627995971118003)
XLA Ops:
  7.3 1.0 copy.27
  8.2 2.1 fusion.20
  11.2 1.2 constant_dynamic-slice_fusion.1
  12.5 2.1 constant_dynamic-slice_fusion
  15.8 60.5 %all-gather.5.cloned.1.call-done = bf16[1024,3200]{1,0:T(8,128)(2,1)} async-done(((bf16[128,3200]{1,0:T(8,128)(2,1)}), bf16[1024,3200]{1,0:T(8,128)(2,1)}) %all-gather.5.cloned.1.call-update) | async-done | bytes 6553616 | tf_op jit(solution)/shard_map/all_gather | solution.py:371
  76.3 5.7 fusion.1.pq.pk.pv
  82.0 2.6 copy-done.2
  84.7 2.2 collective-permute-start
  86.9 2.2 fusion.27.bl_ref.bl
  89.7 27.9 %delta_forward.1 = (bf16[512,1024]{1,0:T(8,128)(2,1)}, bf16[512,1024]{1,0:T(8,128)(2,1)}, bf16[8,4,128,128]{3,2,1,0:T(8,128)(2,1)}, bf16[512,2048]{1,0:T(8,128)(...) custom-call(s32[1]{0:T(128)S(6)} %sub.16.nv_ref, f32[512,3072]{1,0:T(8,128)} %copy-done.2, ...), custom_call_target="tpu_custom_call" | custom-call | tf_op jit(solution)/shard_map/delta_forward/pallas_call | solution.py:139
  117.6 1.1 slice.119
  118.7 1.5 collective-permute-start.1
  120.2 1.3 collective-permute-done.1.s_in
  122.3 6.2 heads_out.1
  128.5 3.4 multiply_reduce_fusion.2
  131.9 83.2 %all-gather.9.cloned.1.call-done = bf16[1024,5632]{1,0:T(8,128)(2,1)} async-done(((bf16[128,5632]{1,0:T(8,128)(2,1)}), bf16[1024,5632]{1,0:T(8,128)(2,1)}) %all-gather.9.cloned.1.call-update) | async-done | bytes 11534352 | tf_op jit(solution)/shard_map/all_gather | solution.py:371
  215.1 13.2 %fusion.37 = f32[512,5632]{1,0:T(8,128)} fusion(bf16[1024,5632]{1,0:T(8,128)(2,1)} %all-gather.9.cloned.1.call-done, f32[512,1024]{1,0:T(8,128)S(1)} %get-tuple-element.88, f32[1024]{0:T(1024)S(1)} %copy-done.17, f32[512]{0:T(512)S(1)} %get-tuple-element.86), kind=kOutput, calls=%fused_computation.82 | convolution fusion | flops 5907152896 | bytes 25171968 | tf_op jit(solution)/shard_map/dot_general | solution.py:433
  228.3 47.7 %all-gather.11.cloned.1.call-done = bf16[2816,1024]{1,0:T(8,128)(2,1)} async-done(((bf16[352,1024]{1,0:T(8,128)(2,1)}), bf16[2816,1024]{1,0:T(8,128)(2,1)}) %all-gather.11.cloned.1.call-update) | async-done | bytes 5767184 | tf_op jit(solution)/shard_map/all_gather | solution.py:371
  276.1 12.2 %multiply_convert_fusion.1 = (bf16[512,2816]{1,0:T(8,128)(2,1)}, bf16[512,2816]{1,0:T(8,128)(2,1)}, bf16[512,2816]{1,0:T(8,128)(2,1)}) fusion(f32[512,5632]{1,0:T(8,128)} %fusion.37, bf16[2816,1024]{1,0:T(8,128)(2,1)} %all-gather.11.cloned.1.call-done, bf16[1,512,1024]{2,1,0:T(8,128)(2,1)} %param.14, f32[512]{0:T(512)S(1)} %fusion.31), kind=kOutput, calls=%fused_computation.8 | convolution fusion | flops 2977431552 | bytes 27002880 | tf_op jit(solution)/shard_map/dot_general | solution.py:445
  288.3 11.9 %multiply_reduce_fusion = (f32[1024]{0:T(1024)S(1)}, f32[512]{0:T(512)S(1)}, f32[512,1024]{1,0:T(8,128)S(1)}) fusion(f32[512,1024]{1,0:T(8,128)S(1)} %get-tuple-element.88, f32[512]{0:T(512)S(1)} %get-tuple-element.86, f32[1024]{0:T(1024)S(1)} %copy-done.17, bf16[1024,5632]{1,0:T(8,128)(2,1)} %all-gather.9.cloned.1.call-done, ...), kind=kOutput, calls=%fused_computation.33 | convolution fusion | flops 5920258560 | bytes 21508096 | tf_op jit(solution)/shard_map/dot_general | solution.py:455
  300.2 2.3 fusion.16
  302.6 2.6 convolution_convert_fusion.3
  305.5 7.9 %convolution_convert_fusion.2 = bf16[2816,1024]{1,0:T(8,128)(2,1)} fusion(bf16[512,2816]{1,0:T(8,128)(2,1)} %get-tuple-element.74, bf16[1,512,1024]{2,1,0:T(8,128)(2,1)} %param.14, f32[512]{0:T(512)S(1)} %fusion.31), kind=kOutput, calls=%fused_computation.11 | convolution fusion | flops 2957246464 | bytes 9701376 | tf_op jit(solution)/shard_map/dot_general | solution.py:450
  313.5 4.2 fusion.22.gm
  317.7 11.2 %delta_backward.1 = (bf16[512,2048]{1,0:T(8,128)(2,1)}, bf16[8,4,128,256]{3,2,1,0:T(8,128)(2,1)}, f32[8,128,256]{2,1,0:T(8,128)}, bf16[512,1024]{1,0:T(8,128)(2,1)}, f32[8,128]{1,0:T(8,128)}) custom-call(s32[1]{0:T(128)S(6)} %sub.16.nv_ref, f32[512,1024]{1,0:T(8,128)} %fusion.22.gm, bf16[512,1024]{1,0:T(8,128)(2,1)} %get-tuple-element.37.o, ...), custom_call_target="tpu_custom_call" | custom-call | tf_op jit(solution)/shard_map/delta_backward/pallas_call | solution.py:234
  328.9 1.1 slice.118
  330.0 1.7 collective-permute-start.2
  331.7 1.7 collective-permute-done.2.ds
  334.2 26.5 %mixer_gradients.1 = (bf16[3,512,1024]{2,1,0:T(8,128)(2,1)}, f32[3,16,1024]{2,1,0:T(8,128)}, f32[3,8,1024]{2,1,0:T(8,128)}, f32[3,4,1024]{2,1,0:T(4,128)}, f32[512,8]{1,0:T(8,128)}) custom-call(s32[1]{0:T(128)S(6)} %sub.16.nv_ref, bf16[512,2048]{1,0:T(8,128)(2,1)} %get-tuple-element.41.g, bf16[8,4,128,256]{3,2,1,0:T(8,128)(2,1)} %get-tuple-element.42.d, ...), custom_call_target="tpu_custom_call" | custom-call | tf_op jit(solution)/shard_map/mixer_gradients/pallas_call | solution.py:341
  360.7 0.9 convert_element_type.104
  361.6 1.3 collective-permute-start.3
  362.9 1.0 convert.22
  364.7 1.6 fusion.30
  366.3 2.2 slice_bitcast_fusion.2
  368.5 0.9 copy-done.6
  370.1 6.8 convolution_convert_fusion.1
  377.2 12.2 %convolution_convert_fusion = bf16[1024,5632]{1,0:T(8,128)(2,1)} fusion(bf16[512,2816]{1,0:T(8,128)(2,1)} %get-tuple-element.73, bf16[512,2816]{1,0:T(8,128)(2,1)} %get-tuple-element.72, f32[512,1024]{1,0:T(8,128)} %copy-done.4, f32[1024]{0:T(1024)S(1)} %copy-done.17, f32[512]{0:T(512)S(1)} %get-tuple-element.86), kind=kOutput, calls=%fused_computation | convolution fusion | flops 5924454400 | bytes 19404800 | tf_op jit(solution)/shard_map/dot_general | solution.py:453
  390.2 14.4 %reduce-scatter.11.cloned.1.call-done = bf16[352,1024]{1,0:T(8,128)(2,1)} async-done(((bf16[2816,1024]{1,0:T(8,128)(2,1)}), bf16[352,1024]{1,0:T(8,128)(2,1)}) %reduce-scatter.11.cloned.1.call-update) | async-done | bytes 720912 | tf_op jit(solution)/shard_map/reduce_scatter | solution.py:375
  404.6 73.0 %reduce-scatter.5.cloned.1.call-done = bf16[128,3200]{1,0:T(8,128)(2,1)} async-done(((bf16[1024,3200]{1,0:T(8,128)(2,1)}), bf16[128,3200]{1,0:T(8,128)(2,1)}) %reduce-scatter.5.cloned.1.call-update) | async-done | bytes 819216 | tf_op jit(solution)/shard_map/reduce_scatter | solution.py:375
  477.6 120.0 %reduce-scatter.9.cloned.1.call-done = bf16[128,5632]{1,0:T(8,128)(2,1)} async-done(((bf16[1024,5632]{1,0:T(8,128)(2,1)}), bf16[128,5632]{1,0:T(8,128)(2,1)}) %reduce-scatter.9.cloned.1.call-update) | async-done | bytes 1441808 | tf_op jit(solution)/shard_map/reduce_scatter | solution.py:375
  597.6 8.4 %fusion.18 = bf16[1,512,1024]{2,1,0:T(8,128)(2,1)} fusion(f32[512,1024]{1,0:T(8,128)} %copy-done.4, bf16[512,2816]{1,0:T(8,128)(2,1)} %get-tuple-element.74, bf16[2816,1024]{1,0:T(8,128)(2,1)} %all-gather.11.cloned.1.call-done), kind=kOutput, calls=%fused_computation.43 | convolution fusion | flops 2953838592 | bytes 11796480 | tf_op jit(solution)/shard_map/dot_general | solution.py:439
  606.1 9.1 %fusion.13 = (f32[1024]{0:T(1024)S(1)}, f32[512]{0:T(512)S(1)}, f32[512,1024]{1,0:T(8,128)}) fusion(bf16[1,512,1024]{2,1,0:T(8,128)(2,1)S(1)} %copy-done.3, f32[512]{0:T(512)S(1)} %get-tuple-element.84, f32[1024]{0:T(1024)S(1)} %copy-done.18, bf16[1024,3200]{1,0:T(8,128)(2,1)} %all-gather.5.cloned.1.call-done, bf16[512,8]{1,0:T(8,128)(2,1)S(1)} %convert.22, ...), kind=kOutput, calls=%fused_computation.28 | convolution fusion | flops 3375495680 | bytes 12865536 | tf_op jit(solution)/shard_map/dot_general | solution.py:503
  615.1 42.7 %psum.35 = f32[14464]{0:T(1024)S(1)} all-reduce(f32[14464]{0:T(1024)S(1)} %pad_maximum_fusion.3), channel_id=1, replica_groups=mesh['dp'=4,'fsdp'=4,'ctx'=2] {'dp','fsdp','ctx'}, use_global_device_ids=true, to_apply=%region_6.7 | all-reduce | flops 14464 | bytes 115712 | tf_op jit(solution)/shard_map/psum | solution.py:524
  659.6 3.1 fusion.19
  662.7 29.8 %all-reduce.5.cloned.1.call-done = (bf16[128,3200]{1,0:T(8,128)(2,1)}, bf16[128,1024]{1,0:T(8,128)(2,1)}, bf16[128,5632]{1,0:T(8,128)(2,1)}, bf16[352,1024]{1,0:T(8,128)(2,1)}) async-done(((bf16[128,3200]{1,0:T(8,128)(2,1)}, bf16[128,1024]{1,0:T(8,128)(2,1)}, bf16[128,5632]{1,0:T(8,128)(2,1)}, bf16[352,1024]{1,0:T(8,128)(2,1)}), (bf16[128,3200]{1,0:T(8,128)(2,1)}, bf16[128,1024]{1,0:T(8,128)(2,1)}, ...) | async-done | bytes 3244048 | tf_op jit(solution)/shard_map/psum | solution.py:376
  693.3 2.4 slice.91
  697.2 2.5 convert_element_type.115
  699.7 3.2 convert_element_type.113
  (82 shorter events, 10.6 us)
Async XLA Ops:
  7.2 4.1 copy-start
  7.2 3.2 copy-start.15
  7.2 69.1 %all-gather.5.cloned.1.call-start = ((), (), s32[]{:S(2)}) async-start(), calls=%async_computation.4 | async-start | bytes 7372800 | tf_op jit(solution)/shard_map/all_gather | solution.py:371
  10.4 118.2 %all-gather.7.cloned.1.call-start = ((), (), s32[]{:S(2)}) async-start(), calls=%async_computation.5 | async-start | bytes 2359296 | tf_op jit(solution)/shard_map/all_gather | solution.py:371
  11.2 203.9 %all-gather.9.cloned.1.call-start = ((), (), s32[]{:S(2)}) async-start(), calls=%async_computation.6 | async-start | bytes 12976128 | tf_op jit(solution)/shard_map/all_gather | solution.py:371
  12.4 3.0 copy-start.3
  12.4 63.8 %copy-start.18 = (f32[1024]{0:T(1024)S(1)}, f32[1024]{0:T(1024)}, u32[]{:S(2)}) copy-start(f32[1024]{0:T(1024)} %param.15) | copy-start | bytes 12292
  12.5 263.6 %all-gather.11.cloned.1.call-start = ((), (), s32[]{:S(2)}) async-start(), calls=%async_computation.7 | async-start | bytes 6488064 | tf_op jit(solution)/shard_map/all_gather | solution.py:371
  14.7 375.5 %reduce-scatter.7.cloned.1.call-start = ((), (), s32[]{:S(2)}) async-start(), calls=%async_computation.9 | async-start | bytes 2359296 | tf_op jit(solution)/shard_map/reduce_scatter | solution.py:375
  82.0 2.6 copy-start.2
  84.7 4.3 collective-permute-start
  118.7 2.8 collective-permute-start.1
  121.6 0.7 copy-start.14
  128.5 86.6 %copy-start.17 = (f32[1024]{0:T(1024)S(1)}, f32[1024]{0:T(1024)}, u32[]{:S(2)}) copy-start(f32[1024]{0:T(1024)} %param.21) | copy-start | bytes 12292
  131.9 156.4 %copy-start.4 = (f32[512,1024]{1,0:T(8,128)}, f32[512,1024]{1,0:T(8,128)S(1)}, u32[]{:S(2)}) copy-start(f32[512,1024]{1,0:T(8,128)S(1)} %get-tuple-element.88) | copy-start | bytes 6291460
  288.3 11.9 %copy-start.5 = (bf16[1,512,1024]{2,1,0:T(8,128)(2,1)S(1)}, bf16[1,512,1024]{2,1,0:T(8,128)(2,1)}, u32[]{:S(2)}) copy-start(bf16[1,512,1024]{2,1,0:T(8,128)(2,1)} %param.14) | copy-start | bytes 3145732
  300.2 2.3 copy-start.19
  305.2 99.4 %reduce-scatter.11.cloned.1.call-start = ((), (), s32[]{:S(2)}) async-start(), calls=%async_computation.11 | async-start | bytes 6488064 | tf_op jit(solution)/shard_map/reduce_scatter | solution.py:375
  313.4 164.1 %reduce-scatter.5.cloned.1.call-start = ((), (), s32[]{:S(2)}) async-start(), calls=%async_computation.8 | async-start | bytes 7372800 | tf_op jit(solution)/shard_map/reduce_scatter | solution.py:375
  330.0 3.4 collective-permute-start.2
  333.5 0.7 copy-start.12
  361.6 3.1 collective-permute-start.3
  368.5 1.0 copy-start.6
  368.5 1.3 copy-start.8
  368.5 1.6 copy-start.10
  377.0 220.6 %reduce-scatter.9.cloned.1.call-start = ((), (), s32[]{:S(2)}) async-start(), calls=%async_computation.10 | async-start | bytes 12976128 | tf_op jit(solution)/shard_map/reduce_scatter | solution.py:375
  389.4 303.0 %all-reduce.5.cloned.1.call-start = ((), (), s32[]{:S(2)}) async-start(), calls=%async_computation.12 | async-start | bytes 6488064 | tf_op jit(solution)/shard_map/psum | solution.py:376
  597.6 8.4 %copy-start.16 = (f32[3,4,1024]{2,1,0:T(4,128)S(1)}, f32[3,4,1024]{2,1,0:T(4,128)}, u32[]{:S(2)}) copy-start(f32[3,4,1024]{2,1,0:T(4,128)} %get-tuple-element.52) | copy-start | bytes 147460
  597.6 8.4 %copy-start.7 = (bf16[512,1024]{1,0:T(8,128)(2,1)S(1)}, bf16[512,1024]{1,0:T(8,128)(2,1)}, u32[]{:S(2)}) copy-start(bf16[512,1024]{1,0:T(8,128)(2,1)} %copy-done.6) | copy-start | bytes 3145732
  597.6 8.4 %copy-start.9 = (bf16[512,1024]{1,0:T(8,128)(2,1)S(1)}, bf16[512,1024]{1,0:T(8,128)(2,1)}, u32[]{:S(2)}) copy-start(bf16[512,1024]{1,0:T(8,128)(2,1)} %copy-done.8) | copy-start | bytes 3145732
  597.6 8.4 %copy-start.11 = (bf16[512,1024]{1,0:T(8,128)(2,1)S(1)}, bf16[512,1024]{1,0:T(8,128)(2,1)}, u32[]{:S(2)}) copy-start(bf16[512,1024]{1,0:T(8,128)(2,1)} %copy-done.10) | copy-start | bytes 3145732
  692.5 3.9 copy-start.13
  697.2 5.8 copy-start.1
Sparse Core Ops, SparseCore 0:
  10.5 65.7 all-gather.4
  77.9 30.0 all-gather.6
  110.2 104.8 all-gather.8
  216.6 59.4 all-gather.10
  305.4 32.7 reduce-scatter.6
  340.3 64.2 reduce-scatter.10
  406.9 70.6 reduce-scatter.4
  479.9 117.6 reduce-scatter.8
  601.0 91.4 all-reduce.4

commit v2 on v1

v2 whole, which is shorter than its diff:
```python
import functools
import jax, jax.numpy as jnp
from jax import lax
from jax.experimental import pallas as pl
from jax.experimental.pallas import tpu as pltpu
from jax.sharding import PartitionSpec as P

HD = 128
KERNEL = 4
CHUNK = 128
bf16 = jnp.bfloat16
f32 = jnp.float32

def dot(a, b):
    return jnp.dot(a, b, preferred_element_type=f32)

def dot_nt(a, b):
    return lax.dot_general(a, b, (((1,), (1,)), ((), ())), preferred_element_type=f32)

def dot_tn(a, b):
    return lax.dot_general(a, b, (((0,), (0,)), ((), ())), preferred_element_type=f32)

def halves(a):
    high = a.astype(bf16)
    return high, (a - high.astype(f32)).astype(bf16)

def fine_dot(a, b):
    n = b[0].shape[1]
    left = jnp.concatenate(a, 1)
    row = jnp.concatenate(b, 1)
    both = dot(left, jnp.concatenate([row, row], 0))
    return both[:, :n] + both[:, n:]

def unit_lower_inverses(lowers, size):
    rows = lax.broadcasted_iota(jnp.int32, (size, size), 0)
    cols = lax.broadcasted_iota(jnp.int32, (size, size), 1)
    eye = jnp.where(rows == cols, 1.0, 0.0)
    def joins(b):
        return (rows // (2 * b) == cols // (2 * b)) & ((rows // b) % 2 == 1) & ((cols // b) % 2 == 0)
    mask = joins(1)
    invs = [eye - jnp.where(mask, t, 0.0) for t in lowers]
    b = 2
    while b < size:
        mask = joins(b)
        parts = [halves(jnp.where(mask, t, 0.0)) for t in lowers]
        splits = [halves(t) for t in invs]
        inner = [halves(fine_dot(p, t)) for p, t in zip(parts, splits)]
        invs = [i - fine_dot(t, n) for i, t, n in zip(invs, splits, inner)]
        b *= 2
    return invs

def conv_rows(ref, weight, length):
    total = weight[0:1] * ref[pl.ds(5, length), :]
    for j in range(1, KERNEL):
        total = total + weight[j:j+1] * ref[pl.ds(5 + j, length), :]
    return total


def head_beta(logits, head, valid):
    lane = lax.broadcasted_iota(jnp.int32, logits.shape, 1)
    logit = jnp.sum(jnp.where(lane == head, logits, 0.0), -1, keepdims=True)
    return jnp.where(valid, jax.nn.sigmoid(logit), 0.0)


def mixer_forward_kernel(hb, nv_ref, pq, pk, pv, wq, wk, wv, bl, gain,
                         q_ref, k_ref, t_ref, e_ref, s_ref, o_ref, m_ref, ext):
    length = pq.shape[0]
    valid = lax.broadcasted_iota(jnp.int32, (length, 1), 0) < nv_ref[0]
    rows = lax.broadcasted_iota(jnp.int32, (CHUNK, CHUNK), 0)
    cols = lax.broadcasted_iota(jnp.int32, (CHUNK, CHUNK), 1)
    group = pl.program_id(0)
    acts = []
    for i, (p, w) in enumerate(((pq, wq), (pk, wk), (pv, wv))):
        ext[i, 0:8, :] = jnp.zeros((8, ext.shape[2]), f32)
        ext[i, 8:, :] = jnp.where(valid, p[...], 0.0)
        c = conv_rows(ext.at[i], w, length)
        acts.append(c * jax.nn.sigmoid(c))
    count = length // CHUNK
    spans = [slice(c * CHUNK, (c + 1) * CHUNK) for c in range(count)]
    heads = []
    for h in range(hb):
        lanes = slice(h * HD, (h + 1) * HD)
        a, b, v = (t[:, lanes] for t in acts)
        q = (a * (lax.rsqrt(jnp.sum(a * a, -1, keepdims=True) + 1e-6) * HD ** -0.5)).astype(bf16)
        k = (b * lax.rsqrt(jnp.sum(b * b, -1, keepdims=True) + 1e-6)).astype(bf16)
        beta = head_beta(bl[...], group * hb + h, valid)
        q_ref[:, lanes] = q
        k_ref[:, lanes] = k
        heads.append((q, k, (k.astype(f32) * beta).astype(bf16), (v * beta).astype(bf16)))
    cells = [(h, s) for h in range(hb) for s in spans]
    boths = [dot_nt(jnp.concatenate([heads[h][2][s], heads[h][0][s]], 0), heads[h][1][s]) for h, s in cells]
    invs = unit_lower_inverses([jnp.where(rows > cols, t[:CHUNK], 0.0) for t in boths], CHUNK)
    invs = [t.astype(bf16) for t in invs]
    blends = [dot(t, jnp.concatenate([heads[h][2][s], heads[h][3][s]], 1)) for t, (h, s) in zip(invs, cells)]
    states = [jnp.zeros((HD, HD), f32)] * hb
    for c, s in enumerate(spans):
        for h in range(hb):
            lanes = slice(h * HD, (h + 1) * HD)
            q, k = heads[h][:2]
            cell = h * count + c
            t_ref[h, c] = invs[cell]
            score = jnp.where(rows >= cols, boths[cell][CHUNK:], 0.0).astype(bf16)
            low = states[h].astype(bf16)
            s_ref[h, c] = low
            both = dot(jnp.concatenate([blends[cell][:, :HD].astype(bf16), q[s]], 0), low)
            err = (blends[cell][:, HD:] - both[:CHUNK]).astype(bf16)
            e_ref[s, lanes] = err
            states[h] = states[h] + dot_tn(k[s], err)
            out = both[CHUNK:] + dot(score, err)
            scale = lax.rsqrt(jnp.mean(out * out, -1, keepdims=True) + 1e-05)
            o_ref[s, lanes] = out.astype(bf16)
            m_ref[s, lanes] = (out * scale * gain[...]).astype(bf16)


def heads_per_step(heads):
    return 2 if heads % 2 == 0 else 1


def mixer_forward(projected, conv_w, gain, nv, heads):
    length = projected.shape[0]
    nc = length // CHUNK
    hb = heads_per_step(heads)
    groups = heads // hb
    w = hb * HD
    col = lambda off: (lambda i, *_: (0, i + off * groups))
    tok = pl.BlockSpec((length, w), lambda i, *_: (0, i))
    sq = pl.BlockSpec((hb, nc, HD, HD), lambda i, *_: (i, 0, 0, 0))
    in_specs = [pl.BlockSpec((length, w), col(o)) for o in range(3)]
    in_specs += [pl.BlockSpec((KERNEL, w), col(o)) for o in range(3)]
    in_specs += [pl.BlockSpec((length, HD), lambda i, *_: (0, 3 * heads)), pl.BlockSpec((1, HD), lambda i, *_: (0, 0))]
    flat = jax.ShapeDtypeStruct((length, heads * HD), bf16)
    square = jax.ShapeDtypeStruct((heads, nc, HD, HD), bf16)
    return pl.pallas_call(
        functools.partial(mixer_forward_kernel, hb),
        out_shape=(flat, flat, square, flat, square, flat, flat),
        grid_spec=pltpu.PrefetchScalarGridSpec(
            num_scalar_prefetch=1, grid=(groups,), in_specs=in_specs,
            out_specs=(tok, tok, sq, tok, sq, tok, tok),
            scratch_shapes=[pltpu.VMEM((3, length + 8, w), f32)]),
        name="mixer_forward",
    )(nv, projected, projected, projected, conv_w, conv_w, conv_w, projected, gain)


def mixer_backward_kernel(hb, heads_all, nv_ref, gm, o, q, k, t, e, s_c, bl, pq, pk, pv, wq, wk, wv, gain,
                          gp_ref, conv_ref, hg_ref, ext, gext):
    length = gm.shape[0]
    count = length // CHUNK
    group = pl.program_id(0)
    width = hb * HD
    valid = lax.broadcasted_iota(jnp.int32, (length, 1), 0) < nv_ref[0]
    rows = lax.broadcasted_iota(jnp.int32, (CHUNK, CHUNK), 0)
    cols = lax.broadcasted_iota(jnp.int32, (CHUNK, CHUNK), 1)
    spans = [slice(c * CHUNK, (c + 1) * CHUNK) for c in range(count)]
    logits_at = slice(3 * heads_all * HD, (3 * heads_all + 1) * HD)
    @pl.when(group == 0)
    def _():
        hg_ref[...] = jnp.zeros_like(hg_ref)
        gp_ref[:, logits_at] = jnp.zeros((length, HD), bf16)
    heads = []
    for h in range(hb):
        lanes = slice(h * HD, (h + 1) * HD)
        grad, out = gm[:, lanes].astype(f32), o[:, lanes].astype(f32)
        scale = lax.rsqrt(jnp.mean(out * out, -1, keepdims=True) + 1e-05)
        hg_ref[0:1, :] += jnp.sum(grad * out * scale, 0, keepdims=True)
        scaled = grad * gain[...]
        down = (scale * scaled - scale * scale * scale * out * jnp.mean(scaled * out, -1, keepdims=True)).astype(bf16)
        heads.append((q[:, lanes], k[:, lanes], down, head_beta(bl[...], group * hb + h, valid), e[:, lanes]))
    cells = [(h, c) for h in range(hb) for c in range(count)]
    scores = [jnp.where(rows >= cols, dot_nt(heads[h][0][spans[c]], heads[h][1][spans[c]]), 0.0).astype(bf16) for h, c in cells]
    errs = [dot_tn(m, heads[h][2][spans[c]]).astype(bf16) for m, (h, c) in zip(scores, cells)]
    firsts = [dot_tn(t[h, c], jnp.concatenate([r, heads[h][1][spans[c]]], 1)) for r, (h, c) in zip(errs, cells)]
    adds = [dot_tn(heads[h][0][spans[c]], heads[h][2][spans[c]]) for h, c in cells]
    states = [jnp.zeros((HD, HD), f32)] * hb
    backs, outs, gls = {}, {}, {}
    for c in reversed(range(count)):
        s = spans[c]
        for h in range(hb):
            cell = h * count + c
            low = states[h].astype(bf16)
            outs[h, c] = low
            full = firsts[cell][:, :HD] + dot(firsts[cell][:, HD:].astype(bf16), low)
            beta = heads[h][3][s]
            gls[h, c] = jnp.sum(full * heads[h][4][s].astype(f32), -1, keepdims=True) * (1.0 - beta)
            backs[h, c] = full * beta
            states[h] = states[h] + adds[cell] - dot_tn(heads[h][1][s], backs[h, c].astype(bf16))
    lane = lax.broadcasted_iota(jnp.int32, (length, HD), 1)
    total = jnp.zeros((length, HD), f32)
    grads = ([], [], [])
    for h in range(hb):
        gl = jnp.concatenate([gls[h, c] for c in range(count)], 0)
        total = jnp.where((lane == group * hb + h) & valid, gl, total)
        qh, kh, dh, _, err = heads[h]
        grads[2].append(jnp.concatenate([backs[h, c] for c in range(count)], 0))
        left = [jnp.concatenate([dh[s], (-backs[h, c]).astype(bf16)], 0) for c, s in enumerate(spans)]
        pairs = [dot_nt(p, err[s]) for p, s in zip(left, spans)]
        pairs = [jnp.concatenate([jnp.where(rows >= cols, p[:CHUNK], 0.0), jnp.where(rows > cols, p[CHUNK:], 0.0)], 0).astype(bf16) for p in pairs]
        first = [dot_nt(p, s_c[h, c]) for c, p in enumerate(left)]
        second = [dot(p, kh[s]) for p, s in zip(pairs, spans)]
        third = [dot_nt(err[s], outs[h, c]) for c, s in enumerate(spans)]
        fourth = [dot_tn(p, jnp.concatenate([qh[s], kh[s]], 0)) for p, s in zip(pairs, spans)]
        grads[0].append(jnp.concatenate([a[:CHUNK] + b[:CHUNK] for a, b in zip(first, second)], 0))
        grads[1].append(jnp.concatenate([a[CHUNK:] + b[CHUNK:] + x + y for a, b, x, y in zip(first, second, third, fourth)], 0))
    gp_ref[:, logits_at] = gp_ref[:, logits_at] + total.astype(bf16)
    for i, (p, w) in enumerate(((pq, wq), (pk, wk), (pv, wv))):
        ext[0:8, :] = jnp.zeros((8, width), f32)
        ext[8:, :] = jnp.where(valid, p[...], 0.0)
        pre = conv_rows(ext, w, length)
        sig = jax.nn.sigmoid(pre)
        pieces = []
        for h in range(hb):
            grad = grads[i][h]
            if i < 2:
                raw = (pre * sig)[:, h * HD:(h + 1) * HD]
                scale = lax.rsqrt(jnp.sum(raw * raw, -1, keepdims=True) + 1e-06)
                grad = scale * (grad - scale * scale * raw * jnp.sum(raw * grad, -1, keepdims=True))
                if i == 0:
                    grad = grad * HD ** -0.5
            pieces.append(grad)
        grad = jnp.concatenate(pieces, 1) if hb > 1 else pieces[0]
        grad = grad * sig * (1.0 + pre * (1.0 - sig))
        gext[0:length, :] = grad
        gext[length:, :] = jnp.zeros((8, width), f32)
        at = pl.ds(pl.multiple_of(i * heads_all * HD + group * width, HD), width)
        for j in range(KERNEL):
            conv_ref[j:j + 1, at] = jnp.sum(grad * ext[5 + j:5 + j + length, :], 0, keepdims=True)
        back = w[3:4] * grad
        for j in range(KERNEL - 1):
            back = back + w[j:j + 1] * gext[3 - j:3 - j + length, :]
        gp_ref[:, at] = jnp.where(valid, back, 0.0).astype(bf16)


def mixer_backward(gm, o, q, k, t, e, s_c, projected, conv_w, gain, nv):
    length = gm.shape[0]
    heads, nc = t.shape[:2]
    hb = heads_per_step(heads)
    groups = heads // hb
    w = hb * HD
    tok = pl.BlockSpec((length, w), lambda i, *_: (0, i))
    sq = pl.BlockSpec((hb, nc, HD, HD), lambda i, *_: (i, 0, 0, 0))
    col = lambda off: (lambda i, *_: (0, i + off * groups))
    fixed = lambda shape: pl.BlockSpec(shape, lambda i, *_: (0, 0))
    in_specs = [tok, tok, tok, tok, sq, tok, sq, pl.BlockSpec((length, HD), lambda i, *_: (0, 3 * heads))]
    in_specs += [pl.BlockSpec((length, w), col(n)) for n in range(3)]
    in_specs += [pl.BlockSpec((KERNEL, w), col(n)) for n in range(3)]
    in_specs += [fixed((1, HD))]
    wide = (length, (3 * heads + 1) * HD)
    return pl.pallas_call(
        functools.partial(mixer_backward_kernel, hb, heads),
        out_shape=(
            jax.ShapeDtypeStruct(wide, bf16),
            jax.ShapeDtypeStruct((KERNEL, 3 * heads * HD), f32),
            jax.ShapeDtypeStruct((8, HD), f32),
        ),
        grid_spec=pltpu.PrefetchScalarGridSpec(
            num_scalar_prefetch=1, grid=(groups,), in_specs=in_specs,
            out_specs=(fixed(wide), fixed((KERNEL, 3 * heads * HD)), fixed((8, HD))),
            scratch_shapes=[pltpu.VMEM((length + 8, w), f32), pltpu.VMEM((length + 8, w), f32)]),
        name="mixer_backward",
    )(nv, gm, o, q, k, t, e, s_c, projected, projected, projected, projected, conv_w, conv_w, conv_w, gain)


def xor(value, axis, step):
    return lax.ppermute(value, axis, [(i, i ^ step) for i in range(lax.axis_size(axis))])


def pick(tensor, index, axis=0):
    return lax.dynamic_index_in_dim(tensor, index, axis, keepdims=False)


def added(a, b):
    return (a.astype(f32) + b.astype(f32)).astype(bf16)


def direct():
    return (lax.axis_size("dp"), lax.axis_size("fsdp"), lax.axis_size("ctx")) == (4, 4, 2)


def mixer_columns(weight, heads):
    n = lax.axis_size("ctx")
    view = weight.reshape(weight.shape[0], 3, heads // n, n, HD)
    return pick(view, lax.axis_index("ctx"), 3).reshape(weight.shape[0], -1)


def beta_columns(weight, heads):
    n = lax.axis_size("ctx")
    view = weight.reshape(weight.shape[0], heads // n, n)
    return jnp.pad(pick(view, lax.axis_index("ctx"), 2), ((0, 0), (0, HD - heads // n)))


def feed_columns(weight):
    n = lax.axis_size("ctx")
    view = weight.reshape(weight.shape[0], 2, n, weight.shape[1] // (2 * n))
    return pick(view, lax.axis_index("ctx"), 2).reshape(weight.shape[0], -1)


def after(value, *others):
    return lax.optimization_barrier((value,) + others)


def start_pieces(tags, places, sources, outs, sems, z, d):
    copies = []
    for tag in tags:
        source, at_first, row_step, same, other = tag
        for at, index, row, col in places(tag, z ^ row_step, other if same else d ^ other):
            rows, width = (s.stop - s.start for s in at)
            target = outs[index].at[pl.ds(row, rows), pl.ds(col, width)]
            copy = pltpu.make_async_copy(
                sources[source].at[at_first + at], target, sems.at[len(copies)]
            )
            copy.start()
            copies.append(copy)
    return copies


def positions():
    return jnp.stack([lax.axis_index(a) for a in ("fsdp", "dp", "ctx")]).astype(jnp.int32)


def project_kernel(tags, places, count, where_ref, x_own, x_far, gain, *refs):
    sources = refs[:count]
    normed_ref, out_ref, full_ref, weight, sems, out_sem = refs[count:]
    step, steps = pl.program_id(0), pl.num_programs(0)
    z, d, c = where_ref[0], where_ref[1], where_ref[2]
    kept = pltpu.make_async_copy(weight, full_ref, out_sem)

    @pl.when(step == 0)
    def _():
        for copy in start_pieces(tags, places, sources, (weight,), sems, z, d):
            copy.wait()
        kept.start()

    x = jnp.where(step // (steps // 2) == c, x_own[...], x_far[...]).astype(f32)
    scale = lax.rsqrt(jnp.mean(x * x, -1, keepdims=True) + 1e-06)
    normed = (x * scale * gain[...]).astype(bf16)
    normed_ref[...] = normed
    out_ref[...] = dot(normed, weight[...])

    @pl.when(step == steps - 1)
    def _():
        kept.wait()


def project(x_own, x_far, gain, pieces, width):
    arrays, tags, places = pieces
    rows, depth = x_own.shape
    block = rows // 2
    half = pl.BlockSpec((block, depth), lambda i, *_: (i % 2, 0))
    each = lambda w: pl.BlockSpec((block, w), lambda i, *_: (i, 0))
    anywhere = pl.BlockSpec(memory_space=pl.ANY)
    return pl.pallas_call(
        functools.partial(project_kernel, tags, places, len(arrays)),
        out_shape=(
            jax.ShapeDtypeStruct((2 * rows, depth), bf16),
            jax.ShapeDtypeStruct((2 * rows, width), f32),
            jax.ShapeDtypeStruct((depth, width), bf16),
        ),
        grid_spec=pltpu.PrefetchScalarGridSpec(
            num_scalar_prefetch=1,
            grid=(4,),
            in_specs=[half, half, pl.BlockSpec((1, depth), lambda i, *_: (0, 0))]
            + [anywhere] * len(arrays),
            out_specs=(each(depth), each(width), anywhere),
            scratch_shapes=[
                pltpu.VMEM((depth, width), bf16),
                pltpu.SemaphoreType.DMA((len(tags),)),
                pltpu.SemaphoreType.DMA,
            ],
        ),
        name="projections",
    )(positions(), x_own, x_far, gain, *arrays)


def near_first(i, where):
    return ((where[2] * 2 + i) % 4, 0)


def attend_kernel(tags, places, count, where_ref, merged, *refs):
    sources = refs[:count]
    near, far, full_ref, weight, sems, out_sem = refs[count:]
    step, steps = pl.program_id(0), pl.num_programs(0)
    z, d = where_ref[0], where_ref[1]
    kept = pltpu.make_async_copy(weight, full_ref, out_sem)

    @pl.when(step == 0)
    def _():
        for copy in start_pieces(tags, places, sources, (weight,), sems, z, d):
            copy.wait()
        kept.start()

    total = dot(merged[...], weight[...])

    @pl.when(step < 2)
    def _():
        near[...] = total

    @pl.when(step >= 2)
    def _():
        far[...] = total.astype(bf16)

    @pl.when(step == steps - 1)
    def _():
        kept.wait()


def near_spec(block, width):
    return pl.BlockSpec((block, width), lambda i, *_: (jnp.minimum(i, 1), 0))


def far_spec(block, width):
    return pl.BlockSpec((block, width), lambda i, *_: (jnp.maximum(i - 2, 0), 0))


def attend(merged, pieces, width):
    arrays, tags, places = pieces
    rows, depth = merged.shape
    block = rows // 4
    anywhere = pl.BlockSpec(memory_space=pl.ANY)
    return pl.pallas_call(
        functools.partial(attend_kernel, tags, places, len(arrays)),
        out_shape=(
            jax.ShapeDtypeStruct((rows // 2, width), f32),
            jax.ShapeDtypeStruct((rows // 2, width), bf16),
            jax.ShapeDtypeStruct((depth, width), bf16),
        ),
        grid_spec=pltpu.PrefetchScalarGridSpec(
            num_scalar_prefetch=1,
            grid=(4,),
            in_specs=[pl.BlockSpec((block, depth), near_first)] + [anywhere] * len(arrays),
            out_specs=(near_spec(block, width), far_spec(block, width), anywhere),
            scratch_shapes=[
                pltpu.VMEM((depth, width), bf16),
                pltpu.SemaphoreType.DMA((2 * len(tags),)),
                pltpu.SemaphoreType.DMA,
            ],
        ),
        name="mixer_out",
    )(positions(), merged, *arrays)


def merged_grad_kernel(where_ref, own, far, weight, out):
    grad = jnp.where(pl.program_id(0) < 2, own[...], far[...])
    out[...] = dot_nt(grad, weight[...])


def merged_grad(own, far, weight):
    rows, width = own.shape
    depth = weight.shape[0]
    block = rows // 2
    return pl.pallas_call(
        merged_grad_kernel,
        out_shape=jax.ShapeDtypeStruct((2 * rows, depth), f32),
        grid_spec=pltpu.PrefetchScalarGridSpec(
            num_scalar_prefetch=1,
            grid=(4,),
            in_specs=[
                near_spec(block, width),
                far_spec(block, width),
                pl.BlockSpec((depth, width), lambda i, *_: (0, 0)),
            ],
            out_specs=pl.BlockSpec((block, depth), near_first),
        ),
        name="merged_gradient",
    )(positions(), own, far, weight)


def normed_grad_kernel(where_ref, grad, weight, near, far):
    total = dot_nt(grad[...], weight[...])

    @pl.when(pl.program_id(0) < 2)
    def _():
        near[...] = total

    @pl.when(pl.program_id(0) >= 2)
    def _():
        far[...] = total.astype(bf16)


def normed_grad(grad, weight):
    rows, width = grad.shape
    depth = weight.shape[0]
    block = rows // 4
    return pl.pallas_call(
        normed_grad_kernel,
        out_shape=(
            jax.ShapeDtypeStruct((rows // 2, depth), f32),
            jax.ShapeDtypeStruct((rows // 2, depth), bf16),
        ),
        grid_spec=pltpu.PrefetchScalarGridSpec(
            num_scalar_prefetch=1,
            grid=(4,),
            in_specs=[
                pl.BlockSpec((block, width), near_first),
                pl.BlockSpec((depth, width), lambda i, *_: (0, 0)),
            ],
            out_specs=(near_spec(block, depth), far_spec(block, depth)),
        ),
        name="normed_gradient",
    )(positions(), grad, weight)


def weight_grad_kernel(parts, with_out, where_ref, *refs):
    lefts, grad = refs[:parts], refs[parts]
    z = pl.program_id(0)
    d, c = where_ref[1], where_ref[2]
    first_low, first_high = d % 2 == 0, d // 2 == 0
    total, at = 0.0, 0
    for left in lefts:
        rows = left.shape[0]
        total = total + dot_tn(left[...], grad[at : at + rows, :])
        at += rows
    total = total.astype(bf16)
    short = total.shape[0] // 8
    blocks = [total[i * short : (i + 1) * short] for i in range(8)]
    if with_out:
        merged, own, far = refs[parts + 1 : parts + 4]
        rows, half = own.shape[0], own.shape[1] // 2
        mine = merged[pl.ds(pl.multiple_of(c * rows, rows), rows), :]
        theirs = merged[pl.ds(pl.multiple_of((1 - c) * rows, rows), rows), :]
        out = (dot_tn(mine, own[...]) + dot_tn(theirs, far[...])).astype(bf16)
        lines = short // 2
        for i in range(8):
            part = out[i * lines : (i + 1) * lines]
            part = jnp.concatenate([part[:, :half], part[:, half:]], 0)
            blocks[i] = jnp.concatenate([blocks[i], part], 1)
    low_keep, low_send, high_keep, high_send = refs[-4:]

    @pl.when(z < 2)
    def _():
        for i in range(4):
            a, b = blocks[2 * i], blocks[2 * i + 1]
            low_keep[0, i // 2, i % 2] = jnp.where(first_low, a, b)
            low_send[0, i // 2, i % 2] = jnp.where(first_low, b, a)

    @pl.when(z >= 2)
    def _():
        for i in range(4):
            k = (i // 2) * 4 + i % 2
            a, b = blocks[k], blocks[k + 2]
            high_keep[0, i // 2, i % 2] = jnp.where(first_high, a, b)
            high_send[0, i // 2, i % 2] = jnp.where(first_high, b, a)


def weight_grad(lefts, grad, out=()):
    depth = lefts[0].shape[1] // 4
    width = grad.shape[1] + (out[1].shape[1] // 2 if out else 0)
    short = depth // 8
    shape = jax.ShapeDtypeStruct((2, 2, 2, short, width), bf16)
    low = pl.BlockSpec((1, 2, 2, short, width), lambda i, *_: (jnp.minimum(i, 1), 0, 0, 0, 0))
    high = pl.BlockSpec((1, 2, 2, short, width), lambda i, *_: (jnp.maximum(i - 2, 0), 0, 0, 0, 0))
    whole = lambda a: pl.BlockSpec(a.shape, lambda i, *_: (0, 0))
    column = lambda a: pl.BlockSpec((a.shape[0], a.shape[1] // 4), lambda i, *_: (0, i))
    specs = [column(a) for a in lefts] + [whole(grad)]
    if out:
        specs += [column(out[0]), whole(out[1]), whole(out[2])]
    return pl.pallas_call(
        functools.partial(weight_grad_kernel, len(lefts), bool(out)),
        out_shape=(shape,) * 4,
        grid_spec=pltpu.PrefetchScalarGridSpec(
            num_scalar_prefetch=1, grid=(4,), in_specs=specs, out_specs=(low, low, high, high)
        ),
        name="weight_gradient",
    )(positions(), *lefts, grad, *out)


def down_grad_kernel(hidden, own, far, out):
    rows = own.shape[0]
    total = dot_tn(hidden[:rows, :], own[...]) + dot_tn(hidden[rows:, :], far[...])
    out[...] = total.astype(bf16)


def down_gradient(hidden, own, far):
    rows, width = own.shape
    half = hidden.shape[1]
    return pl.pallas_call(
        down_grad_kernel,
        out_shape=jax.ShapeDtypeStruct((half, width), bf16),
        grid=(half // HD,),
        in_specs=[
            pl.BlockSpec((2 * rows, HD), lambda i: (0, i)),
            pl.BlockSpec((rows, width), lambda i: (0, 0)),
            pl.BlockSpec((rows, width), lambda i: (0, 0)),
        ],
        out_specs=pl.BlockSpec((HD, width), lambda i: (i, 0)),
        name="down_gradient",
    )(hidden, own, far)


def whole_rows(weight):
    return lax.all_gather(weight, "fsdp", axis=0, tiled=True)


def exchange(blocks, axis):
    return lax.all_to_all(blocks, axis, 0, 0, tiled=True)


def to_all(piece, axis):
    return exchange(jnp.broadcast_to(piece, (lax.axis_size(axis),) + piece.shape), axis)


def bounds(total, step):
    return [slice(i, min(i + step, total)) for i in range(0, total, step)]


def feed_kernel(tags, places, count_down, own, where_ref, x_own, x_other, e_own, e_other, *refs):
    count = 1 + max(t[0] for t in tags)
    sources, downs = refs[:count], refs[count : count + count_down]
    hidden_ref, grad_ref, near_out, far_out, near_grad, far_grad = refs[count + count_down : -3]
    gateup, down, sems = refs[-3:]
    step = pl.program_id(0)
    z, d, c = where_ref[0], where_ref[1], where_ref[2]

    @pl.when(step == 0)
    def _():
        copies = start_pieces(tags, places, sources, (gateup,), sems, z, d)
        rows, cols = downs[1].shape[1:]
        for j in range(2):
            for source, at, first in ((downs[0], 2 * c + j, c), (downs[1], j, 1 - c)):
                col = pl.multiple_of(first * cols, HD)
                copy = pltpu.make_async_copy(
                    source.at[at],
                    down.at[pl.ds(j * rows, rows), pl.ds(col, cols)],
                    sems.at[len(copies)],
                )
                copy.start()
                copies.append(copy)
        for copy in copies:
            copy.wait()

    near = step < own
    x = jnp.where(near, x_own[...], x_other[...])
    e = jnp.where(near, e_own[...], e_other[...])
    half = down.shape[0]
    for j in bounds(half, 256):
        up_j = slice(half + j.start, half + j.stop)
        gate = dot(x, gateup[:, j])
        up = dot(x, gateup[:, up_j])
        grad = dot_nt(e, down[j, :])
        sig = jax.nn.sigmoid(gate)
        act = gate * sig
        hidden_ref[:, j] = (act * up).astype(bf16)
        grad_ref[:, j] = (grad * up * sig * (1.0 + gate * (1.0 - sig))).astype(bf16)
        grad_ref[:, up_j] = (grad * act).astype(bf16)
    out = dot(hidden_ref[...], down[...])
    back = dot_nt(grad_ref[...], gateup[...])

    @pl.when(near)
    def _():
        near_out[...] = out
        near_grad[...] = back

    @pl.when(jnp.logical_not(near))
    def _():
        far_out[...] = out.astype(bf16)
        far_grad[...] = back.astype(bf16)


def feed(x_own, x_other, e_own, e_other, wide, down):
    arrays, tags, places = wide
    rows, width = x_own.shape
    others = x_other.shape[0]
    half = 2 * down[1].shape[1]
    block = min(256, rows)
    own, steps = rows // block, (rows + others) // block
    near = lambda w: pl.BlockSpec((block, w), lambda i, *_: (jnp.minimum(i, own - 1), 0))
    far = lambda w: pl.BlockSpec((block, w), lambda i, *_: (jnp.maximum(i - own, 0), 0))
    each = lambda w: pl.BlockSpec((block, w), lambda i, *_: (i, 0))
    anywhere = pl.BlockSpec(memory_space=pl.ANY)
    return pl.pallas_call(
        functools.partial(feed_kernel, tags, places, len(down), own),
        out_shape=(
            jax.ShapeDtypeStruct((rows + others, half), bf16),
            jax.ShapeDtypeStruct((rows + others, 2 * half), bf16),
            jax.ShapeDtypeStruct((rows, width), f32),
            jax.ShapeDtypeStruct((others, width), bf16),
            jax.ShapeDtypeStruct((rows, width), f32),
            jax.ShapeDtypeStruct((others, width), bf16),
        ),
        grid_spec=pltpu.PrefetchScalarGridSpec(
            num_scalar_prefetch=1,
            grid=(steps,),
            in_specs=[near(width), far(width), near(width), far(width)]
            + [anywhere] * (len(arrays) + len(down)),
            out_specs=(each(half), each(2 * half), near(width), far(width), near(width), far(width)),
            scratch_shapes=[
                pltpu.VMEM((width, 2 * half), bf16),
                pltpu.VMEM((half, width), bf16),
                pltpu.SemaphoreType.DMA((4 + len(tags),)),
            ],
        ),
        name="feed_forward",
    )(positions(), x_own, x_other, e_own, e_other, *arrays, *down)


def pack_kernel(heads, where_ref, qkv, beta, out, gateup, all_ref, mixed_ref, wide_ref):
    rows = qkv.shape[0]
    strips = qkv.shape[1] // (2 * HD)
    mixed = (strips + 1) * HD
    width = gateup.shape[1] // 4
    half = out.shape[1] // 2
    short = out.shape[0]
    for c in range(2):

        @pl.when(where_ref[1] == c)
        def _():
            for i in range(strips):
                at = (2 * i + c) * HD
                all_ref[:, i * HD : (i + 1) * HD] = qkv[:, at : at + HD]
            source = lax.broadcasted_iota(jnp.int32, (heads, HD), 0)
            lane = lax.broadcasted_iota(jnp.int32, (heads, HD), 1)
            chosen = (source == 2 * lane + c).astype(f32).astype(bf16)
            all_ref[:, strips * HD : mixed] = dot(beta[...], chosen).astype(bf16)
            for i in range(2):
                at = (2 * i + c) * width
                to = mixed + i * width
                all_ref[:, to : to + width] = gateup[:, at : at + width]

    last = mixed + 2 * width
    all_ref[:short, last:] = out[:, :half]
    all_ref[short:, last:] = out[:, half:]
    for i in range(4):
        mixed_ref[i] = all_ref[:, :mixed]
    wide_ref[...] = all_ref[:, mixed:]


def pack(w_qkv, w_beta, w_out, w_gateup):
    rows, short = w_qkv.shape[0] // 4, HD // 4
    heads = w_beta.shape[1]
    here = jnp.stack([lax.axis_index("dp"), lax.axis_index("ctx")]).astype(jnp.int32)
    mixed = w_qkv.shape[1] // 2 + HD
    wide = w_gateup.shape[1] // 2 + w_out.shape[1] // 2
    fixed = lambda *shape: pl.BlockSpec(shape, lambda i, *_: (0,) * len(shape))
    mine = lambda width: pl.BlockSpec((rows, width), lambda i, at: (at[0], 0))
    shapes = ((rows, mixed + wide), (4, rows, mixed), (rows, wide))
    return pl.pallas_call(
        functools.partial(pack_kernel, heads),
        out_shape=tuple(jax.ShapeDtypeStruct(s, bf16) for s in shapes),
        grid_spec=pltpu.PrefetchScalarGridSpec(
            num_scalar_prefetch=1,
            grid=(1,),
            in_specs=[
                mine(w_qkv.shape[1]),
                mine(heads),
                pl.BlockSpec((short, w_out.shape[1]), lambda i, at: (at[1] * 4 + at[0], 0)),
                mine(w_gateup.shape[1]),
            ],
            out_specs=tuple(fixed(*s) for s in shapes),
        ),
        name="weight_pieces",
    )(here, w_qkv, w_beta, w_out, w_gateup)


def gather_direct(pieces, mixed_piece, wide_piece, down_shard):
    z, c = lax.axis_index("fsdp"), lax.axis_index("ctx")
    own = [pieces] + [xor(pieces, "dp", k) for k in (1, 2, 3)]
    rows = exchange(mixed_piece, "fsdp")
    wide_piece, rows = after(wide_piece, rows)
    wide_rows = [xor(wide_piece, "fsdp", k) for k in (1, 2, 3)]
    rows, *own[1:] = after(rows, *own[1:])
    rest = to_all(jnp.stack([pick(rows, z ^ k) for k in (1, 2, 3)]), "dp")
    half = down_shard.shape[1] // 2
    mine = lax.dynamic_slice_in_dim(down_shard, c * half, half, 1)
    rest, mine, *wide_rows = after(rest, mine, *wide_rows)
    down = to_all(mine, "fsdp")
    half = pieces.shape[1] // 3
    low = jnp.stack([w[:, :half] for w in wide_rows])
    high = jnp.stack([w[:, half:] for w in wide_rows])
    low, high = [low, xor(low, "dp", 1)], [high, xor(high, "dp", 2)]
    own_tags = [(k, (), 0, False, k) for k in range(4)]
    mixed_tags = own_tags + [(4, (i, k - 1), k, True, i) for i in range(4) for k in (1, 2, 3)]
    return own, rest, low, high, mixed_tags, down


def spread_further(own, low, high):
    low = low + [xor(low[0], "dp", 2), xor(low[1], "dp", 2)]
    high = [high[0], xor(high[0], "dp", 1), high[1], xor(high[1], "dp", 1)]
    tags = [(k, (), 0, False, k) for k in range(4)]
    tags += [(4 + i, (k - 1,), k, False, i) for i in range(4) for k in (1, 2, 3)]
    tags += [(8 + i, (k - 1,), k, False, i) for i in range(4) for k in (1, 2, 3)]
    return own + low + high, tags


def gather_weights(w_qkv, w_beta, w_out, w_gateup, w_down, heads):
    n, c = lax.axis_size("ctx"), lax.axis_index("ctx")
    if not direct():
        mixed = jnp.concatenate([mixer_columns(w_qkv, heads), beta_columns(w_beta, heads)], 1)
        out = whole_rows(w_out).reshape(heads // n, n, HD, -1)
        down = whole_rows(w_down)
        return (
            whole_rows(mixed),
            whole_rows(feed_columns(w_gateup)),
            pick(out, c, 1).reshape(-1, w_out.shape[1]),
            pick(down.reshape(n, -1, down.shape[1]), c),
        )
    rows, short = w_qkv.shape[0] // 4, HD // 4
    pieces, mixed_piece, wide_piece = pack(w_qkv, w_beta, w_out, w_gateup)
    mixed, width, half = mixed_piece.shape[2], w_gateup.shape[1] // 2, w_out.shape[1] // 2
    own, rest, low, high, mixed_tags, down = gather_direct(
        pieces, mixed_piece, wide_piece, w_down
    )
    cut = low[0].shape[2]

    def mixed_places(tag, z, d):
        row = pl.multiple_of(z * (4 * rows) + d * rows, rows)
        return [((slice(0, rows), slice(0, mixed)), 0, row, 0)]

    def out_places(tag, z, d):
        row = pl.multiple_of(z * HD + d * short, short)
        if tag[0] < 4:
            at = slice(mixed + width, mixed + width + half)
        else:
            at = slice(width - cut, width - cut + half)
        return [
            ((slice(0, short), at), 0, row, 0),
            ((slice(short, 2 * short), at), 0, row, half),
        ]

    def feed_places(tag, z, d):
        row = pl.multiple_of(z * (4 * rows) + d * rows, rows)
        if tag[0] < 4:
            at, col = slice(mixed, mixed + width), 0
        elif tag[0] < 8:
            at, col = slice(0, cut), 0
        else:
            at, col = slice(0, width - cut), cut
        return [((slice(0, rows), at), 0, row, col)]

    def further(full):
        full, low[1], high[1] = after(full, low[1], high[1])
        wide_all, wide_tags = spread_further(own, low, high)
        out_tags = [t for t in wide_tags if not 4 <= t[0] < 8]
        return full, (wide_all, wide_tags, feed_places), (wide_all, out_tags, out_places)

    return (own + [rest], mixed_tags, mixed_places), further, down


def feed_both(normed, grad_feed, gateup, down):
    if direct():
        normed_far, grad_far = xor(normed, "ctx", 1), xor(grad_feed, "ctx", 1)
        theirs = pick(down.reshape((2, 2) + down.shape[1:]), 1 - lax.axis_index("ctx"))
        down = [down, xor(theirs, "ctx", 1)]
        hidden, grad, out, out_far, back, back_far = feed(
            normed, normed_far, grad_feed, grad_far, gateup, down
        )
        out = out + xor(out_far, "ctx", 1).astype(f32)
        back = back + xor(back_far, "ctx", 1).astype(f32)
        return (normed, normed_far), (grad_feed, grad_far), hidden, grad, out, back
    normed, grad_feed = both_pieces(normed), both_pieces(grad_feed)
    gate_up = jnp.dot(normed, gateup, preferred_element_type=f32)
    ff_width = gate_up.shape[1] // 2
    gate_part = gate_up[:, :ff_width]
    up_part = gate_up[:, ff_width:]
    gate_sig = jax.nn.sigmoid(gate_part)
    hidden = (gate_part * gate_sig * up_part).astype(bf16)
    contract_cols = (((1,), (1,)), ((), ()))
    grad_hidden = lax.dot_general(grad_feed, down, contract_cols, preferred_element_type=f32)
    grad_gate = grad_hidden * up_part * gate_sig * (1.0 + gate_part * (1.0 - gate_sig))
    grad = jnp.concatenate([grad_gate, grad_hidden * gate_part * gate_sig], 1).astype(bf16)
    out = own_piece(jnp.dot(hidden, down, preferred_element_type=f32))
    back = own_piece(lax.dot_general(grad, gateup, contract_cols, preferred_element_type=f32))
    return normed, grad_feed, hidden, grad, out, back


def both_pieces(mine):
    n = lax.axis_size("ctx")
    if n != 2:
        return lax.all_gather(mine, "ctx", axis=0, tiled=True)
    other = xor(mine, "ctx", 1)
    first = lax.axis_index("ctx") == 0
    return jnp.concatenate([jnp.where(first, mine, other), jnp.where(first, other, mine)], 0)


def own_piece(partial):
    n = lax.axis_size("ctx")
    rows = partial.shape[0] // n
    if n != 2:
        return lax.psum_scatter(
            partial.astype(bf16), "ctx", scatter_dimension=0, tiled=True
        ).astype(f32)
    here = lax.axis_index("ctx")
    theirs = lax.dynamic_slice_in_dim(partial, (1 - here) * rows, rows, 0).astype(bf16)
    mine = lax.dynamic_slice_in_dim(partial, here * rows, rows, 0)
    return mine.astype(f32) + xor(theirs, "ctx", 1).astype(f32)


def replicas_first(part):
    d = lax.axis_index("dp")
    high, low = d // 2, d % 2
    a, b = part[:2], part[2:]
    got = xor(pick(a, 1 - low, 3), "dp", 1), xor(pick(b, 1 - high, 2), "dp", 2)
    return (pick(a, low, 3), pick(b, high, 2)), got


def replicas_second(kept, got):
    d = lax.axis_index("dp")
    high, low = d // 2, d % 2
    a, b = added(kept[0], got[0]), added(kept[1], got[1])
    got = xor(pick(a, 1 - high, 2), "dp", 2), xor(pick(b, 1 - low, 2), "dp", 1)
    return (pick(a, high, 2), pick(b, low, 2)), got


def rows_sent(kept, got):
    z = lax.axis_index("fsdp")
    part = jnp.concatenate([added(kept[0], got[0]), added(kept[1], got[1])], 0)
    return pick(part, z), [xor(pick(part, z ^ k), "fsdp", k) for k in (1, 2, 3)]


def summed_rows(own, got):
    total = own.astype(f32)
    for part in got:
        total = total + part.astype(f32)
    return total.astype(bf16)


def both_columns(part):
    c = lax.axis_index("ctx")
    other = xor(pick(part, 1 - c), "ctx", 1)
    mine = pick(part, c)
    first = c == 0
    return jnp.stack([jnp.where(first, mine, other), jnp.where(first, other, mine)])


def finish_kernel(moves, source, *outs):
    for at, index, to in moves:
        outs[index][to] = source[at].astype(f32)


def finish(source, moves, shapes, name):
    return pl.pallas_call(
        functools.partial(finish_kernel, moves),
        out_shape=tuple(jax.ShapeDtypeStruct(s, f32) for s in shapes),
        name=name,
    )(source)


def blocks_of(grad, n, z):
    return grad.reshape(z, n, 2, 2, grad.shape[0] // (4 * z * n), grad.shape[1])


def scattered(full):
    share = lax.psum_scatter(full.astype(bf16), ("fsdp", "ctx"), scatter_dimension=0, tiled=True)
    return lax.psum(share, "dp").astype(f32)


def placed_at_ctx(part, axis):
    n = lax.axis_size("ctx")
    shape = [1] * (part.ndim + 1)
    shape[axis] = n
    here = (jnp.arange(n) == lax.axis_index("ctx")).reshape(shape)
    return jnp.where(here, jnp.expand_dims(part, axis), 0)


def sum_columns(grad, views, widths):
    outs, start = [], 0
    for shape, size in zip(views, widths):
        part = grad[:, start : start + size].reshape((grad.shape[0],) + shape)
        full = placed_at_ctx(part, part.ndim - 1)
        outs.append(scattered(full.reshape(grad.shape[0], -1)))
        start += size
    return outs


def added_up(parts):
    total = parts[0].astype(f32)
    for i in range(1, parts.shape[0]):
        total = total + parts[i].astype(f32)
    return total.astype(bf16)


def down_summed(got):
    part = added_up(got)
    rows, cols = part.shape[0], part.shape[1] // 4
    part = added_up(exchange(jnp.transpose(part.reshape(rows, 4, cols), (1, 0, 2)), "dp"))
    pairs = [(z * 2 + c, (2 * c + z // 2) * 2 + z % 2) for z in range(4) for c in range(2)]
    every = to_all(lax.ppermute(part, ("fsdp", "ctx"), pairs), "dp")
    moves = [((i,), 0, (slice(None), slice(i * cols, (i + 1) * cols))) for i in range(4)]
    return finish(every, moves, [(rows, 4 * cols)], "down_total")[0]


def sum_small(vector):
    if not direct():
        return lax.psum(vector, ("dp", "fsdp", "ctx"))
    for axis, step in (("ctx", 1), ("dp", 1), ("dp", 2), ("fsdp", 1), ("fsdp", 2)):
        vector = vector + xor(vector, axis, step)
    return vector


def local(
    inputs,
    lengths,
    cotangent,
    norm_gain1,
    w_qkv,
    w_beta,
    conv_weight,
    head_gain,
    w_out,
    norm_gain2,
    w_gateup,
    w_down,
):
    n = lax.axis_size("ctx")
    heads_all = w_beta.shape[1]
    heads = heads_all // n
    tokens_in = inputs[0].astype(f32)
    piece_len, model_width = tokens_in.shape
    length = piece_len * n
    conv_mine = mixer_columns(conv_weight, heads_all)
    positions_here = jnp.arange(length, dtype=jnp.int32)
    start = lax.axis_index("ctx") * piece_len
    valid = ((start + positions_here[:piece_len]) < lengths[0]).astype(f32)[:, None]
    grad_feed = (cotangent[0].astype(f32) * valid).astype(bf16)
    if direct():
        pieces, further, down = gather_weights(w_qkv, w_beta, w_out, w_gateup, w_down, heads_all)
        far_rows = xor(inputs[0], "ctx", 1)
        normed_one, projected, mixed = project(
            inputs[0], far_rows, norm_gain1[None], pieces, (3 * heads + 1) * HD
        )
        projected, gateup, out = further(projected)
    else:
        mixed, gateup, out, down = gather_weights(
            w_qkv, w_beta, w_out, w_gateup, w_down, heads_all
        )
        tokens_all = both_pieces(inputs[0]).astype(f32)
        scale_all = lax.rsqrt(jnp.mean(tokens_all * tokens_all, -1, keepdims=True) + 1e-06)
        normed_one = (tokens_all * scale_all * norm_gain1).astype(bf16)
        projected = jnp.dot(normed_one, mixed, preferred_element_type=f32)
    queries, keys, inverse, errors, states, heads_out, merged = mixer_forward(
        projected, conv_mine, head_gain[None], lengths, heads
    )
    if direct():
        near, far, out = attend(merged, out, model_width)
        attention = near + xor(far, "ctx", 1).astype(f32)
    else:
        attention = own_piece(jnp.dot(merged, out, preferred_element_type=f32))
    middle = tokens_in + attention
    scale_two = lax.rsqrt(jnp.mean(middle * middle, -1, keepdims=True) + 1e-06)
    normed_two = (middle * scale_two * norm_gain2).astype(bf16)
    normed_two, feed_all, hidden, grad_gate_up, feed_out, grad_normed_two = feed_both(
        normed_two, grad_feed, gateup, down
    )
    output = (middle + feed_out).astype(bf16)
    contract_cols = (((1,), (1,)), ((), ()))
    contract_rows = (((0,), (0,)), ((), ()))
    ff_width = hidden.shape[1]
    if direct():
        down_grad = down_gradient(hidden, *feed_all)
        grad_normed_two, down_grad = after(grad_normed_two, down_grad)
        down_got = exchange(down_grad.reshape(4, down_grad.shape[0] // 4, -1), "fsdp")
    else:
        down_grad = lax.dot_general(
            hidden, feed_all, contract_rows, preferred_element_type=f32
        ).astype(bf16)
        gateup_grad = lax.dot_general(
            normed_two, grad_gate_up, contract_rows, preferred_element_type=f32
        ).astype(bf16)
    gain_two_term = jnp.sum(grad_normed_two * middle * scale_two, 0)
    scaled_two = grad_normed_two * norm_gain2
    grad_middle = (
        grad_feed.astype(f32)
        + scale_two * scaled_two
        - scale_two
        * scale_two
        * scale_two
        * middle
        * jnp.mean(scaled_two * middle, -1, keepdims=True)
    )
    grad_attention = grad_middle.astype(bf16)
    if direct():
        grad_far = xor(grad_attention, "ctx", 1)
        low_kept, low_sent, high_kept, high_sent = weight_grad(
            normed_two, grad_gate_up, (merged, grad_attention, grad_far)
        )
        wide_kept = low_kept, high_kept
        wide_got = xor(low_sent, "dp", 1), xor(high_sent, "dp", 2)
        grad_merged = merged_grad(grad_attention, grad_far, out)
    else:
        grad_attention = both_pieces(grad_attention)
        out_grad = lax.dot_general(
            merged, grad_attention, contract_rows, preferred_element_type=f32
        ).astype(bf16)
        grad_merged = lax.dot_general(
            grad_attention, out, contract_cols, preferred_element_type=f32
        )
    grad_mixed, conv_term, gain_rows = mixer_backward(
        grad_merged, heads_out, queries, keys, inverse, errors, states,
        projected, conv_mine, head_gain[None], lengths,
    )
    if direct():
        grad_mixed, *wide_got = after(grad_mixed, *wide_got)
        wide_kept, wide_got = replicas_second(wide_kept, wide_got)
        low_kept, low_sent, high_kept, high_sent = weight_grad((normed_one,), grad_mixed)
        mixed_kept = low_kept, high_kept
        mixed_got = xor(low_sent, "dp", 1), xor(high_sent, "dp", 2)
        wide_own, wide_got = rows_sent(wide_kept, wide_got)
        near, far = normed_grad(grad_mixed, mixed)
        grad_normed_one = near + xor(far, "ctx", 1).astype(f32)
        mixed_kept, mixed_got = replicas_second(mixed_kept, mixed_got)
        down_total = down_summed(down_got)
        mixed = summed_rows(*rows_sent(mixed_kept, mixed_got))
        wide = summed_rows(wide_own, wide_got)
        feed_part = both_columns(wide[..., : 2 * ff_width])
        wide = to_all(jnp.concatenate([feed_part, wide[..., 2 * ff_width :]], 2), "dp")
        short, rows, half = wide.shape[2], HD // (4 * n), model_width // 2
        moves = []
        for i in range(4):
            for j in range(n):
                lines = slice(i * short, (i + 1) * short)
                for k in range(2):
                    at = slice(k * ff_width, (k + 1) * ff_width)
                    to = (k * n + j) * ff_width
                    moves.append(((i, j, slice(None), at), 0, (lines, slice(to, to + ff_width))))
                for k in range(2):
                    at = slice(k * rows, (k + 1) * rows), slice(2 * ff_width, None)
                    low = j * 4 * rows + i * rows
                    to = slice(low, low + rows), slice(k * half, (k + 1) * half)
                    moves.append(((i, j) + at, 1, to))
        shapes = [(4 * short, 2 * n * ff_width), (4 * n * rows, model_width)]
        gateup_total, out_total = finish(wide, moves, shapes, "wide_totals")
        both = to_all(both_columns(mixed), "dp")
        moves = []
        for i in range(4):
            for j in range(n):
                for k in range(3 * heads):
                    at = (i, j, slice(None), slice(k * HD, (k + 1) * HD))
                    to = (k * n + j) * HD
                    lines = slice(i * short, (i + 1) * short)
                    moves.append((at, 0, (lines, slice(to, to + HD))))
        (qkv_total,) = finish(both, moves, [(4 * short, 3 * heads_all * HD)], "mixed_totals")
        beta_total = both[..., 3 * heads * HD : 3 * heads * HD + heads].astype(f32)
        beta_total = jnp.transpose(beta_total, (0, 2, 3, 1)).reshape(4 * short, heads_all)
    else:
        mixed_grad = lax.dot_general(
            normed_one, grad_mixed, contract_rows, preferred_element_type=f32
        ).astype(bf16)
        grad_normed_one = own_piece(
            lax.dot_general(grad_mixed, mixed, contract_cols, preferred_element_type=f32)
        )
        (gateup_total,) = sum_columns(gateup_grad, [(2, ff_width)], [2 * ff_width])
        down_total = scattered(placed_at_ctx(down_grad, 0).reshape(-1, model_width))
        view = placed_at_ctx(out_grad.reshape(heads, HD, model_width), 1)
        out_total = scattered(view.reshape(-1, model_width))
        views, widths = [(3, heads, HD), (1, heads, 1)], [3 * heads * HD, heads]
        qkv_total, beta_total = sum_columns(mixed_grad, views, widths)
    scale_one = lax.rsqrt(jnp.mean(tokens_in * tokens_in, -1, keepdims=True) + 1e-06)
    gain_one_term = jnp.sum(grad_normed_one * tokens_in * scale_one, 0)
    scaled_one = grad_normed_one * norm_gain1
    grad_tokens = (
        grad_middle
        + scale_one * scaled_one
        - scale_one
        * scale_one
        * scale_one
        * tokens_in
        * jnp.mean(scaled_one * tokens_in, -1, keepdims=True)
    )
    conv_term = placed_at_ctx(conv_term.reshape(KERNEL, 3, heads, HD), 3)
    small = jnp.concatenate([gain_one_term, gain_two_term, gain_rows[0], conv_term.reshape(-1)], 0)
    cuts = [model_width, 2 * model_width, 2 * model_width + HD]
    gain_one, gain_two, gain_head, conv_total = jnp.split(sum_small(small), cuts)
    return (
        output[None],
        grad_tokens.astype(bf16)[None],
        gain_one,
        qkv_total,
        beta_total,
        conv_total.reshape(conv_weight.shape),
        gain_head,
        out_total,
        gain_two,
        gateup_total,
        down_total,
    )


def solution(mesh):
    placed = (
        P(("dp", "fsdp"), "ctx", None),
        P(("dp", "fsdp")),
        P(("dp", "fsdp"), "ctx", None),
        P(),
        P("fsdp", None),
        P("fsdp", None),
        P(),
        P(),
        P("fsdp", None),
        P(),
        P("fsdp", None),
        P("fsdp", None),
    )
    return jax.shard_map(
        local,
        mesh=mesh,
        in_specs=placed,
        out_specs=(
            P(("dp", "fsdp"), "ctx", None),
            P(("dp", "fsdp"), "ctx", None),
            P(),
            P(("fsdp", "ctx"), None),
            P(("fsdp", "ctx"), None),
            P(),
            P(),
            P(("fsdp", "ctx"), None),
            P(),
            P(("fsdp", "ctx"), None),
            P(("fsdp", "ctx"), None),
        ),
        check_vma=False,
    )
```

time: 718 us -> 485 us (0.68)
  waiting for transfers between devices: 433 us -> 169 us
  matrix products: 99.9 us -> 0 us
  Pallas kernels: 71.8 us -> 165 us
  starting transfers between devices: 7.37 us -> 75.8 us
  blocking collectives: 42.7 us -> 0 us
  local copies, waits for them, and re-layouts: 21.6 us -> 36.6 us
  between operations: 15.1 us -> 2.25 us
  other arithmetic: 18.7 us -> 31.4 us
    reduce_scatter x4 -> x0, waiting for transfers between devices: 207 us -> none  [summed(): lax.psum_scatter(partial.astype(bf16), ('fsdp', 'ctx'), scatter_dimension...]
    all_gather x4 -> x0, waiting for transfers between devices: 191 us -> none  [gathered(): return lax.all_gather(mine, ('fsdp', 'ctx'), axis=0, tiled=True)]
    ppermute x4 -> x43, waiting for transfers between devices: 3.91 us -> 133 us  [the longest x42 127 us: xor(): lax.ppermute(value, axis, [(i, i ^ step) for i in range(lax.axis_size(axi...]
    dot_general x13 -> x0, matrix products: 99.9 us -> none  [the longest x1 13.2 us: local(): gate_up = jnp.dot(normed_two, gateup_full, preferred_element_type=f32)]
    pallas_call x4 -> x14, Pallas kernels: 71.8 us -> 165 us  [the longest x1 30.3 us: mixer_backward(): pl.pallas_call(functools.partial(mixer_backward_kernel, hb, heads), out_s...]
    psum x1 -> x0, blocking collectives: 42.7 us -> none  [local(): small = lax.psum(small, ('dp', 'fsdp', 'ctx'))]
    all_to_all x0 -> x8, starting transfers between devices: none -> 39.4 us  [exchange(): return lax.all_to_all(blocks, axis, 0, 0, tiled=True)]
    all_to_all x0 -> x8, waiting for transfers between devices: none -> 36.1 us  [exchange(): return lax.all_to_all(blocks, axis, 0, 0, tiled=True)]
  transfers between devices with their start and end apart: 13 -> 51, of which waited for: 10 -> 23; matrix products, arithmetic and copies ran while one was open for 13% -> 9% of each run, Pallas kernels for 10% -> 24%
where the time goes in v2:
time: 485 us; the launch traced here: 480 us
  waiting for transfers between devices  169 us (35%)
  Pallas kernels  165 us (34%)
  starting transfers between devices  75.8 us (16%)
  local copies, waits for them, and re-layouts  36.6 us (8%)
  other arithmetic  31.4 us (6%)
    ppermute x42, waiting for transfers between devices, xor(): lax.ppermute(value, axis, [(i, i ^ step) for i in range(lax.axis_size(axi...  127 us
    all_to_all x8, starting transfers between devices, exchange(): return lax.all_to_all(blocks, axis, 0, 0, tiled=True)  39.4 us
    all_to_all x8, waiting for transfers between devices, exchange(): return lax.all_to_all(blocks, axis, 0, 0, tiled=True)  36.1 us
    ppermute x42, starting transfers between devices, xor(): lax.ppermute(value, axis, [(i, i ^ step) for i in range(lax.axis_size(axi...  34.5 us
    pallas_call x1, Pallas kernels, mixer_backward(): pl.pallas_call(functools.partial(mixer_backward_kernel, hb, heads), out_s...  30.3 us
    pallas_call x1, Pallas kernels, feed(): pl.pallas_call(functools.partial(feed_kernel, tags, places, len(down), ow...  29.1 us
    pallas_call x1, Pallas kernels, mixer_forward(): pl.pallas_call(functools.partial(mixer_forward_kernel, hb), out_shape=(fl...  25.3 us
    pallas_call x2, Pallas kernels, weight_grad(): pl.pallas_call(functools.partial(weight_grad_kernel, len(lefts), bool(out...  23.9 us
  transfers between devices with their start and end apart: 51, of which 23 were waited for; matrix products, arithmetic and copies ran while one was open for 9% of the time, Pallas kernels for 24%

profile of v2, /device:TPU:10, one launch (start us, length us, event | category | flops | bytes accessed | tf_op | source)
XLA Modules:
  0.0 479.8 jit_solution(9960064693242050742)
XLA Ops:
  2.8 3.4 weight_pieces.1
  6.2 5.3 %all-to-all-start = ((bf16[4,64,1664]{2,1,0:T(8,128)(2,1)}), bf16[4,64,1664]{2,1,0:T(8,128)(2,1)}, u32[]{:S(2)}, u32[]{:S(2)}) async-start(bf16[4,64,1664]{2,1,0:T(8,128)(2,1)} %get-tuple-element.69), calls=%async_computation | async-start | bytes 1703936 | tf_op jit(solution)/shard_map/all_to_all | solution.py:593
  15.0 14.8 %all-to-all-done = bf16[4,64,1664]{2,1,0:T(8,128)(2,1)} async-done(((bf16[4,64,1664]{2,1,0:T(8,128)(2,1)}), bf16[4,64,1664]{2,1,0:T(8,128)(2,1)}, u32[]{:S(2)}, u32[]{:S(2)}) %all-to-all-start) | async-done | bytes 852000 | tf_op jit(solution)/shard_map/all_to_all | solution.py:593
  29.8 10.7 %collective-permute-done.2.refs_2_ = bf16[64,4992]{1,0:T(8,128)(2,1)S(1)} collective-permute-done((bf16[64,4992]{1,0:T(8,128)(2,1)}, bf16[64,4992]{1,0:T(8,128)(2,1)S(1)}, u32[]{:S(2)}, u32[]{:S(2)}) %collective-permute-start.2) | collective-permute-done | bytes 639008 | tf_op jit(solution)/shard_map/ppermute | solution.py:263
  45.2 5.6 %all-to-all-start.1 = ((bf16[4,3,64,1664]{3,2,1,0:T(8,128)(2,1)}), bf16[4,3,64,1664]{3,2,1,0:T(8,128)(2,1)}, u32[]{:S(2)}, u32[]{:S(2)}) async-start(bf16[4,3,64,1664]{3,2,1,0:T(8,128)(2,1)} %broadcast_in_dim.59), calls=%async_computation.1 | async-start | bytes 5111808 | tf_op jit(solution)/shard_map/all_to_all | solution.py:593
  51.0 2.6 collective-permute-start.5
  54.3 11.4 %collective-permute-done.4 = bf16[64,3328]{1,0:T(8,128)(2,1)S(1)} collective-permute-done((bf16[64,3328]{1,0:T(8,128)(2,1)}, bf16[64,3328]{1,0:T(8,128)(2,1)S(1)}, u32[]{:S(2)}, u32[]{:S(2)}) %collective-permute-start.4) | collective-permute-done | bytes 426016 | tf_op jit(solution)/shard_map/ppermute | solution.py:263
  65.7 16.8 %collective-permute-done.5 = bf16[64,3328]{1,0:T(8,128)(2,1)S(1)} collective-permute-done((bf16[64,3328]{1,0:T(8,128)(2,1)}, bf16[64,3328]{1,0:T(8,128)(2,1)S(1)}, u32[]{:S(2)}, u32[]{:S(2)}) %collective-permute-start.5) | collective-permute-done | bytes 426016 | tf_op jit(solution)/shard_map/ppermute | solution.py:263
  82.5 6.4 %collective-permute-done.6 = bf16[64,3328]{1,0:T(8,128)(2,1)S(1)} collective-permute-done((bf16[64,3328]{1,0:T(8,128)(2,1)}, bf16[64,3328]{1,0:T(8,128)(2,1)S(1)}, u32[]{:S(2)}, u32[]{:S(2)}) %collective-permute-start.6) | collective-permute-done | bytes 426016 | tf_op jit(solution)/shard_map/ppermute | solution.py:263
  90.7 4.7 all-to-all-start.2
  101.6 11.4 %projections.1 = (bf16[1024,1024]{1,0:T(8,128)(2,1)}, f32[1024,1664]{1,0:T(8,128)}, bf16[1024,1664]{1,0:T(8,128)(2,1)}) custom-call(s32[3]{0:T(128)} %pad_add_fusion.where_ref, bf16[512,1024]{1,0:T(8,128)(2,1)} %bitcast.120, bf16[512,1024]{1,0:T(8,128)(2,1)} %copy-done.32, f32[1,1024]{1,0:T(1,128)} %bitcast.127, bf16[64,4992]{1,0:T(8,128)(2,1)} %get-tuple-element.67.refs_0_, ...), custom_call_target="tpu_custom_call" | custom-call | tf_op jit(solution)/shard_map/projections/pallas_call | solution.py:350
  117.1 25.3 %mixer_forward.1 = (bf16[1024,512]{1,0:T(8,128)(2,1)}, bf16[1024,512]{1,0:T(8,128)(2,1)}, bf16[4,8,128,128]{3,2,1,0:T(8,128)(2,1)}, bf16[1024,512]{1,0:T(8,128)(...) custom-call(s32[1]{0:T(128)} %copy.54.nv_ref, ...), custom_call_target="tpu_custom_call" | custom-call | tf_op jit(solution)/shard_map/mixer_forward/pallas_call | solution.py:133
  143.6 7.4 %mixer_out.1 = (f32[512,1024]{1,0:T(8,128)}, bf16[512,1024]{1,0:T(8,128)(2,1)}, bf16[512,1024]{1,0:T(8,128)(2,1)}) custom-call(s32[3]{0:T(128)} %pad_add_fusion.where_ref, bf16[1024,512]{1,0:T(8,128)(2,1)} %get-tuple-element.82.merged.refs_3_, bf16[64,4992]{1,0:T(8,128)(2,1)} %get-tuple-element.67.refs_0_, bf16[64,4992]{1,0:T(8,128)(2,1)} %copy-done.10, ...), custom_call_target="tpu_custom_call" | custom-call | tf_op jit(solution)/shard_map/mixer_out/pallas_call | solution.py:418
  154.9 2.5 multiply_reduce_fusion.2
  160.7 3.0 collective-permute-done.14.x_other.refs_1_
  164.6 29.1 %feed_forward.1 = (bf16[1024,1408]{1,0:T(8,128)(2,1)}, bf16[1024,2816]{1,0:T(8,128)(2,1)}, f32[512,1024]{1,0:T(8,128)}, bf16[512,1024]{1,0:T(8,128)(2,1)}, f32[5...) custom-call(s32[3]{0:T(128)} %pad_add_fusion.where_ref, bf16[512,1024]{1,0:T(8,128)(2,1)} %copy-done.4, ...), custom_call_target="tpu_custom_call" | custom-call | tf_op jit(solution)/shard_map/feed_forward/pallas_call | solution.py:668
  194.4 10.6 %down_gradient.1 = bf16[1408,1024]{1,0:T(8,128)(2,1)} custom-call(bf16[1024,1408]{1,0:T(8,128)(2,1)} %get-tuple-element.92.hidden, bf16[512,1024]{1,0:T(8,128)(2,1)} %fusion.7.e_own.own, bf16[512,1024]{1,0:T(8,128)(2,1)} %collective-permute-done.15.e_other.far), custom_call_target="tpu_custom_call" | custom-call | tf_op jit(solution)/shard_map/down_gradient/pallas_call | solution.py:574
  209.0 3.4 fusion.43
  213.5 2.5 collective-permute-done.19.far.refs_5_
  217.0 14.8 %weight_gradient.2 = (bf16[2,2,2,32,3328]{4,3,2,1,0:T(8,128)(2,1)}, bf16[2,2,2,32,3328]{4,3,2,1,0:T(8,128)(2,1)}, bf16[2,2,2,32,3328]{4,3,2,1,0:T(8,128)(2,1)}, bf16[2,2,2,32,3328]{4,3,2,1,0:T(8,128)(2,1)}) custom-call(s32[3]{0:T(128)} %pad_add_fusion.where_ref, bf16[512,1024]{1,0:T(8,128)(2,1)} %copy-done.4, bf16[512,1024]{1,0:T(8,128)(2,1)} %copy-done.18, ...), custom_call_target="tpu_custom_call" | custom-call | tf_op jit(solution)/shard_map/weight_gradient/pallas_call | solution.py:555
  231.8 2.8 copy.45
  237.7 4.6 all-to-all-start.5
  242.3 5.8 %merged_gradient.1.gm = f32[1024,512]{1,0:T(8,128)} custom-call(s32[3]{0:T(128)} %pad_add_fusion.where_ref, bf16[512,1024]{1,0:T(8,128)(2,1)} %copy-done.5, bf16[512,1024]{1,0:T(8,128)(2,1)} %copy-done.19, bf16[512,1024]{1,0:T(8,128)(2,1)} %get-tuple-element.94.weight), custom_call_target="tpu_custom_call" | custom-call | tf_op jit(solution)/shard_map/merged_gradient/pallas_call | solution.py:449
  248.1 30.3 %mixer_backward.1 = (bf16[1024,1664]{1,0:T(8,128)(2,1)}, f32[4,1536]{1,0:T(4,128)}, f32[8,128]{1,0:T(8,128)}) custom-call(s32[1]{0:T(128)} %copy.54.nv_ref, f32[1024,512]{1,0:T(8,128)} %merged_gradient.1.gm, bf16[1024,512]{1,0:T(8,128)(2,1)} %get-tuple-element.95.o, bf16[1024,512]{1,0:T(8,128)(2,1)} %get-tuple-element.96.q, ...), custom_call_target="tpu_custom_call" | custom-call | tf_op jit(solution)/shard_map/mixer_backward/pallas_call | solution.py:247
  282.4 2.5 add_convert_fusion
  289.9 9.1 %weight_gradient.3 = (bf16[2,2,2,32,1664]{4,3,2,1,0:T(8,128)(2,1)}, bf16[2,2,2,32,1664]{4,3,2,1,0:T(8,128)(2,1)}, bf16[2,2,2,32,1664]{4,3,2,1,0:T(8,128)(2,1)}, bf16[2,2,2,32,1664]{4,3,2,1,0:T(8,128)(2,1)}) custom-call(s32[3]{0:T(128)} %pad_add_fusion.where_ref, bf16[1024,1024]{1,0:T(8,128)(2,1)} %get-tuple-element.111.refs_0_, ...), custom_call_target="tpu_custom_call" | custom-call | tf_op jit(solution)/shard_map/weight_gradient/pallas_call | solution.py:555
  303.9 9.2 %normed_gradient.1 = (f32[512,1024]{1,0:T(8,128)}, bf16[512,1024]{1,0:T(8,128)(2,1)}) custom-call(s32[3]{0:T(128)} %pad_add_fusion.where_ref, bf16[1024,1664]{1,0:T(8,128)(2,1)} %get-tuple-element.105.grad.refs_1_, bf16[1024,1664]{1,0:T(8,128)(2,1)} %get-tuple-element.106.weight), custom_call_target="tpu_custom_call" | custom-call | tf_op jit(solution)/shard_map/normed_gradient/pallas_call | solution.py:482
  316.8 2.9 collective-permute-start.39
  319.7 8.7 %collective-permute-done.30 = bf16[2,2,2,32,1664]{4,3,2,1,0:T(8,128)(2,1)} collective-permute-done((bf16[2,2,2,32,1664]{4,3,2,1,0:T(8,128)(2,1)}, bf16[2,2,2,32,1664]{4,3,2,1,0:T(8,128)(2,1)}, u32[]{:S(2)}, u32[]{:S(2)}) %collective-permute-start.30) | collective-permute-done | bytes 852000 | tf_op jit(solution)/shard_map/ppermute | solution.py:263
  335.3 12.9 %collective-permute-done.39 = bf16[2,32,3328]{2,1,0:T(8,128)(2,1)S(1)} collective-permute-done((bf16[2,32,3328]{2,1,0:T(8,128)(2,1)S(1)}, bf16[2,32,3328]{2,1,0:T(8,128)(2,1)S(1)}, u32[]{:S(2)}, u32[]{:S(2)}) %collective-permute-start.39) | collective-permute-done | bytes 426016 | tf_op jit(solution)/shard_map/ppermute | solution.py:263
  348.2 9.1 %collective-permute-done.40 = bf16[2,32,3328]{2,1,0:T(8,128)(2,1)S(1)} collective-permute-done((bf16[2,32,3328]{2,1,0:T(8,128)(2,1)S(1)}, bf16[2,32,3328]{2,1,0:T(8,128)(2,1)S(1)}, u32[]{:S(2)}, u32[]{:S(2)}) %collective-permute-start.40) | collective-permute-done | bytes 426016 | tf_op jit(solution)/shard_map/ppermute | solution.py:263
  358.4 2.9 collective-permute-start.33
  362.0 4.6 collective-permute-done.32
  366.6 9.6 %collective-permute-done.33 = bf16[2,32,1664]{2,1,0:T(8,128)(2,1)S(1)} collective-permute-done((bf16[2,32,1664]{2,1,0:T(8,128)(2,1)S(1)}, bf16[2,32,1664]{2,1,0:T(8,128)(2,1)S(1)}, u32[]{:S(2)}, u32[]{:S(2)}) %collective-permute-start.33) | collective-permute-done | bytes 213024 | tf_op jit(solution)/shard_map/ppermute | solution.py:263
  376.2 3.9 collective-permute-done.34
  380.3 2.3 add_convert_fusion.5
  384.1 4.2 all-to-all-start.6
  388.4 10.4 %all-to-all-done.6 = bf16[4,352,256]{2,1,0:T(8,128)(2,1)S(1)} async-done(((bf16[4,352,256]{2,1,0:T(8,128)(2,1)}), bf16[4,352,256]{2,1,0:T(8,128)(2,1)S(1)}, u32[]{:S(2)}, u32[]{:S(2)}) %all-to-all-start.6) | async-done | bytes 720928 | tf_op jit(solution)/shard_map/all_to_all | solution.py:593
  399.9 4.1 all-to-all-start.3
  404.1 11.0 %all-to-all-done.3.source = bf16[4,2,32,1664]{3,2,1,0:T(8,128)(2,1)S(1)} async-done(((bf16[4,2,32,1664]{3,2,1,0:T(8,128)(2,1)}), bf16[4,2,32,1664]{3,2,1,0:T(8,128)(2,1)S(1)}, u32[]{:S(2)}, u32[]{:S(2)}) %all-to-all-start.3) | async-done | bytes 852000 | tf_op jit(solution)/shard_map/all_to_all | solution.py:593
  416.5 5.1 %all-to-all-start.4 = ((bf16[4,2,32,3328]{3,2,1,0:T(8,128)(2,1)}), bf16[4,2,32,3328]{3,2,1,0:T(8,128)(2,1)}, u32[]{:S(2)}, u32[]{:S(2)}) async-start(bf16[4,2,32,3328]{3,2,1,0:T(8,128)(2,1)} %broadcast_in_dim.69), calls=%async_computation.4 | async-start | bytes 3407872 | tf_op jit(solution)/shard_map/all_to_all | solution.py:593
  423.1 18.2 %collective-permute-done.24 = f32[14464]{0:T(1024)S(1)} collective-permute-done((f32[14464]{0:T(1024)S(1)}, f32[14464]{0:T(1024)S(1)}, u32[]{:S(2)}, u32[]{:S(2)}) %collective-permute-start.24) | collective-permute-done | bytes 57888 | tf_op jit(solution)/shard_map/ppermute | solution.py:263
  443.1 2.5 collective-permute-done.25
  451.5 6.1 %collective-permute-done.42 = bf16[352,256]{1,0:T(8,128)(2,1)S(1)} collective-permute-done((bf16[352,256]{1,0:T(8,128)(2,1)S(1)}, bf16[352,256]{1,0:T(8,128)(2,1)S(1)}, u32[]{:S(2)}, u32[]{:S(2)}) %collective-permute-start.42) | collective-permute-done | bytes 180256 | tf_op jit(solution)/shard_map/ppermute | solution.py:974
  458.6 5.9 %all-to-all-start.7 = ((bf16[4,352,256]{2,1,0:T(8,128)(2,1)}), bf16[4,352,256]{2,1,0:T(8,128)(2,1)}, u32[]{:S(2)}, u32[]{:S(2)}) async-start(bf16[4,352,256]{2,1,0:T(8,128)(2,1)} %broadcast_in_dim.70), calls=%async_computation.7 | async-start | bytes 1441792 | tf_op jit(solution)/shard_map/all_to_all | solution.py:593
  464.4 3.6 fusion.11
  471.4 2.5 mixed_totals.1
  473.9 3.4 wide_totals.1
  (231 shorter events, 87.7 us)
Async XLA Ops:
  6.2 23.6 %all-to-all-start = ((bf16[4,64,1664]{2,1,0:T(8,128)(2,1)}), bf16[4,64,1664]{2,1,0:T(8,128)(2,1)}, u32[]{:S(2)}, u32[]{:S(2)}) async-start(bf16[4,64,1664]{2,1,0:T(8,128)(2,1)} %get-tuple-element.69), calls=%async_computation | async-start | bytes 1703936 | tf_op jit(solution)/shard_map/all_to_all | solution.py:593
  11.5 18.2 %collective-permute-start.1 = (bf16[64,4992]{1,0:T(8,128)(2,1)}, bf16[64,4992]{1,0:T(8,128)(2,1)S(1)}, u32[]{:S(2)}, u32[]{:S(2)}) collective-permute-start(bf16[64,4992]{1,0:T(8,128)(2,1)} %get-tuple-element.67.refs_0_), channel_id=1, source_target_pairs={{0,8},{8,0},{16,24},{24,16},{1,9},{9,1},{17,25},{25,17},{2,10},{10... | collective-permute-start | bytes 1916936 | tf_op jit(solution)/shard_map/ppermute | solution.py:263
  12.0 28.4 %collective-permute-start.2 = (bf16[64,4992]{1,0:T(8,128)(2,1)}, bf16[64,4992]{1,0:T(8,128)(2,1)S(1)}, u32[]{:S(2)}, u32[]{:S(2)}) collective-permute-start(bf16[64,4992]{1,0:T(8,128)(2,1)} %get-tuple-element.67.refs_0_), channel_id=1, source_target_pairs={{0,16},{8,24},{16,0},{24,8},{1,17},{9,25},{17,1},{25,9},{2,18},{10... | collective-permute-start | bytes 1916936 | tf_op jit(solution)/shard_map/ppermute | solution.py:263
  13.6 28.4 %collective-permute-start.3 = (bf16[64,4992]{1,0:T(8,128)(2,1)}, bf16[64,4992]{1,0:T(8,128)(2,1)S(1)}, u32[]{:S(2)}, u32[]{:S(2)}) collective-permute-start(bf16[64,4992]{1,0:T(8,128)(2,1)} %get-tuple-element.67.refs_0_), channel_id=1, source_target_pairs={{0,24},{8,16},{16,8},{24,0},{1,25},{9,17},{17,9},{25,1},{2,26},{10... | collective-permute-start | bytes 1916936 | tf_op jit(solution)/shard_map/ppermute | solution.py:263
  45.2 43.7 %all-to-all-start.1 = ((bf16[4,3,64,1664]{3,2,1,0:T(8,128)(2,1)}), bf16[4,3,64,1664]{3,2,1,0:T(8,128)(2,1)}, u32[]{:S(2)}, u32[]{:S(2)}) async-start(bf16[4,3,64,1664]{3,2,1,0:T(8,128)(2,1)} %broadcast_in_dim.59), calls=%async_computation.1 | async-start | bytes 5111808 | tf_op jit(solution)/shard_map/all_to_all | solution.py:593
  50.7 14.9 %collective-permute-start.4 = (bf16[64,3328]{1,0:T(8,128)(2,1)}, bf16[64,3328]{1,0:T(8,128)(2,1)S(1)}, u32[]{:S(2)}, u32[]{:S(2)}) collective-permute-start(bf16[64,3328]{1,0:T(8,128)(2,1)} %get-tuple-element.75), channel_id=1, source_target_pairs={{0,2},{2,0},{4,6},{6,4},{1,3},{3,1},{5,7},{7,5},{8,10},{10,8},{12,... | collective-permute-start | bytes 1277960 | tf_op jit(solution)/shard_map/ppermute | solution.py:263
  51.0 31.5 %collective-permute-start.5 = (bf16[64,3328]{1,0:T(8,128)(2,1)}, bf16[64,3328]{1,0:T(8,128)(2,1)S(1)}, u32[]{:S(2)}, u32[]{:S(2)}) collective-permute-start(bf16[64,3328]{1,0:T(8,128)(2,1)} %get-tuple-element.75), channel_id=1, source_target_pairs={{0,4},{2,6},{4,0},{6,2},{1,5},{3,7},{5,1},{7,3},{8,12},{10,14},{12... | collective-permute-start | bytes 1277960 | tf_op jit(solution)/shard_map/ppermute | solution.py:263
  53.7 35.2 %collective-permute-start.6 = (bf16[64,3328]{1,0:T(8,128)(2,1)}, bf16[64,3328]{1,0:T(8,128)(2,1)S(1)}, u32[]{:S(2)}, u32[]{:S(2)}) collective-permute-start(bf16[64,3328]{1,0:T(8,128)(2,1)} %get-tuple-element.75), channel_id=1, source_target_pairs={{0,6},{2,4},{4,2},{6,0},{1,7},{3,5},{5,3},{7,1},{8,14},{10,12},{12... | collective-permute-start | bytes 1277960 | tf_op jit(solution)/shard_map/ppermute | solution.py:263
  90.7 66.7 %all-to-all-start.2 = ((bf16[4,704,512]{2,1,0:T(8,128)(2,1)}), bf16[4,704,512]{2,1,0:T(8,128)(2,1)}, u32[]{:S(2)}, u32[]{:S(2)}) async-start(bf16[4,704,512]{2,1,0:T(8,128)(2,1)} %broadcast_in_dim.61), calls=%async_computation.2 | async-start | bytes 5767168 | tf_op jit(solution)/shard_map/all_to_all | solution.py:593
  95.5 5.2 %collective-permute-start = (bf16[512,1024]{1,0:T(8,128)(2,1)S(1)}, bf16[512,1024]{1,0:T(8,128)(2,1)S(1)}, u32[]{:S(2)}, u32[]{:S(2)}) collective-permute-start(bf16[512,1024]{1,0:T(8,128)(2,1)S(1)} %bitcast.121), channel_id=1, source_target_pairs={{0,1},{1,0},{2,3},{3,2},{4,5},{5,4},{6,7},{7,6},{8,9},{9,8},{10,11... | collective-permute-start | bytes 3145736 | tf_op jit(solution)/shard_map/ppermute | solution.py:263
  95.8 17.3 %collective-permute-start.8 = (bf16[3,64,1664]{2,1,0:T(8,128)(2,1)S(1)}, bf16[3,64,1664]{2,1,0:T(8,128)(2,1)S(1)}, u32[]{:S(2)}, u32[]{:S(2)}) collective-permute-start(bf16[3,64,1664]{2,1,0:T(8,128)(2,1)S(1)} %pad_maximum_fusion.2.refs_8_), channel_id=1, source_target_pairs={{0,16},{8,24},{16,0},{24,8},{1,17},{9,25},{17,1},{25,9},{2,18},{10... | collective-permute-start | bytes 1916936 | tf_op jit(solution)/shard_map/ppermute | solution.py:263
  97.4 17.4 %collective-permute-start.7 = (bf16[3,64,1664]{2,1,0:T(8,128)(2,1)S(1)}, bf16[3,64,1664]{2,1,0:T(8,128)(2,1)}, u32[]{:S(2)}, u32[]{:S(2)}) collective-permute-start(bf16[3,64,1664]{2,1,0:T(8,128)(2,1)S(1)} %pad_maximum_fusion.1.refs_4_), channel_id=1, source_target_pairs={{0,8},{8,0},{16,24},{24,16},{1,9},{9,1},{17,25},{25,17},{2,10},{10... | collective-permute-start | bytes 1916936 | tf_op jit(solution)/shard_map/ppermute | solution.py:263
  98.6 43.9 %collective-permute-start.11 = (bf16[3,64,1664]{2,1,0:T(8,128)(2,1)S(1)}, bf16[3,64,1664]{2,1,0:T(8,128)(2,1)}, u32[]{:S(2)}, u32[]{:S(2)}) collective-permute-start(bf16[3,64,1664]{2,1,0:T(8,128)(2,1)S(1)} %pad_maximum_fusion.2.refs_8_), channel_id=1, source_target_pairs={{0,8},{8,0},{16,24},{24,16},{1,9},{9,1},{17,25},{25,17},{2,10},{10... | collective-permute-start | bytes 1916936 | tf_op jit(solution)/shard_map/ppermute | solution.py:263
  100.1 42.4 %collective-permute-start.9 = (bf16[3,64,1664]{2,1,0:T(8,128)(2,1)S(1)}, bf16[3,64,1664]{2,1,0:T(8,128)(2,1)}, u32[]{:S(2)}, u32[]{:S(2)}) collective-permute-start(bf16[3,64,1664]{2,1,0:T(8,128)(2,1)S(1)} %pad_maximum_fusion.1.refs_4_), channel_id=1, source_target_pairs={{0,16},{8,24},{16,0},{24,8},{1,17},{9,25},{17,1},{25,9},{2,18},{10... | collective-permute-start | bytes 1916936 | tf_op jit(solution)/shard_map/ppermute | solution.py:263
  114.8 27.7 %collective-permute-start.10 = (bf16[3,64,1664]{2,1,0:T(8,128)(2,1)}, bf16[3,64,1664]{2,1,0:T(8,128)(2,1)S(1)}, u32[]{:S(2)}, u32[]{:S(2)}) collective-permute-start(bf16[3,64,1664]{2,1,0:T(8,128)(2,1)} %collective-permute-done.7.refs_5_), channel_id=1, source_target_pairs={{0,16},{8,24},{16,0},{24,8},{1,17},{9,25},{17,1},{25,9},{2,18},{10... | collective-permute-start | bytes 1916936 | tf_op jit(solution)/shard_map/ppermute | solution.py:263
  115.3 27.2 %collective-permute-start.12 = (bf16[3,64,1664]{2,1,0:T(8,128)(2,1)S(1)}, bf16[3,64,1664]{2,1,0:T(8,128)(2,1)S(1)}, u32[]{:S(2)}, u32[]{:S(2)}) collective-permute-start(bf16[3,64,1664]{2,1,0:T(8,128)(2,1)S(1)} %collective-permute-done.8.refs_10_), channel_id=1, source_target_pairs={{0,8},{8,0},{16,24},{24,16},{1,9},{9,1},{17,25},{25,17},{2,10},{10... | collective-permute-start | bytes 1916936 | tf_op jit(solution)/shard_map/ppermute | solution.py:263
  152.4 8.3 %collective-permute-start.15 = (bf16[512,1024]{1,0:T(8,128)(2,1)}, bf16[512,1024]{1,0:T(8,128)(2,1)}, u32[]{:S(2)}, u32[]{:S(2)}) collective-permute-start(bf16[512,1024]{1,0:T(8,128)(2,1)} %fusion.7.e_own.own), channel_id=1, source_target_pairs={{0,1},{1,0},{2,3},{3,2},{4,5},{5,4},{6,7},{7,6},{8,9},{9,8},{10,11... | collective-permute-start | bytes 3145736 | tf_op jit(solution)/shard_map/ppermute | solution.py:263
  158.9 5.8 %collective-permute-start.16 = (bf16[2,704,512]{2,1,0:T(8,128)(2,1)S(1)}, bf16[2,704,512]{2,1,0:T(8,128)(2,1)}, u32[]{:S(2)}, u32[]{:S(2)}) collective-permute-start(bf16[2,704,512]{2,1,0:T(8,128)(2,1)S(1)} %dynamic-slice_bitcast_fusion), channel_id=1, source_target_pairs={{0,1},{1,0},{2,3},{3,2},{4,5},{5,4},{6,7},{7,6},{8,9},{9,8},{10,11... | collective-permute-start | bytes 4325384 | tf_op jit(solution)/shard_map/ppermute | solution.py:263
  160.3 3.3 collective-permute-start.14
  193.8 11.1 %collective-permute-start.18 = (bf16[512,1024]{1,0:T(8,128)(2,1)}, bf16[512,1024]{1,0:T(8,128)(2,1)}, u32[]{:S(2)}, u32[]{:S(2)}) collective-permute-start(bf16[512,1024]{1,0:T(8,128)(2,1)} %get-tuple-element.91), channel_id=1, source_target_pairs={{0,1},{1,0},{2,3},{3,2},{4,5},{5,4},{6,7},{7,6},{8,9},{9,8},{10,11... | collective-permute-start | bytes 3145736 | tf_op jit(solution)/shard_map/ppermute | solution.py:263
  194.0 13.8 %collective-permute-start.17 = (bf16[512,1024]{1,0:T(8,128)(2,1)}, bf16[512,1024]{1,0:T(8,128)(2,1)}, u32[]{:S(2)}, u32[]{:S(2)}) collective-permute-start(bf16[512,1024]{1,0:T(8,128)(2,1)} %get-tuple-element.89), channel_id=1, source_target_pairs={{0,1},{1,0},{2,3},{3,2},{4,5},{5,4},{6,7},{7,6},{8,9},{9,8},{10,11... | collective-permute-start | bytes 3145736 | tf_op jit(solution)/shard_map/ppermute | solution.py:263
  234.6 46.6 %collective-permute-start.20 = (bf16[2,2,2,32,3328]{4,3,1,0,2:T(8,128)(2,1)}, bf16[2,2,2,32,3328]{4,3,1,0,2:T(8,128)(2,1)S(1)}, u32[]{:S(2)}, u32[]{:S(2)}) collective-permute-start(bf16[2,2,2,32,3328]{4,3,1,0,2:T(8,128)(2,1)} %copy.45), channel_id=1, source_target_pairs={{0,8},{8,0},{16,24},{24,16},{1,9},{9,1},{17,25},{25,17},{2,10},{10... | collective-permute-start | bytes 5111816 | tf_op jit(solution)/shard_map/ppermute | solution.py:263
  236.2 44.9 %collective-permute-start.21 = (bf16[2,2,2,32,3328]{4,3,2,1,0:T(8,128)(2,1)}, bf16[2,2,2,32,3328]{4,3,2,1,0:T(8,128)(2,1)}, u32[]{:S(2)}, u32[]{:S(2)}) collective-permute-start(bf16[2,2,2,32,3328]{4,3,2,1,0:T(8,128)(2,1)} %get-tuple-element.104), channel_id=1, source_target_pairs={{0,16},{8,24},{16,0},{24,8},{1,17},{9,25},{17,1},{25,9},{2,18},{10... | collective-permute-start | bytes 5111816 | tf_op jit(solution)/shard_map/ppermute | solution.py:263
  237.7 142.6 %all-to-all-start.5 = ((bf16[4,352,1024]{2,1,0:T(8,128)(2,1)}), bf16[4,352,1024]{2,1,0:T(8,128)(2,1)}, u32[]{:S(2)}, u32[]{:S(2)}) async-start(bf16[4,352,1024]{2,1,0:T(8,128)(2,1)} %bitcast.122), calls=%async_computation.5 | async-start | bytes 5767168 | tf_op jit(solution)/shard_map/all_to_all | solution.py:593
  285.9 27.2 %collective-permute-start.37 = (bf16[2,2,32,3328]{3,2,1,0:T(8,128)(2,1)}, bf16[2,2,32,3328]{3,2,1,0:T(8,128)(2,1)}, u32[]{:S(2)}, u32[]{:S(2)}) collective-permute-start(bf16[2,2,32,3328]{3,2,1,0:T(8,128)(2,1)} %dynamic-slice_bitcast_fusion.1), channel_id=1, source_target_pairs={{0,8},{8,0},{16,24},{24,16},{1,9},{9,1},{17,25},{25,17},{2,10},{10... | collective-permute-start | bytes 2555912 | tf_op jit(solution)/shard_map/ppermute | solution.py:263
  289.3 25.3 %collective-permute-start.36 = (bf16[2,2,32,3328]{3,2,1,0:T(8,128)(2,1)}, bf16[2,2,32,3328]{3,2,1,0:T(8,128)(2,1)}, u32[]{:S(2)}, u32[]{:S(2)}) collective-permute-start(bf16[2,2,32,3328]{3,2,1,0:T(8,128)(2,1)} %dynamic-slice_bitcast_fusion.2), channel_id=1, source_target_pairs={{0,16},{8,24},{16,0},{24,8},{1,17},{9,25},{17,1},{25,9},{2,18},{10... | collective-permute-start | bytes 2555912 | tf_op jit(solution)/shard_map/ppermute | solution.py:263
  299.0 29.4 %collective-permute-start.30 = (bf16[2,2,2,32,1664]{4,3,2,1,0:T(8,128)(2,1)}, bf16[2,2,2,32,1664]{4,3,2,1,0:T(8,128)(2,1)}, u32[]{:S(2)}, u32[]{:S(2)}) collective-permute-start(bf16[2,2,2,32,1664]{4,3,2,1,0:T(8,128)(2,1)} %get-tuple-element.115), channel_id=1, source_target_pairs={{0,16},{8,24},{16,0},{24,8},{1,17},{9,25},{17,1},{25,9},{2,18},{10... | collective-permute-start | bytes 2555912 | tf_op jit(solution)/shard_map/ppermute | solution.py:263
  302.6 28.7 %collective-permute-start.28 = (bf16[2,2,2,32,1664]{4,3,1,0,2:T(8,128)(2,1)}, bf16[2,2,2,32,1664]{4,3,1,0,2:T(8,128)(2,1)}, u32[]{:S(2)}, u32[]{:S(2)}) collective-permute-start(bf16[2,2,2,32,1664]{4,3,1,0,2:T(8,128)(2,1)} %copy.47), channel_id=1, source_target_pairs={{0,8},{8,0},{16,24},{24,16},{1,9},{9,1},{17,25},{25,17},{2,10},{10... | collective-permute-start | bytes 2555912 | tf_op jit(solution)/shard_map/ppermute | solution.py:263
  313.1 20.7 %collective-permute-start.22 = (bf16[512,1024]{1,0:T(8,128)(2,1)}, bf16[512,1024]{1,0:T(8,128)(2,1)S(1)}, u32[]{:S(2)}, u32[]{:S(2)}) collective-permute-start(bf16[512,1024]{1,0:T(8,128)(2,1)} %get-tuple-element.108), channel_id=1, source_target_pairs={{0,1},{1,0},{2,3},{3,2},{4,5},{5,4},{6,7},{7,6},{8,9},{9,8},{10,11... | collective-permute-start | bytes 3145736 | tf_op jit(solution)/shard_map/ppermute | solution.py:263
  316.7 18.6 %collective-permute-start.38 = (bf16[2,32,3328]{2,1,0:T(8,128)(2,1)S(1)}, bf16[2,32,3328]{2,1,0:T(8,128)(2,1)S(1)}, u32[]{:S(2)}, u32[]{:S(2)}) collective-permute-start(bf16[2,32,3328]{2,1,0:T(8,128)(2,1)S(1)} %get-tuple-element.132), channel_id=1, source_target_pairs={{0,2},{2,0},{4,6},{6,4},{1,3},{3,1},{5,7},{7,5},{8,10},{10,8},{12,... | collective-permute-start | bytes 1277960 | tf_op jit(solution)/shard_map/ppermute | solution.py:263
  316.8 31.4 %collective-permute-start.39 = (bf16[2,32,3328]{2,1,0:T(8,128)(2,1)S(1)}, bf16[2,32,3328]{2,1,0:T(8,128)(2,1)S(1)}, u32[]{:S(2)}, u32[]{:S(2)}) collective-permute-start(bf16[2,32,3328]{2,1,0:T(8,128)(2,1)S(1)} %get-tuple-element.133), channel_id=1, source_target_pairs={{0,4},{2,6},{4,0},{6,2},{1,5},{3,7},{5,1},{7,3},{8,12},{10,14},{12... | collective-permute-start | bytes 1277960 | tf_op jit(solution)/shard_map/ppermute | solution.py:263
  328.4 28.9 %collective-permute-start.40 = (bf16[2,32,3328]{2,1,0:T(8,128)(2,1)S(1)}, bf16[2,32,3328]{2,1,0:T(8,128)(2,1)S(1)}, u32[]{:S(2)}, u32[]{:S(2)}) collective-permute-start(bf16[2,32,3328]{2,1,0:T(8,128)(2,1)S(1)} %get-tuple-element.134), channel_id=1, source_target_pairs={{0,6},{2,4},{4,2},{6,0},{1,7},{3,5},{5,3},{7,1},{8,14},{10,12},{12... | collective-permute-start | bytes 1277960 | tf_op jit(solution)/shard_map/ppermute | solution.py:263
  331.3 26.4 %collective-permute-start.31 = (bf16[2,2,32,1664]{3,2,1,0:T(8,128)(2,1)S(1)}, bf16[2,2,32,1664]{3,2,1,0:T(8,128)(2,1)S(1)}, u32[]{:S(2)}, u32[]{:S(2)}) collective-permute-start(bf16[2,2,32,1664]{3,2,1,0:T(8,128)(2,1)S(1)} %dynamic-slice_bitcast_fusion.3), channel_id=1, source_target_pairs={{0,8},{8,0},{16,24},{24,16},{1,9},{9,1},{17,25},{25,17},{2,10},{10... | collective-permute-start | bytes 1277960 | tf_op jit(solution)/shard_map/ppermute | solution.py:263
  333.8 24.0 %collective-permute-start.29 = (bf16[2,2,32,1664]{3,2,1,0:T(8,128)(2,1)S(1)}, bf16[2,2,32,1664]{3,2,1,0:T(8,128)(2,1)S(1)}, u32[]{:S(2)}, u32[]{:S(2)}) collective-permute-start(bf16[2,2,32,1664]{3,2,1,0:T(8,128)(2,1)S(1)} %dynamic-slice_bitcast_fusion.4), channel_id=1, source_target_pairs={{0,16},{8,24},{16,0},{24,8},{1,17},{9,25},{17,1},{25,9},{2,18},{10... | collective-permute-start | bytes 1277960 | tf_op jit(solution)/shard_map/ppermute | solution.py:263
  358.4 8.2 %collective-permute-start.32 = (bf16[2,32,1664]{2,1,0:T(8,128)(2,1)S(1)}, bf16[2,32,1664]{2,1,0:T(8,128)(2,1)S(1)}, u32[]{:S(2)}, u32[]{:S(2)}) collective-permute-start(bf16[2,32,1664]{2,1,0:T(8,128)(2,1)S(1)} %get-tuple-element.136), channel_id=1, source_target_pairs={{0,2},{2,0},{4,6},{6,4},{1,3},{3,1},{5,7},{7,5},{8,10},{10,8},{12,... | collective-permute-start | bytes 638984 | tf_op jit(solution)/shard_map/ppermute | solution.py:263
  358.4 17.8 %collective-permute-start.33 = (bf16[2,32,1664]{2,1,0:T(8,128)(2,1)S(1)}, bf16[2,32,1664]{2,1,0:T(8,128)(2,1)S(1)}, u32[]{:S(2)}, u32[]{:S(2)}) collective-permute-start(bf16[2,32,1664]{2,1,0:T(8,128)(2,1)S(1)} %get-tuple-element.137), channel_id=1, source_target_pairs={{0,4},{2,6},{4,0},{6,2},{1,5},{3,7},{5,1},{7,3},{8,12},{10,14},{12... | collective-permute-start | bytes 638984 | tf_op jit(solution)/shard_map/ppermute | solution.py:263
  361.4 18.7 %collective-permute-start.34 = (bf16[2,32,1664]{2,1,0:T(8,128)(2,1)S(1)}, bf16[2,32,1664]{2,1,0:T(8,128)(2,1)S(1)}, u32[]{:S(2)}, u32[]{:S(2)}) collective-permute-start(bf16[2,32,1664]{2,1,0:T(8,128)(2,1)S(1)} %get-tuple-element.138), channel_id=1, source_target_pairs={{0,6},{2,4},{4,2},{6,0},{1,7},{3,5},{5,3},{7,1},{8,14},{10,12},{12... | collective-permute-start | bytes 638984 | tf_op jit(solution)/shard_map/ppermute | solution.py:263
  361.9 42.0 %collective-permute-start.41 = (bf16[32,2816]{1,0:T(8,128)(2,1)S(1)}, bf16[32,2816]{1,0:T(8,128)(2,1)S(1)}, u32[]{:S(2)}, u32[]{:S(2)}) collective-permute-start(bf16[32,2816]{1,0:T(8,128)(2,1)S(1)} %dynamic-slice_bitcast_fusion.5), channel_id=1, source_target_pairs={{0,1},{1,0},{2,3},{3,2},{4,5},{5,4},{6,7},{7,6},{8,9},{9,8},{10,11... | collective-permute-start | bytes 540680 | tf_op jit(solution)/shard_map/ppermute | solution.py:263
  380.3 8.1 %collective-permute-start.35 = (bf16[32,1664]{1,0:T(8,128)(2,1)S(1)}, bf16[32,1664]{1,0:T(8,128)(2,1)S(1)}, u32[]{:S(2)}, u32[]{:S(2)}) collective-permute-start(bf16[32,1664]{1,0:T(8,128)(2,1)S(1)} %dynamic-slice_bitcast_fusion.6), channel_id=1, source_target_pairs={{0,1},{1,0},{2,3},{3,2},{4,5},{5,4},{6,7},{7,6},{8,9},{9,8},{10,11... | collective-permute-start | bytes 319496 | tf_op jit(solution)/shard_map/ppermute | solution.py:263
  384.1 14.6 %all-to-all-start.6 = ((bf16[4,352,256]{2,1,0:T(8,128)(2,1)}), bf16[4,352,256]{2,1,0:T(8,128)(2,1)S(1)}, u32[]{:S(2)}, u32[]{:S(2)}) async-start(bf16[4,352,256]{2,1,0:T(8,128)(2,1)} %copy.50), calls=%async_computation.6 | async-start | bytes 1441792 | tf_op jit(solution)/shard_map/all_to_all | solution.py:593
  399.9 15.2 %all-to-all-start.3 = ((bf16[4,2,32,1664]{3,2,1,0:T(8,128)(2,1)}), bf16[4,2,32,1664]{3,2,1,0:T(8,128)(2,1)S(1)}, u32[]{:S(2)}, u32[]{:S(2)}) async-start(bf16[4,2,32,1664]{3,2,1,0:T(8,128)(2,1)} %broadcast_in_dim.68), calls=%async_computation.3 | async-start | bytes 1703936 | tf_op jit(solution)/shard_map/all_to_all | solution.py:593
  416.5 41.1 %all-to-all-start.4 = ((bf16[4,2,32,3328]{3,2,1,0:T(8,128)(2,1)}), bf16[4,2,32,3328]{3,2,1,0:T(8,128)(2,1)}, u32[]{:S(2)}, u32[]{:S(2)}) async-start(bf16[4,2,32,3328]{3,2,1,0:T(8,128)(2,1)} %broadcast_in_dim.69), calls=%async_computation.4 | async-start | bytes 3407872 | tf_op jit(solution)/shard_map/all_to_all | solution.py:593
  423.0 18.4 %collective-permute-start.24 = (f32[14464]{0:T(1024)S(1)}, f32[14464]{0:T(1024)S(1)}, u32[]{:S(2)}, u32[]{:S(2)}) collective-permute-start(f32[14464]{0:T(1024)S(1)} %fusion.42), channel_id=1, source_target_pairs={{0,8},{8,0},{16,24},{24,16},{1,9},{9,1},{17,25},{25,17},{2,10},{10... | collective-permute-start | bytes 173576 | tf_op jit(solution)/shard_map/ppermute | solution.py:263
  441.3 4.3 collective-permute-start.25
  445.6 4.3 collective-permute-start.26
  447.0 10.6 %collective-permute-start.42 = (bf16[352,256]{1,0:T(8,128)(2,1)S(1)}, bf16[352,256]{1,0:T(8,128)(2,1)S(1)}, u32[]{:S(2)}, u32[]{:S(2)}) collective-permute-start(bf16[352,256]{1,0:T(8,128)(2,1)S(1)} %fusion.36), channel_id=1, source_target_pairs={{0,0},{1,4},{2,1},{3,5},{4,2},{5,6},{6,3},{7,7},{8,8},{9,12},{10,9... | collective-permute-start | bytes 540680 | tf_op jit(solution)/shard_map/ppermute | solution.py:974
  449.9 18.0 %collective-permute-start.27 = (f32[14464]{0:T(1024)S(1)}, f32[14464]{0:T(1024)S(1)}, u32[]{:S(2)}, u32[]{:S(2)}) collective-permute-start(f32[14464]{0:T(1024)S(1)} %add.227), channel_id=1, source_target_pairs={{0,4},{2,6},{4,0},{6,2},{1,5},{3,7},{5,1},{7,3},{8,12},{10,14},{12... | collective-permute-start | bytes 173576 | tf_op jit(solution)/shard_map/ppermute | solution.py:263
  458.6 18.8 %all-to-all-start.7 = ((bf16[4,352,256]{2,1,0:T(8,128)(2,1)}), bf16[4,352,256]{2,1,0:T(8,128)(2,1)}, u32[]{:S(2)}, u32[]{:S(2)}) async-start(bf16[4,352,256]{2,1,0:T(8,128)(2,1)} %broadcast_in_dim.70), calls=%async_computation.7 | async-start | bytes 1441792 | tf_op jit(solution)/shard_map/all_to_all | solution.py:593
  (45 other events, 336.7 us)

commit v3 on v2

--- a/solution.py
+++ b/solution.py
@@ -329,7 +329,7 @@
             copy.wait()
         kept.start()
 
-    x = jnp.where(step // (steps // 2) == c, x_own[...], x_far[...]).astype(f32)
+    x = jnp.where(step == c, x_own[...], x_far[...]).astype(f32)
     scale = lax.rsqrt(jnp.mean(x * x, -1, keepdims=True) + 1e-06)
     normed = (x * scale * gain[...]).astype(bf16)
     normed_ref[...] = normed
@@ -343,9 +343,8 @@
 def project(x_own, x_far, gain, pieces, width):
     arrays, tags, places = pieces
     rows, depth = x_own.shape
-    block = rows // 2
-    half = pl.BlockSpec((block, depth), lambda i, *_: (i % 2, 0))
-    each = lambda w: pl.BlockSpec((block, w), lambda i, *_: (i, 0))
+    half = pl.BlockSpec((rows, depth), lambda i, *_: (0, 0))
+    each = lambda w: pl.BlockSpec((rows, w), lambda i, *_: (i, 0))
     anywhere = pl.BlockSpec(memory_space=pl.ANY)
     return pl.pallas_call(
         functools.partial(project_kernel, tags, places, len(arrays)),
@@ -356,7 +355,7 @@
         ),
         grid_spec=pltpu.PrefetchScalarGridSpec(
             num_scalar_prefetch=1,
-            grid=(4,),
+            grid=(2,),
             in_specs=[half, half, pl.BlockSpec((1, depth), lambda i, *_: (0, 0))]
             + [anywhere] * len(arrays),
             out_specs=(each(depth), each(width), anywhere),
@@ -371,7 +370,7 @@
 
 
 def near_first(i, where):
-    return ((where[2] * 2 + i) % 4, 0)
+    return ((where[2] + i) % 2, 0)
 
 
 def attend_kernel(tags, places, count, where_ref, merged, *refs):
@@ -389,11 +388,11 @@
 
     total = dot(merged[...], weight[...])
 
-    @pl.when(step < 2)
+    @pl.when(step == 0)
     def _():
         near[...] = total
 
-    @pl.when(step >= 2)
+    @pl.when(step == 1)
     def _():
         far[...] = total.astype(bf16)
 
@@ -403,17 +402,17 @@
 
 
 def near_spec(block, width):
-    return pl.BlockSpec((block, width), lambda i, *_: (jnp.minimum(i, 1), 0))
+    return pl.BlockSpec((block, width), lambda i, *_: (0, 0))
 
 
 def far_spec(block, width):
-    return pl.BlockSpec((block, width), lambda i, *_: (jnp.maximum(i - 2, 0), 0))
+    return pl.BlockSpec((block, width), lambda i, *_: (0, 0))
 
 
 def attend(merged, pieces, width):
     arrays, tags, places = pieces
     rows, depth = merged.shape
-    block = rows // 4
+    block = rows // 2
     anywhere = pl.BlockSpec(memory_space=pl.ANY)
     return pl.pallas_call(
         functools.partial(attend_kernel, tags, places, len(arrays)),
@@ -424,7 +423,7 @@
         ),
         grid_spec=pltpu.PrefetchScalarGridSpec(
             num_scalar_prefetch=1,
-            grid=(4,),
+            grid=(2,),
             in_specs=[pl.BlockSpec((block, depth), near_first)] + [anywhere] * len(arrays),
             out_specs=(near_spec(block, width), far_spec(block, width), anywhere),
             scratch_shapes=[
@@ -438,20 +437,20 @@
 
 
 def merged_grad_kernel(where_ref, own, far, weight, out):
-    grad = jnp.where(pl.program_id(0) < 2, own[...], far[...])
+    grad = jnp.where(pl.program_id(0) == 0, own[...], far[...])
     out[...] = dot_nt(grad, weight[...])
 
 
 def merged_grad(own, far, weight):
     rows, width = own.shape
     depth = weight.shape[0]
-    block = rows // 2
+    block = rows
     return pl.pallas_call(
         merged_grad_kernel,
         out_shape=jax.ShapeDtypeStruct((2 * rows, depth), f32),
         grid_spec=pltpu.PrefetchScalarGridSpec(
             num_scalar_prefetch=1,
-            grid=(4,),
+            grid=(2,),
             in_specs=[
                 near_spec(block, width),
                 far_spec(block, width),
@@ -466,11 +465,11 @@
 def normed_grad_kernel(where_ref, grad, weight, near, far):
     total = dot_nt(grad[...], weight[...])
 
-    @pl.when(pl.program_id(0) < 2)
+    @pl.when(pl.program_id(0) == 0)
     def _():
         near[...] = total
 
-    @pl.when(pl.program_id(0) >= 2)
+    @pl.when(pl.program_id(0) == 1)
     def _():
         far[...] = total.astype(bf16)
 
@@ -478,7 +477,7 @@
 def normed_grad(grad, weight):
     rows, width = grad.shape
     depth = weight.shape[0]
-    block = rows // 4
+    block = rows // 2
     return pl.pallas_call(
         normed_grad_kernel,
         out_shape=(
@@ -487,7 +486,7 @@
         ),
         grid_spec=pltpu.PrefetchScalarGridSpec(
             num_scalar_prefetch=1,
-            grid=(4,),
+            grid=(2,),
             in_specs=[
                 pl.BlockSpec((block, width), near_first),
                 pl.BlockSpec((depth, width), lambda i, *_: (0, 0)),
@@ -498,89 +497,113 @@
     )(positions(), grad, weight)
 
 
-def weight_grad_kernel(parts, with_out, where_ref, *refs):
+def keep_and_send(total, where_ref, refs, col):
+    low_keep, low_send, high_keep, high_send = refs
+    first_low, first_high = where_ref[1] % 2 == 0, where_ref[1] // 2 == 0
+    short = total.shape[0] // 32
+    block = lambda i: total[i * short : (i + 1) * short]
+    for z in range(2):
+        for i in range(4):
+            a, b = block(8 * z + 2 * i), block(8 * z + 2 * i + 1)
+            low_keep[z, i // 2, i % 2, col, :] = jnp.where(first_low, a, b)
+            low_send[z, i // 2, i % 2, col, :] = jnp.where(first_low, b, a)
+            k = 16 + 8 * z + (i // 2) * 4 + i % 2
+            a, b = block(k), block(k + 2)
+            high_keep[z, i // 2, i % 2, col, :] = jnp.where(first_high, a, b)
+            high_send[z, i // 2, i % 2, col, :] = jnp.where(first_high, b, a)
+
+
+def weight_grad_kernel(parts, steps, where_ref, *refs):
     lefts, grad = refs[:parts], refs[parts]
-    z = pl.program_id(0)
-    d, c = where_ref[1], where_ref[2]
-    first_low, first_high = d % 2 == 0, d // 2 == 0
-    total, at = 0.0, 0
-    for left in lefts:
-        rows = left.shape[0]
-        total = total + dot_tn(left[...], grad[at : at + rows, :])
-        at += rows
-    total = total.astype(bf16)
-    short = total.shape[0] // 8
-    blocks = [total[i * short : (i + 1) * short] for i in range(8)]
-    if with_out:
-        merged, own, far = refs[parts + 1 : parts + 4]
+    turned = refs[-1]
+    step = pl.program_id(0)
+    c = where_ref[2]
+
+    @pl.when(step == 0)
+    def _():
+        at = 0
+        for left in lefts:
+            rows = left.shape[0]
+            turned[:, at : at + rows] = left[...].T
+            at += rows
+
+    if len(refs) == parts + 6:
+        every = slice(None)
+        keep_and_send(dot(turned[...], grad[...]).astype(bf16), where_ref, refs[-5:-1], every)
+        return
+
+    merged, own, far = refs[parts + 1 : parts + 4]
+    outs = refs[-5:-1]
+
+    @pl.when(step < steps)
+    def _():
+        keep_and_send(dot(turned[...], grad[...]).astype(bf16), where_ref, outs, slice(None))
+
+    @pl.when(step >= steps)
+    def _():
         rows, half = own.shape[0], own.shape[1] // 2
         mine = merged[pl.ds(pl.multiple_of(c * rows, rows), rows), :]
         theirs = merged[pl.ds(pl.multiple_of((1 - c) * rows, rows), rows), :]
-        out = (dot_tn(mine, own[...]) + dot_tn(theirs, far[...])).astype(bf16)
-        lines = short // 2
-        for i in range(8):
-            part = out[i * lines : (i + 1) * lines]
-            part = jnp.concatenate([part[:, :half], part[:, half:]], 0)
-            blocks[i] = jnp.concatenate([blocks[i], part], 1)
-    low_keep, low_send, high_keep, high_send = refs[-4:]
-
-    @pl.when(z < 2)
-    def _():
-        for i in range(4):
-            a, b = blocks[2 * i], blocks[2 * i + 1]
-            low_keep[0, i // 2, i % 2] = jnp.where(first_low, a, b)
-            low_send[0, i // 2, i % 2] = jnp.where(first_low, b, a)
-
-    @pl.when(z >= 2)
-    def _():
-        for i in range(4):
-            k = (i // 2) * 4 + i % 2
-            a, b = blocks[k], blocks[k + 2]
-            high_keep[0, i // 2, i % 2] = jnp.where(first_high, a, b)
-            high_send[0, i // 2, i % 2] = jnp.where(first_high, b, a)
+        width = outs[0].shape[-1]
+        for k in range(2):
+            at = pl.ds(pl.multiple_of(k * half + (step - steps) * width, width), width)
+            part = (dot_tn(mine, own[:, at]) + dot_tn(theirs, far[:, at])).astype(bf16)
+            lines = part.shape[0] // 32
+            keep_and_send(part, where_ref, outs, slice(k * lines, (k + 1) * lines))
 
 
 def weight_grad(lefts, grad, out=()):
-    depth = lefts[0].shape[1] // 4
-    width = grad.shape[1] + (out[1].shape[1] // 2 if out else 0)
-    short = depth // 8
-    shape = jax.ShapeDtypeStruct((2, 2, 2, short, width), bf16)
-    low = pl.BlockSpec((1, 2, 2, short, width), lambda i, *_: (jnp.minimum(i, 1), 0, 0, 0, 0))
-    high = pl.BlockSpec((1, 2, 2, short, width), lambda i, *_: (jnp.maximum(i - 2, 0), 0, 0, 0, 0))
+    depth = lefts[0].shape[1]
+    rows = sum(a.shape[0] for a in lefts)
+    block = 256
+    steps = pl.cdiv(grad.shape[1], block)
+    more = out[1].shape[1] // 2 if out else 0
+    shape = jax.ShapeDtypeStruct((2, 2, 2, depth // 32, grad.shape[1] + more), bf16)
+    each = pl.BlockSpec((2, 2, 2, depth // 32, block), lambda i, *_: (0, 0, 0, 0, i))
     whole = lambda a: pl.BlockSpec(a.shape, lambda i, *_: (0, 0))
-    column = lambda a: pl.BlockSpec((a.shape[0], a.shape[1] // 4), lambda i, *_: (0, i))
-    specs = [column(a) for a in lefts] + [whole(grad)]
-    if out:
-        specs += [column(out[0]), whole(out[1]), whole(out[2])]
+    specs = [whole(a) for a in lefts]
+    specs += [pl.BlockSpec((rows, block), lambda i, *_: (0, jnp.minimum(i, steps - 1)))]
+    specs += [whole(a) for a in out]
     return pl.pallas_call(
-        functools.partial(weight_grad_kernel, len(lefts), bool(out)),
+        functools.partial(weight_grad_kernel, len(lefts), steps),
         out_shape=(shape,) * 4,
         grid_spec=pltpu.PrefetchScalarGridSpec(
-            num_scalar_prefetch=1, grid=(4,), in_specs=specs, out_specs=(low, low, high, high)
+            num_scalar_prefetch=1,
+            grid=(steps + more // block,),
+            in_specs=specs,
+            out_specs=(each,) * 4,
+            scratch_shapes=[pltpu.VMEM((depth, rows), bf16)],
         ),
         name="weight_gradient",
     )(positions(), *lefts, grad, *out)
 
 
-def down_grad_kernel(hidden, own, far, out):
+def down_grad_kernel(hidden, own, far, out, turned):
     rows = own.shape[0]
-    total = dot_tn(hidden[:rows, :], own[...]) + dot_tn(hidden[rows:, :], far[...])
+
+    @pl.when(pl.program_id(0) == 0)
+    def _():
+        turned[...] = hidden[...].T
+
+    total = dot(turned[:, :rows], own[...]) + dot(turned[:, rows:], far[...])
     out[...] = total.astype(bf16)
 
 
 def down_gradient(hidden, own, far):
     rows, width = own.shape
     half = hidden.shape[1]
+    block = 256
     return pl.pallas_call(
         down_grad_kernel,
         out_shape=jax.ShapeDtypeStruct((half, width), bf16),
-        grid=(half // HD,),
+        grid=(width // block,),
         in_specs=[
-            pl.BlockSpec((2 * rows, HD), lambda i: (0, i)),
-            pl.BlockSpec((rows, width), lambda i: (0, 0)),
-            pl.BlockSpec((rows, width), lambda i: (0, 0)),
+            pl.BlockSpec((2 * rows, half), lambda i: (0, 0)),
+            pl.BlockSpec((rows, block), lambda i: (0, i)),
+            pl.BlockSpec((rows, block), lambda i: (0, i)),
         ],
-        out_specs=pl.BlockSpec((HD, width), lambda i: (i, 0)),
+        out_specs=pl.BlockSpec((half, block), lambda i: (0, i)),
+        scratch_shapes=[pltpu.VMEM((half, 2 * rows), bf16)],
         name="down_gradient",
     )(hidden, own, far)
 
@@ -659,7 +682,7 @@
     rows, width = x_own.shape
     others = x_other.shape[0]
     half = 2 * down[1].shape[1]
-    block = min(256, rows)
+    block = rows
     own, steps = rows // block, (rows + others) // block
     near = lambda w: pl.BlockSpec((block, w), lambda i, *_: (jnp.minimum(i, own - 1), 0))
     far = lambda w: pl.BlockSpec((block, w), lambda i, *_: (jnp.maximum(i - own, 0), 0))
@@ -691,7 +714,7 @@
     )(positions(), x_own, x_other, e_own, e_other, *arrays, *down)
 
 
-def pack_kernel(heads, where_ref, qkv, beta, out, gateup, all_ref, mixed_ref, wide_ref):
+def pack_kernel(heads, where_ref, qkv, beta, out, gateup, mixed_ref, wide_ref, every):
     rows = qkv.shape[0]
     strips = qkv.shape[1] // (2 * HD)
     mixed = (strips + 1) * HD
@@ -704,22 +727,21 @@
         def _():
             for i in range(strips):
                 at = (2 * i + c) * HD
-                all_ref[:, i * HD : (i + 1) * HD] = qkv[:, at : at + HD]
+                mixed_ref[:, i * HD : (i + 1) * HD] = qkv[:, at : at + HD]
             source = lax.broadcasted_iota(jnp.int32, (heads, HD), 0)
             lane = lax.broadcasted_iota(jnp.int32, (heads, HD), 1)
             chosen = (source == 2 * lane + c).astype(f32).astype(bf16)
-            all_ref[:, strips * HD : mixed] = dot(beta[...], chosen).astype(bf16)
+            every[...] = dot_tn(beta[...], chosen)
+            here = pl.ds(pl.multiple_of(where_ref[0] * rows, rows), rows)
+            mixed_ref[:, strips * HD : mixed] = every[here, :].astype(bf16)
             for i in range(2):
                 at = (2 * i + c) * width
-                to = mixed + i * width
-                all_ref[:, to : to + width] = gateup[:, at : at + width]
-
-    last = mixed + 2 * width
-    all_ref[:short, last:] = out[:, :half]
-    all_ref[short:, last:] = out[:, half:]
-    for i in range(4):
-        mixed_ref[i] = all_ref[:, :mixed]
-    wide_ref[...] = all_ref[:, mixed:]
+                wide_ref[0, :, i * width : (i + 1) * width] = gateup[:, at : at + width]
+
+    wide_ref[0, :short, 2 * width :] = out[:, :half]
+    wide_ref[0, short:, 2 * width :] = out[:, half:]
+    for i in range(1, 4):
+        wide_ref[i] = wide_ref[0]
 
 
 def pack(w_qkv, w_beta, w_out, w_gateup):
@@ -730,7 +752,7 @@
     wide = w_gateup.shape[1] // 2 + w_out.shape[1] // 2
     fixed = lambda *shape: pl.BlockSpec(shape, lambda i, *_: (0,) * len(shape))
     mine = lambda width: pl.BlockSpec((rows, width), lambda i, at: (at[0], 0))
-    shapes = ((rows, mixed + wide), (4, rows, mixed), (rows, wide))
+    shapes = ((rows, mixed), (4, rows, wide))
     return pl.pallas_call(
         functools.partial(pack_kernel, heads),
         out_shape=tuple(jax.ShapeDtypeStruct(s, bf16) for s in shapes),
@@ -739,44 +761,52 @@
             grid=(1,),
             in_specs=[
                 mine(w_qkv.shape[1]),
-                mine(heads),
+                pl.BlockSpec(w_beta.shape[::-1], lambda i, *_: (0, 0)),
                 pl.BlockSpec((short, w_out.shape[1]), lambda i, at: (at[1] * 4 + at[0], 0)),
                 mine(w_gateup.shape[1]),
             ],
             out_specs=tuple(fixed(*s) for s in shapes),
+            scratch_shapes=[pltpu.VMEM((w_beta.shape[0], HD), f32)],
         ),
         name="weight_pieces",
-    )(here, w_qkv, w_beta, w_out, w_gateup)
-
-
-def gather_direct(pieces, mixed_piece, wide_piece, down_shard):
+    )(here, w_qkv, w_beta.T, w_out, w_gateup)
+
+
+def gather_direct(mixed_piece, wide_piece, down_shard):
     z, c = lax.axis_index("fsdp"), lax.axis_index("ctx")
-    own = [pieces] + [xor(pieces, "dp", k) for k in (1, 2, 3)]
-    rows = exchange(mixed_piece, "fsdp")
-    wide_piece, rows = after(wide_piece, rows)
-    wide_rows = [xor(wide_piece, "fsdp", k) for k in (1, 2, 3)]
-    rows, *own[1:] = after(rows, *own[1:])
-    rest = to_all(jnp.stack([pick(rows, z ^ k) for k in (1, 2, 3)]), "dp")
+    own = [mixed_piece] + [xor(mixed_piece, "dp", k) for k in (1, 2, 3)]
+    rows = [xor(mixed_piece, "fsdp", k) for k in (1, 2, 3)]
+    wide_own, *own[1:] = after(wide_piece[0], *own[1:])
+    wide_own = [wide_own] + [xor(wide_own, "dp", k) for k in (1, 2, 3)]
+    wide_piece, *rows = after(wide_piece, *rows)
+    wide_rows = exchange(wide_piece, "fsdp")
+    rows, *wide_own[1:] = after(jnp.stack(rows), *wide_own[1:])
+    rest = [rows] + [xor(rows, "dp", k) for k in (1, 2, 3)]
     half = down_shard.shape[1] // 2
     mine = lax.dynamic_slice_in_dim(down_shard, c * half, half, 1)
-    rest, mine, *wide_rows = after(rest, mine, *wide_rows)
-    down = to_all(mine, "fsdp")
-    half = pieces.shape[1] // 3
-    low = jnp.stack([w[:, :half] for w in wide_rows])
-    high = jnp.stack([w[:, half:] for w in wide_rows])
+    tags = [(k, (), 0, False, k) for k in range(4)]
+    tags += [(4 + i, (k - 1,), k, False, i) for i in range(4) for k in (1, 2, 3)]
+    return own + rest, tags, wide_own, wide_rows, mine
+
+
+def spread_first(own, wide_rows, mine):
+    z = lax.axis_index("fsdp")
+    half = wide_rows.shape[2] // 2
+    low = jnp.stack([pick(wide_rows, z ^ k)[:, :half] for k in (1, 2, 3)])
+    high = jnp.stack([pick(wide_rows, z ^ k)[:, half:] for k in (1, 2, 3)])
     low, high = [low, xor(low, "dp", 1)], [high, xor(high, "dp", 2)]
-    own_tags = [(k, (), 0, False, k) for k in range(4)]
-    mixed_tags = own_tags + [(4, (i, k - 1), k, True, i) for i in range(4) for k in (1, 2, 3)]
-    return own, rest, low, high, mixed_tags, down
-
-
-def spread_further(own, low, high):
+    mine, wide_rows = after(mine, wide_rows)
+    return own, low, high, to_all(mine, "fsdp")
+
+
+def spread_second(full, own, low, high):
+    full, low[1], high[1] = after(full, low[1], high[1])
     low = low + [xor(low[0], "dp", 2), xor(low[1], "dp", 2)]
     high = [high[0], xor(high[0], "dp", 1), high[1], xor(high[1], "dp", 1)]
     tags = [(k, (), 0, False, k) for k in range(4)]
     tags += [(4 + i, (k - 1,), k, False, i) for i in range(4) for k in (1, 2, 3)]
     tags += [(8 + i, (k - 1,), k, False, i) for i in range(4) for k in (1, 2, 3)]
-    return own + low + high, tags
+    return full, own + low + high, tags
 
 
 def gather_weights(w_qkv, w_beta, w_out, w_gateup, w_down, heads):
@@ -792,12 +822,10 @@
             pick(down.reshape(n, -1, down.shape[1]), c),
         )
     rows, short = w_qkv.shape[0] // 4, HD // 4
-    pieces, mixed_piece, wide_piece = pack(w_qkv, w_beta, w_out, w_gateup)
-    mixed, width, half = mixed_piece.shape[2], w_gateup.shape[1] // 2, w_out.shape[1] // 2
-    own, rest, low, high, mixed_tags, down = gather_direct(
-        pieces, mixed_piece, wide_piece, w_down
-    )
-    cut = low[0].shape[2]
+    mixed_piece, wide_piece = pack(w_qkv, w_beta, w_out, w_gateup)
+    mixed, width, half = mixed_piece.shape[1], w_gateup.shape[1] // 2, w_out.shape[1] // 2
+    mixed_all, mixed_tags, own, wide_rows, mine = gather_direct(mixed_piece, wide_piece, w_down)
+    cut = (width + half) // 2
 
     def mixed_places(tag, z, d):
         row = pl.multiple_of(z * (4 * rows) + d * rows, rows)
@@ -805,10 +833,8 @@
 
     def out_places(tag, z, d):
         row = pl.multiple_of(z * HD + d * short, short)
-        if tag[0] < 4:
-            at = slice(mixed + width, mixed + width + half)
-        else:
-            at = slice(width - cut, width - cut + half)
+        first = width if tag[0] < 4 else width - cut
+        at = slice(first, first + half)
         return [
             ((slice(0, short), at), 0, row, 0),
             ((slice(short, 2 * short), at), 0, row, half),
@@ -817,20 +843,22 @@
     def feed_places(tag, z, d):
         row = pl.multiple_of(z * (4 * rows) + d * rows, rows)
         if tag[0] < 4:
-            at, col = slice(mixed, mixed + width), 0
+            at, col = slice(0, width), 0
         elif tag[0] < 8:
             at, col = slice(0, cut), 0
         else:
             at, col = slice(0, width - cut), cut
         return [((slice(0, rows), at), 0, row, col)]
 
+    spread = spread_first(own, wide_rows, mine)
+
     def further(full):
-        full, low[1], high[1] = after(full, low[1], high[1])
-        wide_all, wide_tags = spread_further(own, low, high)
+        full, wide_all, wide_tags = spread_second(full, *spread[:3])
         out_tags = [t for t in wide_tags if not 4 <= t[0] < 8]
-        return full, (wide_all, wide_tags, feed_places), (wide_all, out_tags, out_places)
-
-    return (own + [rest], mixed_tags, mixed_places), further, down
+        wide = wide_all, wide_tags, feed_places
+        return full, wide, (wide_all, out_tags, out_places), spread[3]
+
+    return (mixed_all, mixed_tags, mixed_places), further
 
 
 def feed_both(normed, grad_feed, gateup, down):
@@ -894,14 +922,12 @@
     d = lax.axis_index("dp")
     high, low = d // 2, d % 2
     a, b = added(kept[0], got[0]), added(kept[1], got[1])
-    got = xor(pick(a, 1 - high, 2), "dp", 2), xor(pick(b, 1 - low, 2), "dp", 1)
-    return (pick(a, high, 2), pick(b, low, 2)), got
-
-
-def rows_sent(kept, got):
-    z = lax.axis_index("fsdp")
-    part = jnp.concatenate([added(kept[0], got[0]), added(kept[1], got[1])], 0)
-    return pick(part, z), [xor(pick(part, z ^ k), "fsdp", k) for k in (1, 2, 3)]
+    sent = pick(a, 1 - high, 2), pick(b, 1 - low, 2)
+    return (pick(a, high, 2), pick(b, low, 2)), sent
+
+
+def over_replicas(kept, got):
+    return jnp.concatenate([added(kept[0], got[0]), added(kept[1], got[1])], 0)
 
 
 def summed_rows(own, got):
@@ -919,17 +945,31 @@
     return jnp.stack([jnp.where(first, mine, other), jnp.where(first, other, mine)])
 
 
-def finish_kernel(moves, source, *outs):
-    for at, index, to in moves:
-        outs[index][to] = source[at].astype(f32)
-
-
-def finish(source, moves, shapes, name):
+def finish_kernel(moves, count, where_ref, *refs):
+    sources, outs = refs[:count], refs[count:]
+    d = where_ref[1]
+    for source, at, index, to in moves:
+        if len(to) == 3:
+            if isinstance(to[0], int):
+                to = (pl.ds(pl.multiple_of((d ^ to[0]) * to[1], to[1]), to[1]), to[2])
+            else:
+                to = (to[0], pl.ds(pl.multiple_of((d ^ to[1]) * to[2], HD), to[2]))
+        outs[index][to] = sources[source][at].astype(f32)
+
+
+def finish(sources, moves, shapes, name):
+    whole = lambda shape: pl.BlockSpec(shape, lambda i, *_: (0,) * len(shape))
     return pl.pallas_call(
-        functools.partial(finish_kernel, moves),
+        functools.partial(finish_kernel, moves, len(sources)),
         out_shape=tuple(jax.ShapeDtypeStruct(s, f32) for s in shapes),
+        grid_spec=pltpu.PrefetchScalarGridSpec(
+            num_scalar_prefetch=1,
+            grid=(1,),
+            in_specs=[whole(s.shape) for s in sources],
+            out_specs=tuple(whole(s) for s in shapes),
+        ),
         name=name,
-    )(source)
+    )(positions(), *sources)
 
 
 def blocks_of(grad, n, z):
@@ -966,22 +1006,19 @@
     return total.astype(bf16)
 
 
-def down_summed(got):
-    part = added_up(got)
-    rows, cols = part.shape[0], part.shape[1] // 4
-    part = added_up(exchange(jnp.transpose(part.reshape(rows, 4, cols), (1, 0, 2)), "dp"))
+def quarter(part, k):
+    cols = part.shape[1] // 4
+    return lax.dynamic_slice_in_dim(part, (lax.axis_index("dp") ^ k) * cols, cols, 1)
+
+
+def down_to_owners(part):
     pairs = [(z * 2 + c, (2 * c + z // 2) * 2 + z % 2) for z in range(4) for c in range(2)]
-    every = to_all(lax.ppermute(part, ("fsdp", "ctx"), pairs), "dp")
-    moves = [((i,), 0, (slice(None), slice(i * cols, (i + 1) * cols))) for i in range(4)]
-    return finish(every, moves, [(rows, 4 * cols)], "down_total")[0]
-
-
-def sum_small(vector):
-    if not direct():
-        return lax.psum(vector, ("dp", "fsdp", "ctx"))
-    for axis, step in (("ctx", 1), ("dp", 1), ("dp", 2), ("fsdp", 1), ("fsdp", 2)):
-        vector = vector + xor(vector, axis, step)
-    return vector
+    return lax.ppermute(part, ("fsdp", "ctx"), pairs)
+
+
+def sum_over(vector, axis):
+    got = [xor(vector, axis, k) for k in (1, 2, 3)]
+    return (vector + got[0]) + (got[1] + got[2])
 
 
 def local(
@@ -1010,12 +1047,12 @@
     valid = ((start + positions_here[:piece_len]) < lengths[0]).astype(f32)[:, None]
     grad_feed = (cotangent[0].astype(f32) * valid).astype(bf16)
     if direct():
-        pieces, further, down = gather_weights(w_qkv, w_beta, w_out, w_gateup, w_down, heads_all)
+        pieces, further = gather_weights(w_qkv, w_beta, w_out, w_gateup, w_down, heads_all)
         far_rows = xor(inputs[0], "ctx", 1)
         normed_one, projected, mixed = project(
             inputs[0], far_rows, norm_gain1[None], pieces, (3 * heads + 1) * HD
         )
-        projected, gateup, out = further(projected)
+        projected, gateup, out, down = further(projected)
     else:
         mixed, gateup, out, down = gather_weights(
             w_qkv, w_beta, w_out, w_gateup, w_down, heads_all
@@ -1087,47 +1124,23 @@
     )
     if direct():
         grad_mixed, *wide_got = after(grad_mixed, *wide_got)
-        wide_kept, wide_got = replicas_second(wide_kept, wide_got)
+        wide_kept, wide_sent = replicas_second(wide_kept, wide_got)
+        grad_mixed, *wide_sent = after(grad_mixed, *wide_sent)
+        wide_got = xor(wide_sent[0], "dp", 2), xor(wide_sent[1], "dp", 1)
         low_kept, low_sent, high_kept, high_sent = weight_grad((normed_one,), grad_mixed)
         mixed_kept = low_kept, high_kept
         mixed_got = xor(low_sent, "dp", 1), xor(high_sent, "dp", 2)
-        wide_own, wide_got = rows_sent(wide_kept, wide_got)
+        low_sent, *wide_got = after(low_sent, *wide_got)
+        wide = over_replicas(wide_kept, wide_got)
+        grad_mixed, down_got, wide = after(grad_mixed, down_got, wide)
+        wide = exchange(wide, "fsdp")
         near, far = normed_grad(grad_mixed, mixed)
+        down_part = added_up(down_got)
+        near, *mixed_got = after(near, *mixed_got)
         grad_normed_one = near + xor(far, "ctx", 1).astype(f32)
-        mixed_kept, mixed_got = replicas_second(mixed_kept, mixed_got)
-        down_total = down_summed(down_got)
-        mixed = summed_rows(*rows_sent(mixed_kept, mixed_got))
-        wide = summed_rows(wide_own, wide_got)
-        feed_part = both_columns(wide[..., : 2 * ff_width])
-        wide = to_all(jnp.concatenate([feed_part, wide[..., 2 * ff_width :]], 2), "dp")
-        short, rows, half = wide.shape[2], HD // (4 * n), model_width // 2
-        moves = []
-        for i in range(4):
-            for j in range(n):
-                lines = slice(i * short, (i + 1) * short)
-                for k in range(2):
-                    at = slice(k * ff_width, (k + 1) * ff_width)
-                    to = (k * n + j) * ff_width
-                    moves.append(((i, j, slice(None), at), 0, (lines, slice(to, to + ff_width))))
-                for k in range(2):
-                    at = slice(k * rows, (k + 1) * rows), slice(2 * ff_width, None)
-                    low = j * 4 * rows + i * rows
-                    to = slice(low, low + rows), slice(k * half, (k + 1) * half)
-                    moves.append(((i, j) + at, 1, to))
-        shapes = [(4 * short, 2 * n * ff_width), (4 * n * rows, model_width)]
-        gateup_total, out_total = finish(wide, moves, shapes, "wide_totals")
-        both = to_all(both_columns(mixed), "dp")
-        moves = []
-        for i in range(4):
-            for j in range(n):
-                for k in range(3 * heads):
-                    at = (i, j, slice(None), slice(k * HD, (k + 1) * HD))
-                    to = (k * n + j) * HD
-                    lines = slice(i * short, (i + 1) * short)
-                    moves.append((at, 0, (lines, slice(to, to + HD))))
-        (qkv_total,) = finish(both, moves, [(4 * short, 3 * heads_all * HD)], "mixed_totals")
-        beta_total = both[..., 3 * heads * HD : 3 * heads * HD + heads].astype(f32)
-        beta_total = jnp.transpose(beta_total, (0, 2, 3, 1)).reshape(4 * short, heads_all)
+        mixed_kept, mixed_sent = replicas_second(mixed_kept, mixed_got)
+        mixed_got = xor(mixed_sent[0], "dp", 2), xor(mixed_sent[1], "dp", 1)
+        down_got = [xor(quarter(down_part, k), "dp", k) for k in (1, 2, 3)]
     else:
         mixed_grad = lax.dot_general(
             normed_one, grad_mixed, contract_rows, preferred_element_type=f32
@@ -1152,14 +1165,83 @@
         * scale_one
         * tokens_in
         * jnp.mean(scaled_one * tokens_in, -1, keepdims=True)
-    )
+    ).astype(bf16)
     conv_term = placed_at_ctx(conv_term.reshape(KERNEL, 3, heads, HD), 3)
     small = jnp.concatenate([gain_one_term, gain_two_term, gain_rows[0], conv_term.reshape(-1)], 0)
     cuts = [model_width, 2 * model_width, 2 * model_width + HD]
-    gain_one, gain_two, gain_head, conv_total = jnp.split(sum_small(small), cuts)
+    if direct():
+        small = small + xor(small, "ctx", 1)
+        small, wide, *got = after(small, wide, *mixed_got, *down_got)
+        mixed_got, down_got = got[:2], got[2:]
+        mixed_part = over_replicas(mixed_kept, mixed_got)
+        z = lax.axis_index("fsdp")
+        mixed_sent = [pick(mixed_part, z ^ k) for k in (1, 2, 3)]
+        small, wide, *mixed_sent = after(small, wide, *mixed_sent)
+        mixed_got = [xor(s, "fsdp", k + 1) for k, s in enumerate(mixed_sent)]
+        down_mine = down_to_owners(summed_rows(quarter(down_part, 0), down_got))
+        wide = added_up(wide)
+        feed_part = both_columns(wide[..., : 2 * ff_width])
+        lines, cols = wide.shape[1], down_mine.shape[1]
+        count = down_mine.shape[0] // lines
+        each = pl.cdiv(count, n)
+        down_part = jnp.pad(down_mine, ((0, (n * each - count) * lines), (0, 0)))
+        down_part = jnp.transpose(down_part.reshape(n, each, lines, cols), (0, 2, 1, 3))
+        down_part = down_part.reshape(n, lines, each * cols)
+        wide = jnp.concatenate([feed_part, wide[..., 2 * ff_width :], down_part], 2)
+        small, wide = after(small, wide)
+        small = sum_over(small, "dp")
+        wide = to_all(wide, "dp")
+        mixed_mine = pick(mixed_part, z)
+        ready = after(mixed_mine, small, grad_tokens, *mixed_got)
+        mixed_mine, small, grad_tokens = ready[:3]
+        mixed_got = ready[3:]
+        both = both_columns(summed_rows(mixed_mine, mixed_got))
+        both = [both] + [xor(both, "dp", k) for k in (1, 2, 3)]
+        small_total = sum_over(small, "fsdp")
+        short, rows, half = wide.shape[2], HD // (4 * n), model_width // 2
+        moves = []
+        for i in range(4):
+            for j in range(n):
+                lines = slice(i * short, (i + 1) * short)
+                for k in range(2):
+                    at = slice(k * ff_width, (k + 1) * ff_width)
+                    to = (k * n + j) * ff_width
+                    moves.append((0, (i, j, slice(None), at), 0, (lines, slice(to, to + ff_width))))
+                for k in range(2):
+                    at = slice(2 * ff_width, 2 * ff_width + half)
+                    at = slice(k * rows, (k + 1) * rows), at
+                    low = j * 4 * rows + i * rows
+                    to = slice(low, low + rows), slice(k * half, (k + 1) * half)
+                    moves.append((0, (i, j) + at, 1, to))
+            first = 2 * ff_width + half
+            for m in range(count):
+                at = slice(first + (m % each) * cols, first + (m % each + 1) * cols)
+                to = slice(m * short, (m + 1) * short), slice(i * cols, (i + 1) * cols)
+                moves.append((0, (i, m // each, slice(None), at), 2, to))
+        shapes = [(4 * short, 2 * n * ff_width), (4 * n * rows, model_width)]
+        shapes += [(down_mine.shape[0], 4 * cols)]
+        gateup_total, out_total, down_total = finish([wide], moves, shapes, "wide_totals")
+        ready = after(both[0], *both[1:], gateup_total, out_total, down_total)
+        both, (gateup_total, out_total, down_total) = list(ready[:4]), ready[4:]
+        moves = []
+        for i in range(4):
+            for j in range(n):
+                for k in range(3 * heads):
+                    at = (j, slice(None), slice(k * HD, (k + 1) * HD))
+                    to = (k * n + j) * HD
+                    moves.append((i, at, 0, (i, short, slice(to, to + HD))))
+                at = (j, slice(None), slice(3 * heads * HD, None))
+                moves.append((i, at, 1, (i, short, slice(j * HD, (j + 1) * HD))))
+        shapes = [(4 * short, 3 * heads_all * HD), (4 * short, n * HD)]
+        qkv_total, beta_total = finish(both, moves, shapes, "mixed_totals")
+        beta_total = beta_total.reshape(4 * short, n, HD)[:, :, :heads]
+        beta_total = jnp.transpose(beta_total, (0, 2, 1)).reshape(4 * short, heads_all)
+    else:
+        small_total = lax.psum(small, ("dp", "fsdp", "ctx"))
+    gain_one, gain_two, gain_head, conv_total = jnp.split(small_total, cuts)
     return (
         output[None],
-        grad_tokens.astype(bf16)[None],
+        grad_tokens[None],
         gain_one,
         qkv_total,
         beta_total,

time: 485 us -> 443 us (0.913)
  waiting for transfers between devices: 169 us -> 115 us
  other arithmetic: 31.4 us -> 38.3 us
    ppermute x42 -> x53, waiting for transfers between devices: 127 us -> 94.7 us  [xor(): lax.ppermute(value, axis, [(i, i ^ step) for i in range(lax.axis_size(axi...]
    all_to_all x8 -> x5, waiting for transfers between devices: 36.1 us -> 16.8 us  [exchange(): return lax.all_to_all(blocks, axis, 0, 0, tiled=True)]
    ppermute x42 -> x53, starting transfers between devices: 34.5 us -> 47.5 us  [xor(): lax.ppermute(value, axis, [(i, i ^ step) for i in range(lax.axis_size(axi...]
    all_to_all x8 -> x5, starting transfers between devices: 39.4 us -> 26.6 us  [exchange(): return lax.all_to_all(blocks, axis, 0, 0, tiled=True)]
    pallas_call x5 -> x4, Pallas kernels: 32.2 us -> 35.3 us  [the longest x2 27.4 us: weight_grad(): pl.pallas_call(functools.partial(weight_grad_kernel, len(lefts), steps),...]
    unnamed x83 -> x106, local copies, waits for them, and re-layouts: 12.8 us -> 12.3 us
  transfers between devices with their start and end apart: 51 -> 59, of which waited for: 23 -> 28; matrix products, arithmetic and copies ran while one was open for 9% -> 11% of each run, Pallas kernels for 24% -> 25%
where the time goes in v3:
time: 443 us; the launch traced here: 435 us
  Pallas kernels  165 us (37%)
  waiting for transfers between devices  115 us (26%)
  starting transfers between devices  79.4 us (18%)
  other arithmetic  38.3 us (9%)
  local copies, waits for them, and re-layouts  34 us (8%)
    ppermute x53, waiting for transfers between devices, xor(): lax.ppermute(value, axis, [(i, i ^ step) for i in range(lax.axis_size(axi...  94.7 us
    ppermute x53, starting transfers between devices, xor(): lax.ppermute(value, axis, [(i, i ^ step) for i in range(lax.axis_size(axi...  47.5 us
    pallas_call x1, Pallas kernels, feed(): pl.pallas_call(functools.partial(feed_kernel, tags, places, len(down), ow...  31 us
    pallas_call x1, Pallas kernels, mixer_backward(): pl.pallas_call(functools.partial(mixer_backward_kernel, hb, heads), out_s...  30 us
    pallas_call x2, Pallas kernels, weight_grad(): pl.pallas_call(functools.partial(weight_grad_kernel, len(lefts), steps),...  27.4 us
    all_to_all x5, starting transfers between devices, exchange(): return lax.all_to_all(blocks, axis, 0, 0, tiled=True)  26.6 us
    pallas_call x1, Pallas kernels, mixer_forward(): pl.pallas_call(functools.partial(mixer_forward_kernel, hb), out_shape=(fl...  25 us
    all_to_all x5, waiting for transfers between devices, exchange(): return lax.all_to_all(blocks, axis, 0, 0, tiled=True)  16.8 us
  transfers between devices with their start and end apart: 59, of which 28 were waited for; matrix products, arithmetic and copies ran while one was open for 11% of the time, Pallas kernels for 25%

profile of v3, /device:TPU:10, one launch (start us, length us, event | category | flops | bytes accessed | tf_op | source)
XLA Modules:
  0.0 434.9 jit_solution(17514631824044498916)
XLA Ops:
  1.3 3.4 weight_pieces.1
  5.1 2.6 collective-permute-start.5
  8.2 5.6 %collective-permute-done.4 = bf16[64,1664]{1,0:T(8,128)(2,1)S(1)} collective-permute-done((bf16[64,1664]{1,0:T(8,128)(2,1)}, bf16[64,1664]{1,0:T(8,128)(2,1)S(1)}, u32[]{:S(2)}, u32[]{:S(2)}) %collective-permute-start.4) | collective-permute-done | bytes 213024 | tf_op jit(solution)/shard_map/ppermute | solution.py:263
  13.8 9.1 %collective-permute-done.5 = bf16[64,1664]{1,0:T(8,128)(2,1)S(1)} collective-permute-done((bf16[64,1664]{1,0:T(8,128)(2,1)}, bf16[64,1664]{1,0:T(8,128)(2,1)S(1)}, u32[]{:S(2)}, u32[]{:S(2)}) %collective-permute-start.5) | collective-permute-done | bytes 213024 | tf_op jit(solution)/shard_map/ppermute | solution.py:263
  22.9 4.0 collective-permute-done.6
  26.8 4.5 %all-to-all-start = ((bf16[4,64,3328]{2,1,0:T(8,128)(2,1)}), bf16[4,64,3328]{2,1,0:T(8,128)(2,1)}, u32[]{:S(2)}, u32[]{:S(2)}) async-start(bf16[4,64,3328]{2,1,0:T(8,128)(2,1)} %get-tuple-element.120), calls=%async_computation | async-start | bytes 3407872 | tf_op jit(solution)/shard_map/all_to_all | solution.py:616
  36.0 3.8 collective-permute-done.1.refs_1_
  48.8 7.1 %collective-permute-done.7.refs_1_ = bf16[64,3328]{1,0:T(8,128)(2,1)} collective-permute-done((bf16[64,3328]{1,0:T(8,128)(2,1)S(1)}, bf16[64,3328]{1,0:T(8,128)(2,1)}, u32[]{:S(2)}, u32[]{:S(2)}) %collective-permute-start.7) | collective-permute-done | bytes 426016 | tf_op jit(solution)/shard_map/ppermute | solution.py:263
  55.9 6.9 %collective-permute-done.8.refs_2_ = bf16[64,3328]{1,0:T(8,128)(2,1)} collective-permute-done((bf16[64,3328]{1,0:T(8,128)(2,1)S(1)}, bf16[64,3328]{1,0:T(8,128)(2,1)}, u32[]{:S(2)}, u32[]{:S(2)}) %collective-permute-start.8) | collective-permute-done | bytes 426016 | tf_op jit(solution)/shard_map/ppermute | solution.py:263
  67.2 2.9 broadcast_in_dim.51
  70.2 8.0 %all-to-all-start.1 = ((bf16[4,704,512]{2,1,0:T(8,128)(2,1)}), bf16[4,704,512]{2,1,0:T(8,128)(2,1)}, u32[]{:S(2)}, u32[]{:S(2)}) async-start(bf16[4,704,512]{2,1,0:T(8,128)(2,1)} %broadcast_in_dim.51), calls=%async_computation.1 | async-start | bytes 5767168 | tf_op jit(solution)/shard_map/all_to_all | solution.py:616
  82.7 2.6 collective-permute-done.11.refs_6_
  85.3 9.3 %collective-permute-done.12.refs_7_ = bf16[3,64,1664]{2,1,0:T(8,128)(2,1)} collective-permute-done((bf16[3,64,1664]{2,1,0:T(8,128)(2,1)S(1)}, bf16[3,64,1664]{2,1,0:T(8,128)(2,1)}, u32[]{:S(2)}, u32[]{:S(2)}) %collective-permute-start.12) | collective-permute-done | bytes 639008 | tf_op jit(solution)/shard_map/ppermute | solution.py:263
  94.6 11.4 %projections.1 = (bf16[1024,1024]{1,0:T(8,128)(2,1)}, f32[1024,1664]{1,0:T(8,128)}, bf16[1024,1664]{1,0:T(8,128)(2,1)}) custom-call(s32[3]{0:T(128)} %pad_add_fusion.where_ref, bf16[512,1024]{1,0:T(8,128)(2,1)} %bitcast.129, bf16[512,1024]{1,0:T(8,128)(2,1)} %collective-permute-done.x_far, f32[1,1024]{1,0:T(1,128)} %bitcast.141, ...), custom_call_target="tpu_custom_call" | custom-call | tf_op jit(solution)/shard_map/projections/pallas_call | solution.py:349
  111.5 25.0 %mixer_forward.1 = (bf16[1024,512]{1,0:T(8,128)(2,1)}, bf16[1024,512]{1,0:T(8,128)(2,1)}, bf16[4,8,128,128]{3,2,1,0:T(8,128)(2,1)}, bf16[1024,512]{1,0:T(8,128)(...) custom-call(s32[1]{0:T(128)} %copy.47.nv_ref, ...), custom_call_target="tpu_custom_call" | custom-call | tf_op jit(solution)/shard_map/mixer_forward/pallas_call | solution.py:133
  137.4 7.0 %mixer_out.1 = (f32[512,1024]{1,0:T(8,128)}, bf16[512,1024]{1,0:T(8,128)(2,1)}, bf16[512,1024]{1,0:T(8,128)(2,1)}) custom-call(s32[3]{0:T(128)} %pad_add_fusion.where_ref, bf16[1024,512]{1,0:T(8,128)(2,1)} %get-tuple-element.122.merged.refs_3_, bf16[64,3328]{1,0:T(8,128)(2,1)} %copy-done.16, bf16[64,3328]{1,0:T(8,128)(2,1)} %collective-permute-done.7.refs_1_, ...), custom_call_target="tpu_custom_call" | custom-call | tf_op jit(solution)/shard_map/mixer_out/pallas_call | solution.py:417
  148.3 2.5 multiply_reduce_fusion.2
  154.1 3.0 collective-permute-done.20.x_other.refs_1_
  158.1 31.0 %feed_forward.1 = (bf16[1024,1408]{1,0:T(8,128)(2,1)}, bf16[1024,2816]{1,0:T(8,128)(2,1)}, f32[512,1024]{1,0:T(8,128)}, bf16[512,1024]{1,0:T(8,128)(2,1)}, f32[5...) custom-call(s32[3]{0:T(128)} %pad_add_fusion.where_ref, bf16[512,1024]{1,0:T(8,128)(2,1)} %copy-done.4, ...), custom_call_target="tpu_custom_call" | custom-call | tf_op jit(solution)/shard_map/feed_forward/pallas_call | solution.py:691
  189.7 7.9 %down_gradient.1 = bf16[1408,1024]{1,0:T(8,128)(2,1)} custom-call(bf16[1024,1408]{1,0:T(8,128)(2,1)} %get-tuple-element.136.hidden, bf16[512,1024]{1,0:T(8,128)(2,1)} %fusion.7.e_own.own, bf16[512,1024]{1,0:T(8,128)(2,1)} %collective-permute-done.21.e_other.far), custom_call_target="tpu_custom_call" | custom-call | tf_op jit(solution)/shard_map/down_gradient/pallas_call | solution.py:596
  201.6 3.4 fusion.31
  206.1 2.6 collective-permute-done.25.far.refs_5_
  209.7 17.1 %weight_gradient.2 = (bf16[2,2,2,32,3328]{4,3,2,1,0:T(8,128)(2,1)}, bf16[2,2,2,32,3328]{4,3,2,1,0:T(8,128)(2,1)}, bf16[2,2,2,32,3328]{4,3,2,1,0:T(8,128)(2,1)}, bf16[2,2,2,32,3328]{4,3,2,1,0:T(8,128)(2,1)}) custom-call(s32[3]{0:T(128)} %pad_add_fusion.where_ref, bf16[512,1024]{1,0:T(8,128)(2,1)} %copy-done.4, bf16[512,1024]{1,0:T(8,128)(2,1)} %copy-done.14, ...), custom_call_target="tpu_custom_call" | custom-call | tf_op jit(solution)/shard_map/weight_gradient/pallas_call | solution.py:567
  226.7 2.8 copy.37
  231.4 4.6 %all-to-all-start.2 = ((bf16[4,352,1024]{2,1,0:T(8,128)(2,1)}), bf16[4,352,1024]{2,1,0:T(8,128)(2,1)}, u32[]{:S(2)}, u32[]{:S(2)}) async-start(bf16[4,352,1024]{2,1,0:T(8,128)(2,1)} %bitcast.131), calls=%async_computation.2 | async-start | bytes 5767168 | tf_op jit(solution)/shard_map/all_to_all | solution.py:616
  236.0 5.0 %merged_gradient.1.gm = f32[1024,512]{1,0:T(8,128)} custom-call(s32[3]{0:T(128)} %pad_add_fusion.where_ref, bf16[512,1024]{1,0:T(8,128)(2,1)} %copy-done.5, bf16[512,1024]{1,0:T(8,128)(2,1)} %copy-done.15, bf16[512,1024]{1,0:T(8,128)(2,1)} %get-tuple-element.138.weight), custom_call_target="tpu_custom_call" | custom-call | tf_op jit(solution)/shard_map/merged_gradient/pallas_call | solution.py:448
  241.1 30.0 %mixer_backward.1 = (bf16[1024,1664]{1,0:T(8,128)(2,1)}, f32[4,1536]{1,0:T(4,128)}, f32[8,128]{1,0:T(8,128)}) custom-call(s32[1]{0:T(128)} %copy.47.nv_ref, f32[1024,512]{1,0:T(8,128)} %merged_gradient.1.gm, bf16[1024,512]{1,0:T(8,128)(2,1)} %get-tuple-element.139.o, bf16[1024,512]{1,0:T(8,128)(2,1)} %get-tuple-element.140.q, ...), custom_call_target="tpu_custom_call" | custom-call | tf_op jit(solution)/shard_map/mixer_backward/pallas_call | solution.py:247
  272.4 2.5 add_convert_fusion
  281.4 10.3 %weight_gradient.3 = (bf16[2,2,2,32,1664]{4,3,2,1,0:T(8,128)(2,1)}, bf16[2,2,2,32,1664]{4,3,2,1,0:T(8,128)(2,1)}, bf16[2,2,2,32,1664]{4,3,2,1,0:T(8,128)(2,1)}, bf16[2,2,2,32,1664]{4,3,2,1,0:T(8,128)(2,1)}) custom-call(s32[3]{0:T(128)} %pad_add_fusion.where_ref, bf16[1024,1024]{1,0:T(8,128)(2,1)} %get-tuple-element.133.refs_0_, ...), custom_call_target="tpu_custom_call" | custom-call | tf_op jit(solution)/shard_map/weight_gradient/pallas_call | solution.py:567
  295.9 4.7 %collective-permute-done.28 = bf16[2,2,32,3328]{3,2,1,0:T(8,128)(2,1)} collective-permute-done((bf16[2,2,32,3328]{3,2,1,0:T(8,128)(2,1)}, bf16[2,2,32,3328]{3,2,1,0:T(8,128)(2,1)}, u32[]{:S(2)}, u32[]{:S(2)}) %collective-permute-start.28) | collective-permute-done | bytes 852000 | tf_op jit(solution)/shard_map/ppermute | solution.py:263
  306.4 9.2 %normed_gradient.1 = (f32[512,1024]{1,0:T(8,128)}, bf16[512,1024]{1,0:T(8,128)(2,1)}) custom-call(s32[3]{0:T(128)} %pad_add_fusion.where_ref, bf16[1024,1664]{1,0:T(8,128)(2,1)} %get-tuple-element.162.refs_1_.grad, bf16[1024,1664]{1,0:T(8,128)(2,1)} %get-tuple-element.163.weight), custom_call_target="tpu_custom_call" | custom-call | tf_op jit(solution)/shard_map/normed_gradient/pallas_call | solution.py:481
  315.5 3.3 collective-permute-done.30
  318.9 4.4 %all-to-all-start.3 = ((bf16[4,2,32,3328]{3,2,1,0:T(8,128)(2,1)}), bf16[4,2,32,3328]{3,2,1,0:T(8,128)(2,1)}, u32[]{:S(2)}, u32[]{:S(2)}) async-start(bf16[4,2,32,3328]{3,2,1,0:T(8,128)(2,1)} %pad_maximum_fusion), calls=%async_computation.3 | async-start | bytes 3407872 | tf_op jit(solution)/shard_map/all_to_all | solution.py:616
  328.5 2.3 add_convert_fusion.5
  337.6 3.7 collective-permute-done.36
  341.3 6.1 %collective-permute-done.37 = bf16[352,256]{1,0:T(8,128)(2,1)S(1)} collective-permute-done((bf16[352,256]{1,0:T(8,128)(2,1)S(1)}, bf16[352,256]{1,0:T(8,128)(2,1)S(1)}, u32[]{:S(2)}, u32[]{:S(2)}) %collective-permute-start.37) | collective-permute-done | bytes 180256 | tf_op jit(solution)/shard_map/ppermute | solution.py:263
  348.9 12.1 %all-to-all-done.3 = bf16[4,2,32,3328]{3,2,1,0:T(8,128)(2,1)} async-done(((bf16[4,2,32,3328]{3,2,1,0:T(8,128)(2,1)}), bf16[4,2,32,3328]{3,2,1,0:T(8,128)(2,1)}, u32[]{:S(2)}, u32[]{:S(2)}) %all-to-all-start.3) | async-done | bytes 1703968 | tf_op jit(solution)/shard_map/all_to_all | solution.py:616
  367.6 5.3 %collective-permute-start.40 = (bf16[352,256]{1,0:T(8,128)(2,1)S(1)}, bf16[352,256]{1,0:T(8,128)(2,1)S(1)}, u32[]{:S(2)}, u32[]{:S(2)}) collective-permute-start(bf16[352,256]{1,0:T(8,128)(2,1)S(1)} %fusion.16), channel_id=1, source_target_pairs={{0,0},{1,4},{2,1},{3,5},{4,2},{5,6},{6,3},{7,7},{8,8},{9,12},{10,9... | collective-permute-start | bytes 540680 | tf_op jit(solution)/shard_map/ppermute | solution.py:1016
  372.9 4.0 collective-permute-done.40
  380.6 2.9 fusion.5
  387.3 5.1 %all-to-all-start.4 = ((bf16[4,2,32,4864]{3,2,1,0:T(8,128)(2,1)}), bf16[4,2,32,4864]{3,2,1,0:T(8,128)(2,1)}, u32[]{:S(2)}, u32[]{:S(2)}) async-start(bf16[4,2,32,4864]{3,2,1,0:T(8,128)(2,1)} %broadcast_in_dim.58), calls=%async_computation.4 | async-start | bytes 4980736 | tf_op jit(solution)/shard_map/all_to_all | solution.py:616
  394.6 4.6 %collective-permute-done.45 = bf16[2,32,1664]{2,1,0:T(8,128)(2,1)S(1)} collective-permute-done((bf16[2,32,1664]{2,1,0:T(8,128)(2,1)}, bf16[2,32,1664]{2,1,0:T(8,128)(2,1)S(1)}, u32[]{:S(2)}, u32[]{:S(2)}) %collective-permute-start.45) | collective-permute-done | bytes 213024 | tf_op jit(solution)/shard_map/ppermute | solution.py:263
  399.2 5.6 %collective-permute-done.46 = bf16[2,32,1664]{2,1,0:T(8,128)(2,1)S(1)} collective-permute-done((bf16[2,32,1664]{2,1,0:T(8,128)(2,1)S(1)}, bf16[2,32,1664]{2,1,0:T(8,128)(2,1)S(1)}, u32[]{:S(2)}, u32[]{:S(2)}) %collective-permute-start.46) | collective-permute-done | bytes 213024 | tf_op jit(solution)/shard_map/ppermute | solution.py:263
  404.8 2.4 collective-permute-start.48
  415.7 2.5 collective-permute-start.53
  418.8 3.7 all-to-all-done.4.refs_0_
  422.5 4.7 %wide_totals.1 = (f32[128,5632]{1,0:T(8,128)}, f32[128,1024]{1,0:T(8,128)}, f32[352,1024]{1,0:T(8,128)}) custom-call(s32[3]{0:T(128)} %pad_add_fusion.where_ref, bf16[4,2,32,4864]{3,2,1,0:T(8,128)(2,1)} %all-to-all-done.4.refs_0_), custom_call_target="tpu_custom_call" | custom-call | tf_op jit(solution)/shard_map/wide_totals/pallas_call | solution.py:962
  429.8 3.2 mixed_totals.1
  (265 shorter events, 107.0 us)
Async XLA Ops:
  4.7 9.1 %collective-permute-start.4 = (bf16[64,1664]{1,0:T(8,128)(2,1)}, bf16[64,1664]{1,0:T(8,128)(2,1)S(1)}, u32[]{:S(2)}, u32[]{:S(2)}) collective-permute-start(bf16[64,1664]{1,0:T(8,128)(2,1)} %get-tuple-element.109.refs_0_), channel_id=1, source_target_pairs={{0,2},{2,0},{4,6},{6,4},{1,3},{3,1},{5,7},{7,5},{8,10},{10,8},{12,... | collective-permute-start | bytes 638984 | tf_op jit(solution)/shard_map/ppermute | solution.py:263
  5.1 17.7 %collective-permute-start.5 = (bf16[64,1664]{1,0:T(8,128)(2,1)}, bf16[64,1664]{1,0:T(8,128)(2,1)S(1)}, u32[]{:S(2)}, u32[]{:S(2)}) collective-permute-start(bf16[64,1664]{1,0:T(8,128)(2,1)} %get-tuple-element.109.refs_0_), channel_id=1, source_target_pairs={{0,4},{2,6},{4,0},{6,2},{1,5},{3,7},{5,1},{7,3},{8,12},{10,14},{12... | collective-permute-start | bytes 638984 | tf_op jit(solution)/shard_map/ppermute | solution.py:263
  7.7 19.1 %collective-permute-start.6 = (bf16[64,1664]{1,0:T(8,128)(2,1)}, bf16[64,1664]{1,0:T(8,128)(2,1)S(1)}, u32[]{:S(2)}, u32[]{:S(2)}) collective-permute-start(bf16[64,1664]{1,0:T(8,128)(2,1)} %get-tuple-element.109.refs_0_), channel_id=1, source_target_pairs={{0,6},{2,4},{4,2},{6,0},{1,7},{3,5},{5,3},{7,1},{8,14},{10,12},{12... | collective-permute-start | bytes 638984 | tf_op jit(solution)/shard_map/ppermute | solution.py:263
  26.8 40.4 %all-to-all-start = ((bf16[4,64,3328]{2,1,0:T(8,128)(2,1)}), bf16[4,64,3328]{2,1,0:T(8,128)(2,1)}, u32[]{:S(2)}, u32[]{:S(2)}) async-start(bf16[4,64,3328]{2,1,0:T(8,128)(2,1)} %get-tuple-element.120), calls=%async_computation | async-start | bytes 3407872 | tf_op jit(solution)/shard_map/all_to_all | solution.py:616
  31.3 8.4 %collective-permute-start.1 = (bf16[64,1664]{1,0:T(8,128)(2,1)}, bf16[64,1664]{1,0:T(8,128)(2,1)S(1)}, u32[]{:S(2)}, u32[]{:S(2)}) collective-permute-start(bf16[64,1664]{1,0:T(8,128)(2,1)} %get-tuple-element.109.refs_0_), channel_id=1, source_target_pairs={{0,8},{8,0},{16,24},{24,16},{1,9},{9,1},{17,25},{25,17},{2,10},{10... | collective-permute-start | bytes 638984 | tf_op jit(solution)/shard_map/ppermute | solution.py:263
  31.9 9.5 %collective-permute-start.2 = (bf16[64,1664]{1,0:T(8,128)(2,1)}, bf16[64,1664]{1,0:T(8,128)(2,1)S(1)}, u32[]{:S(2)}, u32[]{:S(2)}) collective-permute-start(bf16[64,1664]{1,0:T(8,128)(2,1)} %get-tuple-element.109.refs_0_), channel_id=1, source_target_pairs={{0,16},{8,24},{16,0},{24,8},{1,17},{9,25},{17,1},{25,9},{2,18},{10... | collective-permute-start | bytes 638984 | tf_op jit(solution)/shard_map/ppermute | solution.py:263
  33.5 9.5 %collective-permute-start.3 = (bf16[64,1664]{1,0:T(8,128)(2,1)}, bf16[64,1664]{1,0:T(8,128)(2,1)S(1)}, u32[]{:S(2)}, u32[]{:S(2)}) collective-permute-start(bf16[64,1664]{1,0:T(8,128)(2,1)} %get-tuple-element.109.refs_0_), channel_id=1, source_target_pairs={{0,24},{8,16},{16,8},{24,0},{1,25},{9,17},{17,9},{25,1},{2,26},{10... | collective-permute-start | bytes 638984 | tf_op jit(solution)/shard_map/ppermute | solution.py:263
  43.0 12.9 %collective-permute-start.7 = (bf16[64,3328]{1,0:T(8,128)(2,1)S(1)}, bf16[64,3328]{1,0:T(8,128)(2,1)}, u32[]{:S(2)}, u32[]{:S(2)}) collective-permute-start(bf16[64,3328]{1,0:T(8,128)(2,1)S(1)} %slice_bitcast_fusion.refs_0_), channel_id=1, source_target_pairs={{0,8},{8,0},{16,24},{24,16},{1,9},{9,1},{17,25},{25,17},{2,10},{10... | collective-permute-start | bytes 1277960 | tf_op jit(solution)/shard_map/ppermute | solution.py:263
  43.9 18.8 %collective-permute-start.8 = (bf16[64,3328]{1,0:T(8,128)(2,1)S(1)}, bf16[64,3328]{1,0:T(8,128)(2,1)}, u32[]{:S(2)}, u32[]{:S(2)}) collective-permute-start(bf16[64,3328]{1,0:T(8,128)(2,1)S(1)} %slice_bitcast_fusion.refs_0_), channel_id=1, source_target_pairs={{0,16},{8,24},{16,0},{24,8},{1,17},{9,25},{17,1},{25,9},{2,18},{10... | collective-permute-start | bytes 1277960 | tf_op jit(solution)/shard_map/ppermute | solution.py:263
  45.4 17.4 %collective-permute-start.9 = (bf16[64,3328]{1,0:T(8,128)(2,1)S(1)}, bf16[64,3328]{1,0:T(8,128)(2,1)}, u32[]{:S(2)}, u32[]{:S(2)}) collective-permute-start(bf16[64,3328]{1,0:T(8,128)(2,1)S(1)} %slice_bitcast_fusion.refs_0_), channel_id=1, source_target_pairs={{0,24},{8,16},{16,8},{24,0},{1,25},{9,17},{17,9},{25,1},{2,26},{10... | collective-permute-start | bytes 1277960 | tf_op jit(solution)/shard_map/ppermute | solution.py:263
  46.5 34.9 %collective-permute-start = (bf16[512,1024]{1,0:T(8,128)(2,1)S(1)}, bf16[512,1024]{1,0:T(8,128)(2,1)}, u32[]{:S(2)}, u32[]{:S(2)}) collective-permute-start(bf16[512,1024]{1,0:T(8,128)(2,1)S(1)} %bitcast.130), channel_id=1, source_target_pairs={{0,1},{1,0},{2,3},{3,2},{4,5},{5,4},{6,7},{7,6},{8,9},{9,8},{10,11... | collective-permute-start | bytes 3145736 | tf_op jit(solution)/shard_map/ppermute | solution.py:263
  62.8 19.9 %collective-permute-start.10 = (bf16[3,64,1664]{2,1,0:T(8,128)(2,1)S(1)}, bf16[3,64,1664]{2,1,0:T(8,128)(2,1)}, u32[]{:S(2)}, u32[]{:S(2)}) collective-permute-start(bf16[3,64,1664]{2,1,0:T(8,128)(2,1)S(1)} %pad_maximum_fusion.1.refs_4_), channel_id=1, source_target_pairs={{0,8},{8,0},{16,24},{24,16},{1,9},{9,1},{17,25},{25,17},{2,10},{10... | collective-permute-start | bytes 1916936 | tf_op jit(solution)/shard_map/ppermute | solution.py:263
  63.9 21.4 %collective-permute-start.11 = (bf16[3,64,1664]{2,1,0:T(8,128)(2,1)S(1)}, bf16[3,64,1664]{2,1,0:T(8,128)(2,1)}, u32[]{:S(2)}, u32[]{:S(2)}) collective-permute-start(bf16[3,64,1664]{2,1,0:T(8,128)(2,1)S(1)} %pad_maximum_fusion.1.refs_4_), channel_id=1, source_target_pairs={{0,16},{8,24},{16,0},{24,8},{1,17},{9,25},{17,1},{25,9},{2,18},{10... | collective-permute-start | bytes 1916936 | tf_op jit(solution)/shard_map/ppermute | solution.py:263
  65.5 29.0 %collective-permute-start.12 = (bf16[3,64,1664]{2,1,0:T(8,128)(2,1)S(1)}, bf16[3,64,1664]{2,1,0:T(8,128)(2,1)}, u32[]{:S(2)}, u32[]{:S(2)}) collective-permute-start(bf16[3,64,1664]{2,1,0:T(8,128)(2,1)S(1)} %pad_maximum_fusion.1.refs_4_), channel_id=1, source_target_pairs={{0,24},{8,16},{16,8},{24,0},{1,25},{9,17},{17,9},{25,1},{2,26},{10... | collective-permute-start | bytes 1916936 | tf_op jit(solution)/shard_map/ppermute | solution.py:263
  70.2 80.6 %all-to-all-start.1 = ((bf16[4,704,512]{2,1,0:T(8,128)(2,1)}), bf16[4,704,512]{2,1,0:T(8,128)(2,1)}, u32[]{:S(2)}, u32[]{:S(2)}) async-start(bf16[4,704,512]{2,1,0:T(8,128)(2,1)} %broadcast_in_dim.51), calls=%async_computation.1 | async-start | bytes 5767168 | tf_op jit(solution)/shard_map/all_to_all | solution.py:616
  79.8 28.2 %collective-permute-start.14 = (bf16[3,64,1664]{2,1,0:T(8,128)(2,1)S(1)}, bf16[3,64,1664]{2,1,0:T(8,128)(2,1)}, u32[]{:S(2)}, u32[]{:S(2)}) collective-permute-start(bf16[3,64,1664]{2,1,0:T(8,128)(2,1)S(1)} %pad_maximum_fusion.3.refs_8_), channel_id=1, source_target_pairs={{0,16},{8,24},{16,0},{24,8},{1,17},{9,25},{17,1},{25,9},{2,18},{10... | collective-permute-start | bytes 1916936 | tf_op jit(solution)/shard_map/ppermute | solution.py:263
  81.5 26.5 %collective-permute-start.13 = (bf16[3,64,1664]{2,1,0:T(8,128)(2,1)S(1)}, bf16[3,64,1664]{2,1,0:T(8,128)(2,1)S(1)}, u32[]{:S(2)}, u32[]{:S(2)}) collective-permute-start(bf16[3,64,1664]{2,1,0:T(8,128)(2,1)S(1)} %pad_maximum_fusion.2.refs_4_), channel_id=1, source_target_pairs={{0,8},{8,0},{16,24},{24,16},{1,9},{9,1},{17,25},{25,17},{2,10},{10... | collective-permute-start | bytes 1916936 | tf_op jit(solution)/shard_map/ppermute | solution.py:263
  106.0 30.6 %collective-permute-start.17 = (bf16[3,64,1664]{2,1,0:T(8,128)(2,1)S(1)}, bf16[3,64,1664]{2,1,0:T(8,128)(2,1)S(1)}, u32[]{:S(2)}, u32[]{:S(2)}) collective-permute-start(bf16[3,64,1664]{2,1,0:T(8,128)(2,1)S(1)} %pad_maximum_fusion.3.refs_8_), channel_id=1, source_target_pairs={{0,8},{8,0},{16,24},{24,16},{1,9},{9,1},{17,25},{25,17},{2,10},{10... | collective-permute-start | bytes 1916936 | tf_op jit(solution)/shard_map/ppermute | solution.py:263
  107.6 29.0 %collective-permute-start.15 = (bf16[3,64,1664]{2,1,0:T(8,128)(2,1)S(1)}, bf16[3,64,1664]{2,1,0:T(8,128)(2,1)}, u32[]{:S(2)}, u32[]{:S(2)}) collective-permute-start(bf16[3,64,1664]{2,1,0:T(8,128)(2,1)S(1)} %pad_maximum_fusion.2.refs_4_), channel_id=1, source_target_pairs={{0,16},{8,24},{16,0},{24,8},{1,17},{9,25},{17,1},{25,9},{2,18},{10... | collective-permute-start | bytes 1916936 | tf_op jit(solution)/shard_map/ppermute | solution.py:263
  107.9 28.7 %collective-permute-start.16 = (bf16[3,64,1664]{2,1,0:T(8,128)(2,1)S(1)}, bf16[3,64,1664]{2,1,0:T(8,128)(2,1)}, u32[]{:S(2)}, u32[]{:S(2)}) collective-permute-start(bf16[3,64,1664]{2,1,0:T(8,128)(2,1)S(1)} %collective-permute-done.13.refs_5_), channel_id=1, source_target_pairs={{0,16},{8,24},{16,0},{24,8},{1,17},{9,25},{17,1},{25,9},{2,18},{10... | collective-permute-start | bytes 1916936 | tf_op jit(solution)/shard_map/ppermute | solution.py:263
  109.7 26.9 %collective-permute-start.18 = (bf16[3,64,1664]{2,1,0:T(8,128)(2,1)}, bf16[3,64,1664]{2,1,0:T(8,128)(2,1)}, u32[]{:S(2)}, u32[]{:S(2)}) collective-permute-start(bf16[3,64,1664]{2,1,0:T(8,128)(2,1)} %collective-permute-done.14.refs_10_), channel_id=1, source_target_pairs={{0,8},{8,0},{16,24},{24,16},{1,9},{9,1},{17,25},{25,17},{2,10},{10... | collective-permute-start | bytes 1916936 | tf_op jit(solution)/shard_map/ppermute | solution.py:263
  189.1 8.5 %collective-permute-start.24 = (bf16[512,1024]{1,0:T(8,128)(2,1)}, bf16[512,1024]{1,0:T(8,128)(2,1)}, u32[]{:S(2)}, u32[]{:S(2)}) collective-permute-start(bf16[512,1024]{1,0:T(8,128)(2,1)} %get-tuple-element.135), channel_id=1, source_target_pairs={{0,1},{1,0},{2,3},{3,2},{4,5},{5,4},{6,7},{7,6},{8,9},{9,8},{10,11... | collective-permute-start | bytes 3145736 | tf_op jit(solution)/shard_map/ppermute | solution.py:263
  189.3 11.2 %collective-permute-start.23 = (bf16[512,1024]{1,0:T(8,128)(2,1)}, bf16[512,1024]{1,0:T(8,128)(2,1)}, u32[]{:S(2)}, u32[]{:S(2)}) collective-permute-start(bf16[512,1024]{1,0:T(8,128)(2,1)} %get-tuple-element.132), channel_id=1, source_target_pairs={{0,1},{1,0},{2,3},{3,2},{4,5},{5,4},{6,7},{7,6},{8,9},{9,8},{10,11... | collective-permute-start | bytes 3145736 | tf_op jit(solution)/shard_map/ppermute | solution.py:263
  229.5 41.6 %collective-permute-start.26 = (bf16[2,2,2,32,3328]{4,3,1,0,2:T(8,128)(2,1)}, bf16[2,2,2,32,3328]{4,3,1,0,2:T(8,128)(2,1)S(1)}, u32[]{:S(2)}, u32[]{:S(2)}) collective-permute-start(bf16[2,2,2,32,3328]{4,3,1,0,2:T(8,128)(2,1)} %copy.37), channel_id=1, source_target_pairs={{0,8},{8,0},{16,24},{24,16},{1,9},{9,1},{17,25},{25,17},{2,10},{10... | collective-permute-start | bytes 5111816 | tf_op jit(solution)/shard_map/ppermute | solution.py:263
  231.1 40.1 %collective-permute-start.27 = (bf16[2,2,2,32,3328]{4,3,2,1,0:T(8,128)(2,1)}, bf16[2,2,2,32,3328]{4,3,2,1,0:T(8,128)(2,1)}, u32[]{:S(2)}, u32[]{:S(2)}) collective-permute-start(bf16[2,2,2,32,3328]{4,3,2,1,0:T(8,128)(2,1)} %get-tuple-element.148), channel_id=1, source_target_pairs={{0,16},{8,24},{16,0},{24,8},{1,17},{9,25},{17,1},{25,9},{2,18},{10... | collective-permute-start | bytes 5111816 | tf_op jit(solution)/shard_map/ppermute | solution.py:263
  231.4 74.9 %all-to-all-start.2 = ((bf16[4,352,1024]{2,1,0:T(8,128)(2,1)}), bf16[4,352,1024]{2,1,0:T(8,128)(2,1)}, u32[]{:S(2)}, u32[]{:S(2)}) async-start(bf16[4,352,1024]{2,1,0:T(8,128)(2,1)} %bitcast.131), calls=%async_computation.2 | async-start | bytes 5767168 | tf_op jit(solution)/shard_map/all_to_all | solution.py:616
  278.4 22.2 %collective-permute-start.28 = (bf16[2,2,32,3328]{3,2,1,0:T(8,128)(2,1)}, bf16[2,2,32,3328]{3,2,1,0:T(8,128)(2,1)}, u32[]{:S(2)}, u32[]{:S(2)}) collective-permute-start(bf16[2,2,32,3328]{3,2,1,0:T(8,128)(2,1)} %dynamic-slice_bitcast_fusion.2), channel_id=1, source_target_pairs={{0,16},{8,24},{16,0},{24,8},{1,17},{9,25},{17,1},{25,9},{2,18},{10... | collective-permute-start | bytes 2555912 | tf_op jit(solution)/shard_map/ppermute | solution.py:263
  280.1 22.2 %collective-permute-start.29 = (bf16[2,2,32,3328]{3,2,1,0:T(8,128)(2,1)}, bf16[2,2,32,3328]{3,2,1,0:T(8,128)(2,1)}, u32[]{:S(2)}, u32[]{:S(2)}) collective-permute-start(bf16[2,2,32,3328]{3,2,1,0:T(8,128)(2,1)} %dynamic-slice_bitcast_fusion.1), channel_id=1, source_target_pairs={{0,8},{8,0},{16,24},{24,16},{1,9},{9,1},{17,25},{25,17},{2,10},{10... | collective-permute-start | bytes 2555912 | tf_op jit(solution)/shard_map/ppermute | solution.py:263
  294.0 24.9 %collective-permute-start.30 = (bf16[2,2,2,32,1664]{4,3,1,0,2:T(8,128)(2,1)}, bf16[2,2,2,32,1664]{4,3,1,0,2:T(8,128)(2,1)}, u32[]{:S(2)}, u32[]{:S(2)}) collective-permute-start(bf16[2,2,2,32,1664]{4,3,1,0,2:T(8,128)(2,1)} %copy.40), channel_id=1, source_target_pairs={{0,8},{8,0},{16,24},{24,16},{1,9},{9,1},{17,25},{25,17},{2,10},{10... | collective-permute-start | bytes 2555912 | tf_op jit(solution)/shard_map/ppermute | solution.py:263
  295.5 23.3 %collective-permute-start.31 = (bf16[2,2,2,32,1664]{4,3,2,1,0:T(8,128)(2,1)}, bf16[2,2,2,32,1664]{4,3,2,1,0:T(8,128)(2,1)}, u32[]{:S(2)}, u32[]{:S(2)}) collective-permute-start(bf16[2,2,2,32,1664]{4,3,2,1,0:T(8,128)(2,1)} %get-tuple-element.165), channel_id=1, source_target_pairs={{0,16},{8,24},{16,0},{24,8},{1,17},{9,25},{17,1},{25,9},{2,18},{10... | collective-permute-start | bytes 2555912 | tf_op jit(solution)/shard_map/ppermute | solution.py:263
  318.9 12.0 %collective-permute-start.32 = (bf16[512,1024]{1,0:T(8,128)(2,1)}, bf16[512,1024]{1,0:T(8,128)(2,1)}, u32[]{:S(2)}, u32[]{:S(2)}) collective-permute-start(bf16[512,1024]{1,0:T(8,128)(2,1)} %get-tuple-element.168), channel_id=1, source_target_pairs={{0,1},{1,0},{2,3},{3,2},{4,5},{5,4},{6,7},{7,6},{8,9},{9,8},{10,11... | collective-permute-start | bytes 3145736 | tf_op jit(solution)/shard_map/ppermute | solution.py:263
  318.9 42.1 %all-to-all-start.3 = ((bf16[4,2,32,3328]{3,2,1,0:T(8,128)(2,1)}), bf16[4,2,32,3328]{3,2,1,0:T(8,128)(2,1)}, u32[]{:S(2)}, u32[]{:S(2)}) async-start(bf16[4,2,32,3328]{3,2,1,0:T(8,128)(2,1)} %pad_maximum_fusion), calls=%async_computation.3 | async-start | bytes 3407872 | tf_op jit(solution)/shard_map/all_to_all | solution.py:616
  324.8 22.6 %collective-permute-start.35 = (bf16[2,2,32,1664]{3,2,1,0:T(8,128)(2,1)S(1)}, bf16[2,2,32,1664]{3,2,1,0:T(8,128)(2,1)S(1)}, u32[]{:S(2)}, u32[]{:S(2)}) collective-permute-start(bf16[2,2,32,1664]{3,2,1,0:T(8,128)(2,1)S(1)} %dynamic-slice_bitcast_fusion.3), channel_id=1, source_target_pairs={{0,8},{8,0},{16,24},{24,16},{1,9},{9,1},{17,25},{25,17},{2,10},{10... | collective-permute-start | bytes 1277960 | tf_op jit(solution)/shard_map/ppermute | solution.py:263
  327.6 21.2 %collective-permute-start.34 = (bf16[2,2,32,1664]{3,2,1,0:T(8,128)(2,1)S(1)}, bf16[2,2,32,1664]{3,2,1,0:T(8,128)(2,1)}, u32[]{:S(2)}, u32[]{:S(2)}) collective-permute-start(bf16[2,2,32,1664]{3,2,1,0:T(8,128)(2,1)S(1)} %dynamic-slice_bitcast_fusion.4), channel_id=1, source_target_pairs={{0,16},{8,24},{16,0},{24,8},{1,17},{9,25},{17,1},{25,9},{2,18},{10... | collective-permute-start | bytes 1277960 | tf_op jit(solution)/shard_map/ppermute | solution.py:263
  334.7 12.7 %collective-permute-start.37 = (bf16[352,256]{1,0:T(8,128)(2,1)S(1)}, bf16[352,256]{1,0:T(8,128)(2,1)S(1)}, u32[]{:S(2)}, u32[]{:S(2)}) collective-permute-start(bf16[352,256]{1,0:T(8,128)(2,1)S(1)} %get-tuple-element.225), channel_id=1, source_target_pairs={{0,16},{8,24},{16,0},{24,8},{1,17},{9,25},{17,1},{25,9},{2,18},{10... | collective-permute-start | bytes 540680 | tf_op jit(solution)/shard_map/ppermute | solution.py:263
  336.2 11.2 %collective-permute-start.38 = (bf16[352,256]{1,0:T(8,128)(2,1)S(1)}, bf16[352,256]{1,0:T(8,128)(2,1)S(1)}, u32[]{:S(2)}, u32[]{:S(2)}) collective-permute-start(bf16[352,256]{1,0:T(8,128)(2,1)S(1)} %get-tuple-element.224), channel_id=1, source_target_pairs={{0,24},{8,16},{16,8},{24,0},{1,25},{9,17},{17,9},{25,1},{2,26},{10... | collective-permute-start | bytes 540680 | tf_op jit(solution)/shard_map/ppermute | solution.py:263
  366.4 10.6 %collective-permute-start.39 = (bf16[32,2816]{1,0:T(8,128)(2,1)S(1)}, bf16[32,2816]{1,0:T(8,128)(2,1)S(1)}, u32[]{:S(2)}, u32[]{:S(2)}) collective-permute-start(bf16[32,2816]{1,0:T(8,128)(2,1)S(1)} %dynamic-slice_bitcast_fusion.8), channel_id=1, source_target_pairs={{0,1},{1,0},{2,3},{3,2},{4,5},{5,4},{6,7},{7,6},{8,9},{9,8},{10,11... | collective-permute-start | bytes 540680 | tf_op jit(solution)/shard_map/ppermute | solution.py:263
  367.6 9.3 %collective-permute-start.40 = (bf16[352,256]{1,0:T(8,128)(2,1)S(1)}, bf16[352,256]{1,0:T(8,128)(2,1)S(1)}, u32[]{:S(2)}, u32[]{:S(2)}) collective-permute-start(bf16[352,256]{1,0:T(8,128)(2,1)S(1)} %fusion.16), channel_id=1, source_target_pairs={{0,0},{1,4},{2,1},{3,5},{4,2},{5,6},{6,3},{7,7},{8,8},{9,12},{10,9... | collective-permute-start | bytes 540680 | tf_op jit(solution)/shard_map/ppermute | solution.py:1016
  377.1 15.3 %collective-permute-start.41 = (f32[14464]{0:T(1024)}, f32[14464]{0:T(1024)S(1)}, u32[]{:S(2)}, u32[]{:S(2)}) collective-permute-start(f32[14464]{0:T(1024)} %fusion.30), channel_id=1, source_target_pairs={{0,8},{8,0},{16,24},{24,16},{1,9},{9,1},{17,25},{25,17},{2,10},{10... | collective-permute-start | bytes 173576 | tf_op jit(solution)/shard_map/ppermute | solution.py:263
  377.6 16.1 %collective-permute-start.42 = (f32[14464]{0:T(1024)}, f32[14464]{0:T(1024)S(1)}, u32[]{:S(2)}, u32[]{:S(2)}) collective-permute-start(f32[14464]{0:T(1024)} %fusion.30), channel_id=1, source_target_pairs={{0,16},{8,24},{16,0},{24,8},{1,17},{9,25},{17,1},{25,9},{2,18},{10... | collective-permute-start | bytes 173576 | tf_op jit(solution)/shard_map/ppermute | solution.py:263
  378.4 15.3 %collective-permute-start.43 = (f32[14464]{0:T(1024)}, f32[14464]{0:T(1024)S(1)}, u32[]{:S(2)}, u32[]{:S(2)}) collective-permute-start(f32[14464]{0:T(1024)} %fusion.30), channel_id=1, source_target_pairs={{0,24},{8,16},{16,8},{24,0},{1,25},{9,17},{17,9},{25,1},{2,26},{10... | collective-permute-start | bytes 173576 | tf_op jit(solution)/shard_map/ppermute | solution.py:263
  383.5 11.1 %collective-permute-start.44 = (bf16[2,32,1664]{2,1,0:T(8,128)(2,1)}, bf16[2,32,1664]{2,1,0:T(8,128)(2,1)S(1)}, u32[]{:S(2)}, u32[]{:S(2)}) collective-permute-start(bf16[2,32,1664]{2,1,0:T(8,128)(2,1)} %get-tuple-element.185), channel_id=1, source_target_pairs={{0,2},{2,0},{4,6},{6,4},{1,3},{3,1},{5,7},{7,5},{8,10},{10,8},{12,... | collective-permute-start | bytes 638984 | tf_op jit(solution)/shard_map/ppermute | solution.py:263
  383.5 15.7 %collective-permute-start.45 = (bf16[2,32,1664]{2,1,0:T(8,128)(2,1)}, bf16[2,32,1664]{2,1,0:T(8,128)(2,1)S(1)}, u32[]{:S(2)}, u32[]{:S(2)}) collective-permute-start(bf16[2,32,1664]{2,1,0:T(8,128)(2,1)} %get-tuple-element.186), channel_id=1, source_target_pairs={{0,4},{2,6},{4,0},{6,2},{1,5},{3,7},{5,1},{7,3},{8,12},{10,14},{12... | collective-permute-start | bytes 638984 | tf_op jit(solution)/shard_map/ppermute | solution.py:263
  387.3 35.2 %all-to-all-start.4 = ((bf16[4,2,32,4864]{3,2,1,0:T(8,128)(2,1)}), bf16[4,2,32,4864]{3,2,1,0:T(8,128)(2,1)}, u32[]{:S(2)}, u32[]{:S(2)}) async-start(bf16[4,2,32,4864]{3,2,1,0:T(8,128)(2,1)} %broadcast_in_dim.58), calls=%async_computation.4 | async-start | bytes 4980736 | tf_op jit(solution)/shard_map/all_to_all | solution.py:616
  392.4 12.4 %collective-permute-start.46 = (bf16[2,32,1664]{2,1,0:T(8,128)(2,1)S(1)}, bf16[2,32,1664]{2,1,0:T(8,128)(2,1)S(1)}, u32[]{:S(2)}, u32[]{:S(2)}) collective-permute-start(bf16[2,32,1664]{2,1,0:T(8,128)(2,1)S(1)} %copy-done.36), channel_id=1, source_target_pairs={{0,6},{2,4},{4,2},{6,0},{1,7},{3,5},{5,3},{7,1},{8,14},{10,12},{12... | collective-permute-start | bytes 638984 | tf_op jit(solution)/shard_map/ppermute | solution.py:263
  414.6 12.6 %collective-permute-start.51 = (bf16[2,32,1664]{2,1,0:T(8,128)(2,1)S(1)}, bf16[2,32,1664]{2,1,0:T(8,128)(2,1)S(1)}, u32[]{:S(2)}, u32[]{:S(2)}) collective-permute-start(bf16[2,32,1664]{2,1,0:T(8,128)(2,1)S(1)} %pad_maximum_fusion.5.refs_0_), channel_id=1, source_target_pairs={{0,8},{8,0},{16,24},{24,16},{1,9},{9,1},{17,25},{25,17},{2,10},{10... | collective-permute-start | bytes 638984 | tf_op jit(solution)/shard_map/ppermute | solution.py:263
  415.1 12.2 %collective-permute-start.52 = (bf16[2,32,1664]{2,1,0:T(8,128)(2,1)S(1)}, bf16[2,32,1664]{2,1,0:T(8,128)(2,1)S(1)}, u32[]{:S(2)}, u32[]{:S(2)}) collective-permute-start(bf16[2,32,1664]{2,1,0:T(8,128)(2,1)S(1)} %pad_maximum_fusion.5.refs_0_), channel_id=1, source_target_pairs={{0,16},{8,24},{16,0},{24,8},{1,17},{9,25},{17,1},{25,9},{2,18},{10... | collective-permute-start | bytes 638984 | tf_op jit(solution)/shard_map/ppermute | solution.py:263
  415.7 13.4 %collective-permute-start.53 = (bf16[2,32,1664]{2,1,0:T(8,128)(2,1)S(1)}, bf16[2,32,1664]{2,1,0:T(8,128)(2,1)S(1)}, u32[]{:S(2)}, u32[]{:S(2)}) collective-permute-start(bf16[2,32,1664]{2,1,0:T(8,128)(2,1)S(1)} %pad_maximum_fusion.5.refs_0_), channel_id=1, source_target_pairs={{0,24},{8,16},{16,8},{24,0},{1,25},{9,17},{17,9},{25,1},{2,26},{10... | collective-permute-start | bytes 638984 | tf_op jit(solution)/shard_map/ppermute | solution.py:263
  (64 other events, 498.9 us)
